TPU v7x, 32 devices: a whole 2x2x4 slice. The times are simulated.
32 devices in a mesh: groups: 2 (over x), ctx: 16 (over z, y, core).
Axes of the slice: x: 2, y: 2, z: 4, core: 2. Of those that a mesh axis runs over, the one named last changes fastest.
Arguments:
- events: bfloat16 [16384, 1024], P(('groups', 'ctx')), parts along dimension 0, may hold values from -6 to 6
- w_in: bfloat16 [1024, 4096], replicated, may hold values from -0.1875 to 0.1875
- w_out: bfloat16 [1024, 1024], replicated, may hold values from -0.1875 to 0.1875
- rel_bias: float32 [16, 16], replicated, may hold values from -3 to 3
- lengths: int32 [8], P('groups'), parts along dimension 0, may hold values from 1 to 4096, as said below
- block_lists: int32 [32, 2], P(('groups', 'ctx')), parts along dimension 0, may hold values from 1 to 4, as said below
- candidates: int32 [32, 128], P('groups'), parts along dimension 0, may hold values from 0 to 8191, as said below
Outputs:
- layer_output: bfloat16 [16384, 1024], P(('groups', 'ctx')), parts along dimension 0
- next_score: float32 [16384], P(('groups', 'ctx')), parts along dimension 0
- candidate_score_table: float32 [16384, 128], P(('groups', 'ctx')), parts along dimension 0
There are 2 independent parts, one for each index of `groups`. A program takes and returns all parts, laid end to end along the dimension named above; an argument that names none is the same for every part. Nothing has to cross between parts.
Inputs may be any that keep to these rules, and one draw needn't show every extreme that they name: `lengths`: the first user has exactly 4096 events. `block_lists`: each row holds 2 different distances; row 0 lists distance 1. `candidates`: of one row's 128 rows at most 16 lie in one block, and exactly 16 in some block.
All inputs are finite; a program needn't handle non-finite values.
Results may differ from a plain program's by a relative error of at most 0.007.
Values may be sent and summed in bfloat16 or wider, within the bound.
No kernel may reach another device: no remote copies, remote signals or barrier semaphores. Data moves between devices by JAX's collectives and lax.ppermute only.
A program may use at most 128 MiB of HBM per device.

v0:
```python
import jax
import jax.numpy as jnp
from jax import lax
from jax.sharding import PartitionSpec as P

SPAN = 4


def passed_along(value, axis, steps):
    count = lax.axis_size(axis)
    pairs = [(source, (source + steps) % count) for source in range(count)]
    return lax.ppermute(value, axis, pairs)


def layer_norm(values):
    values = values.astype(jnp.float32)
    center = values - jnp.mean(values, -1, keepdims=True)
    spread = jnp.mean(center * center, -1, keepdims=True)
    return center * lax.rsqrt(spread + 1e-05)


def bucket_bias(distance, rel_bias):
    buckets = rel_bias.shape[1]
    bucket = jnp.zeros(distance.shape, jnp.int32)
    for degree in range(buckets - 1):
        bucket = bucket + (distance >= 2**degree).astype(jnp.int32)
    rel_terms = jnp.zeros((rel_bias.shape[0],) + distance.shape, rel_bias.dtype)
    for degree in range(buckets):
        rel_terms = jnp.where(
            (bucket == degree)[None], rel_bias[:, degree][:, None, None], rel_terms
        )
    return rel_terms


def user_of(positions, user_ends):
    return jnp.sum((positions[:, None] >= user_ends[None, :]).astype(jnp.int32), axis=1)


def attend(queries, query_pos, query_user, key_rows, value_rows, key_pos, key_user, rel_bias):
    attention_scale = queries.shape[-1] ** (-0.5)
    scores = jnp.einsum("qhd,khd->hqk", queries, key_rows, preferred_element_type=jnp.float32)
    distance = query_pos[:, None] - key_pos[None, :]
    rel_terms = bucket_bias(distance, rel_bias)
    allowed = (distance >= 0) & (query_user[:, None] == key_user[None, :])
    weights = jnp.where(
        allowed[None], jax.nn.silu(scores * attention_scale + rel_terms), 0.0
    ).astype(jnp.bfloat16)
    return jnp.einsum("hqk,khd->qhd", weights, value_rows, preferred_element_type=jnp.float32)


def slot_ids(request, ctx_size, event_row_count, slot_cap):
    owner_dev = request // event_row_count
    local_row = request % event_row_count
    owner_hits = (owner_dev[:, None] == jnp.arange(ctx_size, dtype=jnp.int32)[None, :]).astype(
        jnp.int32
    )
    slot_rank = jnp.sum(jnp.cumsum(owner_hits, axis=0) * owner_hits, axis=1) - 1
    slot_id = owner_dev * slot_cap + slot_rank
    slot_hits = slot_id[:, None] == jnp.arange(ctx_size * slot_cap, dtype=jnp.int32)[None, :]
    row_ids = jnp.sum(jnp.where(slot_hits, local_row[:, None] + 1, 0), axis=0) - 1
    return (row_ids.reshape(ctx_size, slot_cap), slot_hits)


def shards(events, w_in, w_out, rel_bias, lengths, block_lists, candidates):
    event_row_count, hidden_width = events.shape
    head_count = rel_bias.shape[0]
    head_size = hidden_width // head_count
    ctx_size = lax.axis_size("ctx")
    my_index = lax.axis_index("ctx")
    total_rows = ctx_size * event_row_count
    user_ends = jnp.cumsum(lengths)

    def times_of(block_num):
        return (
            block_num * event_row_count
            + jnp.arange(event_row_count, dtype=jnp.int32)
            + total_rows // 4
        ) % total_rows

    query_pos = times_of(my_index)
    query_user = user_of(query_pos, user_ends)
    normed = layer_norm(events).astype(jnp.bfloat16)
    projected = jax.nn.silu(jnp.dot(normed, w_in, preferred_element_type=jnp.float32)).astype(
        jnp.bfloat16
    )
    gate_u = projected[:, :hidden_width]
    queries = projected[:, hidden_width : 2 * hidden_width].reshape(
        event_row_count, head_count, head_size
    )
    key_values = projected[:, 2 * hidden_width :]

    def split_pair(paired):
        value_rows = paired[:, :hidden_width].reshape(event_row_count, head_count, head_size)
        key_rows = paired[:, hidden_width:].reshape(event_row_count, head_count, head_size)
        return (key_rows, value_rows)

    own_keys, own_values = split_pair(key_values)
    running = attend(
        queries, query_pos, query_user, own_keys, own_values, query_pos, query_user, rel_bias
    )
    wanted_list = block_lists[0]

    def contribute(operands):
        arrived, key_pos, key_user = operands
        key_rows, value_rows = split_pair(arrived)
        return attend(
            queries, query_pos, query_user, key_rows, value_rows, key_pos, key_user, rel_bias
        )

    def nothing(operands):
        return jnp.zeros((event_row_count, head_count, head_size), jnp.float32)

    carried = key_values
    for offset in range(1, SPAN + 1):
        carried = passed_along(carried, "ctx", 1)
        source_block = (my_index - offset) % ctx_size
        key_pos = times_of(source_block)
        key_user = user_of(key_pos, user_ends)
        useful = (
            jnp.any(wanted_list == offset)
            & (key_pos[0] < query_pos[0])
            & (key_user[event_row_count - 1] >= query_user[0])
        )
        running = running + lax.cond(useful, contribute, nothing, (carried, key_pos, key_user))
    attended = running.reshape(event_row_count, hidden_width)
    gated_rows = (layer_norm(attended) * gate_u.astype(jnp.float32)).astype(jnp.bfloat16)
    layer_output = (
        events.astype(jnp.float32) + jnp.dot(gated_rows, w_out, preferred_element_type=jnp.float32)
    ).astype(jnp.bfloat16)
    attention_scale = hidden_width ** (-0.5)
    next_first = passed_along(events[:1], "ctx", -1)
    following = jnp.concatenate([events[1:], next_first], axis=0)
    next_user = user_of(query_pos + 1, user_ends)
    inner = (
        jnp.sum(layer_output.astype(jnp.float32) * following.astype(jnp.float32), axis=1)
        * attention_scale
    )
    next_score = jnp.where(next_user == query_user, inner, 0.0)
    cand_count = candidates.shape[1]
    slot_cap = 2 * cand_count // ctx_size
    own_request = lax.dynamic_slice_in_dim(candidates, my_index, 1, 0)[0]
    own_ids, own_hits = slot_ids(own_request, ctx_size, event_row_count, slot_cap)
    every_ids = jax.vmap(lambda request: slot_ids(request, ctx_size, event_row_count, slot_cap)[0])(
        candidates
    )
    my_part = lax.dynamic_index_in_dim(every_ids, my_index, 1, keepdims=False)
    flat_ids = my_part.reshape(-1)
    picks = (flat_ids[:, None] == jnp.arange(event_row_count, dtype=jnp.int32)[None, :]).astype(
        jnp.bfloat16
    )
    fetched = jnp.dot(picks, events, preferred_element_type=jnp.float32).astype(jnp.bfloat16)
    arrived_rows = lax.all_to_all(
        fetched.reshape(my_part.shape + (hidden_width,)),
        "ctx",
        split_axis=0,
        concat_axis=0,
        tiled=True,
    )
    flat_rows = arrived_rows.reshape(ctx_size * slot_cap, hidden_width)
    candidate_row_list = jnp.dot(
        own_hits.astype(jnp.bfloat16), flat_rows, preferred_element_type=jnp.float32
    ).astype(jnp.bfloat16)
    candidate_score_table = (
        jnp.dot(layer_output, candidate_row_list.T, preferred_element_type=jnp.float32)
        * attention_scale
    )
    return (layer_output, next_score, candidate_score_table)


def solution(mesh):
    in_specs = (
        P(("groups", "ctx"), None),
        P(),
        P(),
        P(),
        P("groups"),
        P(("groups", "ctx"), None),
        P("groups", None),
    )
    out_specs = (P(("groups", "ctx"), None), P(("groups", "ctx")), P(("groups", "ctx"), None))
    return jax.shard_map(shards, mesh=mesh, in_specs=in_specs, out_specs=out_specs, check_vma=False)
```

profile of v0, /device:TPU:2, one launch (start us, length us, event | category | flops | bytes accessed | tf_op | source)
XLA Modules:
  0.0 285.6 jit_solution(220536213522138258)
XLA Ops:
  2.2 1.6 fusion.48
  3.9 9.2 %multiply_convert_fusion = bf16[512,4096]{1,0:T(8,128)(2,1)S(1)} fusion(bf16[1024,4096]{1,0:T(8,128)(2,1)} %param.16, bf16[512,1024]{1,0:T(8,128)(2,1)} %param.15, f32[512]{0:T(512)S(1)} %add_rsqrt_fusion.1, f32[512]{0:T(512)S(1)} %broadcast_multiply_fusion.1), kind=kOutput, calls=%fused_computation.230 | convolution fusion | flops 4307550208 | bytes 13635584 | tf_op jit(solution)/shard_map/dot_general | solution.py:83
  13.1 1.9 copy-done.4
  15.4 28.2 %collective-permute-done = bf16[512,2048]{1,0:T(8,128)(2,1)} collective-permute-done((bf16[512,2048]{1,0:T(8,128)(2,1)S(1)}, bf16[512,2048]{1,0:T(8,128)(2,1)}, u32[]{:S(2)}, u32[]{:S(2)}) %collective-permute-start) | collective-permute-done | bytes 2097184 | tf_op jit(solution)/shard_map/ppermute | solution.py:12
  44.2 4.4 %collective-permute-start.4 = (bf16[1,1024]{1,0:T(2,128)(2,1)}, bf16[1,1024]{1,0:T(2,128)(2,1)}, u32[]{:S(2)}, u32[]{:S(2)}) collective-permute-start(bf16[1,1024]{1,0:T(2,128)(2,1)} %slice.355), channel_id=1, source_target_pairs={{0,15},{1,0},{2,1},{3,2},{4,3},{5,4},{6,5},{7,6},{8,7},{9,8},{10,9... | collective-permute-start | bytes 6152 | tf_op jit(solution)/shard_map/ppermute | solution.py:12
  48.8 2.8 select_reduce_fusion.1
  53.9 4.2 %all-to-all-start = ((bf16[16,16,1024]{2,1,0:T(8,128)(2,1)}), bf16[16,16,1024]{2,1,0:T(8,128)(2,1)}, u32[]{:S(2)}, u32[]{:S(2)}) async-start(bf16[16,16,1024]{2,1,0:T(8,128)(2,1)} %bitcast.200), calls=%async_computation | async-start | bytes 1048576 | tf_op jit(solution)/shard_map/all_to_all | solution.py:152
  58.2 18.3 %collective-permute-done.1 = bf16[512,2048]{1,0:T(8,128)(2,1)} collective-permute-done((bf16[512,2048]{1,0:T(8,128)(2,1)}, bf16[512,2048]{1,0:T(8,128)(2,1)}, u32[]{:S(2)}, u32[]{:S(2)}) %collective-permute-start.1) | collective-permute-done | bytes 2097184 | tf_op jit(solution)/shard_map/ppermute | solution.py:12
  76.7 3.6 %fusion.90 = (bf16[512,1024]{1,0:T(8,128)(2,1)}, bf16[512,1024]{1,0:T(8,128)(2,1)}, bf16[512,1024]{1,0:T(8,128)(2,1)}) fusion(bf16[512,4096]{1,0:T(8,128)(2,1)} %copy-done.4), kind=kLoop, calls=%fused_computation.399 | loop fusion | bytes 6291456 | tf_op jit(solution)/shard_map/slice | solution.py:94
  80.5 2.3 copy.77
  82.8 2.3 copy.76
  85.1 2.3 copy.78
  88.6 6.3 %fusion.67 = (pred[512,512]{1,0:T(8,128)(4,1)S(1)}, pred[512,512]{1,0:T(8,128)(4,1)}, pred[512,512]{1,0:T(8,128)(4,1)}, pred[512,512]{1,0:T(8,128)(4,1)}, pred[5...) fusion(s32[512]{0:T(512)S(1)} %get-tuple-element.260, ...), kind=kLoop, calls=%fused_computation.296 | loop fusion | flops 16777216 | bytes 4460544 | tf_op jit(solution)/shard_map/and | solution.py:44
  95.0 10.3 %collective-permute-done.2 = bf16[512,2048]{1,0:T(8,128)(2,1)} collective-permute-done((bf16[512,2048]{1,0:T(8,128)(2,1)}, bf16[512,2048]{1,0:T(8,128)(2,1)}, u32[]{:S(2)}, u32[]{:S(2)}) %collective-permute-start.2) | collective-permute-done | bytes 2097184 | tf_op jit(solution)/shard_map/ppermute | solution.py:12
  105.3 38.3 %fusion.24 = f32[16,64,512]{2,1,0:T(8,128)} fusion(bf16[512,16,64]{0,2,1:T(8,128)(2,1)} %bitcast.206, bf16[512,16,64]{0,2,1:T(8,128)(2,1)} %bitcast.201, bf16[512,16,64]{0,2,1:T(8,128)(2,1)} %bitcast.207, f32[16]{0:T(128)S(1)} %get-tuple-element.240, f32[16]{0:T(128)S(1)} %get-tuple-element.241, f32[16]{0:T(128)S(1)} %get-tuple-element.242, ...), kind=kOutput, calls=%fused_computation.225 | convolution fusion | flops 1174405120 | bytes 9700352 | tf_op jit(solution)/shard_map/hqk,khd->qhd/dot_general | solution.py:48
  164.2 41.2 %conditional.4 = (f32[512,16,64]{0,2,1:T(8,128)}) conditional(s32[]{:T(128)} %convert_element_type.4005, () %tuple.32, (s32[512]{0:T(512)S(1)}, s32[512]{0:T(512)S(1)}, s32[512]{0:T(512)S(1)}, s32[512]{0:T(512)S(1)}, bf16[512,2048]{1,0:T(8,128)(2,1)}, /*index=5*/bf16[512,16,64]{0,2,1:T(8,128)(2,1)}, f32[16,16]{1,0:T(8,128)S(1)}) %tuple.245), branch_computations={%region_6.7_spmd, %region_7.8_spmd} | conditional | flops 1191182336 | bytes 26752036 | solution.py:124
  164.3 6.3 %fusion.2 = (pred[512,512]{1,0:T(8,128)(4,1)S(1)}, pred[512,512]{1,0:T(8,128)(4,1)}, pred[512,512]{1,0:T(8,128)(4,1)}, pred[512,512]{1,0:T(8,128)(4,1)}, pred[51...) fusion(s32[512]{0:T(512)S(1)} %get-tuple-element.63, ...), kind=kLoop, calls=%fused_computation.20 | loop fusion | flops 16777216 | bytes 4464640 | tf_op jit(solution)/shard_map/cond/branch_1_fun/and | solution.py:44
  170.7 3.9 %copy.79 = bf16[512,2048]{0,1:T(8,128)(2,1)} copy(bf16[512,2048]{1,0:T(8,128)(2,1)} %get-tuple-element.215) | data formatting | bytes 4194304 | tf_op jit(solution)/shard_map
  174.6 3.0 %fusion.86 = (bf16[512,1024]{0,1:T(8,128)(2,1)}, bf16[512,1024]{0,1:T(8,128)(2,1)}) fusion(bf16[512,2048]{0,1:T(8,128)(2,1)} %copy.79), kind=kLoop, calls=%fused_computation.395 | loop fusion | bytes 4194304 | tf_op jit(solution)/shard_map/cond/branch_1_fun/slice | solution.py:94
  177.6 27.5 %fusion.1 = f32[512,16,64]{0,2,1:T(8,128)} fusion(bf16[512,16,64]{0,2,1:T(8,128)(2,1)} %bitcast.209, bf16[512,16,64]{0,2,1:T(8,128)(2,1)S(1)} %copy-done.6, bf16[512,16,64]{0,2,1:T(8,128)(2,1)} %bitcast.208, f32[16]{0:T(128)S(1)} %get-tuple-element.284, f32[16]{0:T(128)S(1)} %get-tuple-element.270, f32[16]{0:T(128)S(1)} %get-tuple-element.271, ...), kind=kOutput, calls=%fused_computation.18 | convolution fusion | flops 1174405120 | bytes 9700352 | tf_op jit(solution)/shard_map/cond/branch_1_fun/hqk,khd->qhd/dot_general | solution.py:48
  205.5 10.2 %conditional.5 = (f32[512,16,64]{0,2,1:T(8,128)}) conditional(s32[]{:T(128)} %convert_element_type.4007, () %tuple.34, (s32[512]{0:T(512)S(1)}, s32[512]{0:T(512)S(1)}, s32[512]{0:T(512)S(1)}, s32[512]{0:T(512)S(1)}, bf16[512,2048]{1,0:T(8,128)(2,1)}, /*index=5*/bf16[512,16,64]{0,2,1:T(8,128)(2,1)}, f32[16,16]{1,0:T(8,128)S(1)}) %tuple.246), branch_computations={%region_10.11_spmd, %region_11.12_spmd} | conditional | flops 1191182336 | bytes 26752036 | solution.py:124
  205.5 1.6 broadcast.6248
  215.7 10.3 %conditional.6 = (f32[512,16,64]{0,2,1:T(8,128)}) conditional(s32[]{:T(128)} %convert_element_type.4009, () %tuple.36, (s32[512]{0:T(512)S(1)}, s32[512]{0:T(512)S(1)}, s32[512]{0:T(512)S(1)}, s32[512]{0:T(512)S(1)}, bf16[512,2048]{1,0:T(8,128)(2,1)}, /*index=5*/bf16[512,16,64]{0,2,1:T(8,128)(2,1)}, f32[16,16]{1,0:T(8,128)S(1)}) %tuple.247), branch_computations={%region_14.15_spmd, %region_15.16_spmd} | conditional | flops 1191182336 | bytes 26752036 | solution.py:124
  226.0 41.1 %conditional.7 = (f32[512,16,64]{0,2,1:T(8,128)}) conditional(s32[]{:T(128)} %convert_element_type.4011, () %tuple.38, (s32[512]{0:T(512)S(1)}, s32[512]{0:T(512)S(1)}, s32[512]{0:T(512)S(1)}, s32[512]{0:T(512)S(1)}, bf16[512,2048]{1,0:T(8,128)(2,1)}, /*index=5*/bf16[512,16,64]{0,2,1:T(8,128)(2,1)}, f32[16,16]{1,0:T(8,128)S(1)}) %tuple.250), branch_computations={%region_18.19_spmd, %region_19.20_spmd} | conditional | flops 1191182336 | bytes 26752036 | solution.py:124
  226.1 6.4 %fusion.20 = (pred[512,512]{1,0:T(8,128)(4,1)S(1)}, pred[512,512]{1,0:T(8,128)(4,1)}, pred[512,512]{1,0:T(8,128)(4,1)}, pred[512,512]{1,0:T(8,128)(4,1)}, pred[5...) fusion(s32[512]{0:T(512)S(1)} %get-tuple-element.92, ...), kind=kLoop, calls=%fused_computation.188 | loop fusion | flops 16777216 | bytes 4464640 | tf_op jit(solution)/shard_map/cond/branch_1_fun/and | solution.py:44
  232.5 3.9 %copy.85 = bf16[512,2048]{0,1:T(8,128)(2,1)} copy(bf16[512,2048]{1,0:T(8,128)(2,1)} %get-tuple-element.236) | data formatting | bytes 4194304 | tf_op jit(solution)/shard_map
  236.4 3.0 %fusion.89 = (bf16[512,1024]{0,1:T(8,128)(2,1)}, bf16[512,1024]{0,1:T(8,128)(2,1)}) fusion(bf16[512,2048]{0,1:T(8,128)(2,1)} %copy.85), kind=kLoop, calls=%fused_computation.398 | loop fusion | bytes 4194304 | tf_op jit(solution)/shard_map/cond/branch_1_fun/slice | solution.py:94
  239.5 27.5 %fusion.19 = f32[512,16,64]{0,2,1:T(8,128)} fusion(bf16[512,16,64]{0,2,1:T(8,128)(2,1)} %bitcast.215, bf16[512,16,64]{0,2,1:T(8,128)(2,1)S(1)} %copy-done.9, bf16[512,16,64]{0,2,1:T(8,128)(2,1)} %bitcast.214, f32[16]{0:T(128)S(1)} %get-tuple-element.389, f32[16]{0:T(128)S(1)} %get-tuple-element.375, f32[16]{0:T(128)S(1)} %get-tuple-element.376, ...), kind=kOutput, calls=%fused_computation.186 | convolution fusion | flops 1174405120 | bytes 9700352 | tf_op jit(solution)/shard_map/cond/branch_1_fun/hqk,khd->qhd/dot_general | solution.py:48
  267.2 5.5 %fusion.84 = (f32[512]{0:T(512)S(1)}, f32[512,16,64]{0,2,1:T(8,128)S(1)}) fusion(f32[512,16,64]{0,2,1:T(8,128)} %get-tuple-element.434, f32[512,16,64]{0,2,1:T(8,128)} %get-tuple-element.433, f32[512,16,64]{0,2,1:T(8,128)} %get-tuple-element.432, f32[512,16,64]{0,2,1:T(8,128)} %get-tuple-element.431, f32[16,64,512]{2,1,0:T(8,128)} %fusion.24), kind=kLoop, calls=%fused_computation.394 | loop fusion | flops 2620928 | bytes 12584960 | tf_op jit(solution)/shard_map/reduce_sum | solution.py:17
  274.3 2.9 %copy.87 = f32[512,1024]{1,0:T(8,128)} copy(f32[512,1024]{0,1:T(8,128)} %bitcast.199) | data formatting | bytes 4194304 | tf_op jit(solution)/shard_map/reshape | solution.py:125
  277.2 4.6 %multiply_reduce_fusion = (f32[512]{0:T(512)S(1)}, bf16[512,1024]{1,0:T(8,128)(2,1)}) fusion(bf16[1,1024]{1,0:T(2,128)(2,1)} %collective-permute-done.4, bf16[511,1024]{1,0:T(8,128)(2,1)} %slice.354, bf16[1024,1024]{1,0:T(8,128)(2,1)S(1)} %copy-done, f32[512,1024]{1,0:T(8,128)} %copy.87, bf16[512,4096]{1,0:T(8,128)(2,1)} %copy-done.4, ...), kind=kOutput, calls=%fused_computation.278 | convolution fusion | flops 1081605632 | bytes 8398848 | tf_op jit(solution)/shard_map/dot_general | solution.py:128
  282.4 2.7 fusion.55
  (90 shorter events, 18.9 us)
Async XLA Ops:
  0.6 276.6 %copy-start = (bf16[1024,1024]{1,0:T(8,128)(2,1)S(1)}, bf16[1024,1024]{1,0:T(8,128)(2,1)}, u32[]{:S(2)}) copy-start(bf16[1024,1024]{1,0:T(8,128)(2,1)} %param.17) | copy-start | bytes 6291460
  3.9 39.7 %copy-start.2 = (bf16[512,1024]{1,0:T(8,128)(2,1)S(1)}, bf16[512,1024]{1,0:T(8,128)(2,1)}, u32[]{:S(2)}) copy-start(bf16[512,1024]{1,0:T(8,128)(2,1)} %param.15) | copy-start | bytes 3145732
  3.9 44.8 %copy-start.10 = (s32[16,128]{1,0:T(8,128)S(1)}, s32[16,128]{1,0:T(8,128)}, u32[]{:S(2)}) copy-start(s32[16,128]{1,0:T(8,128)} %param.21) | copy-start | bytes 24580
  13.1 1.9 copy-start.4
  15.1 65.3 %copy-start.18 = (s32[4]{0:T(128)S(1)}, s32[4]{0:T(128)}, u32[]{:S(2)}) copy-start(s32[4]{0:T(128)} %param.19) | copy-start | bytes 52
  15.3 72.2 %copy-start.5 = (f32[16,16]{1,0:T(8,128)S(1)}, f32[16,16]{1,0:T(8,128)}, u32[]{:S(2)}) copy-start(f32[16,16]{1,0:T(8,128)} %param.18) | copy-start | bytes 3076
  15.3 28.3 %collective-permute-start = (bf16[512,2048]{1,0:T(8,128)(2,1)S(1)}, bf16[512,2048]{1,0:T(8,128)(2,1)}, u32[]{:S(2)}, u32[]{:S(2)}) collective-permute-start(bf16[512,2048]{1,0:T(8,128)(2,1)S(1)} %slice.431), channel_id=1, source_target_pairs={{0,1},{1,2},{2,3},{3,4},{4,5},{5,6},{6,7},{7,8},{8,9},{9,10},{10,1... | collective-permute-start | bytes 6291464 | tf_op jit(solution)/shard_map/ppermute | solution.py:12
  43.6 32.8 %collective-permute-start.1 = (bf16[512,2048]{1,0:T(8,128)(2,1)}, bf16[512,2048]{1,0:T(8,128)(2,1)}, u32[]{:S(2)}, u32[]{:S(2)}) collective-permute-start(bf16[512,2048]{1,0:T(8,128)(2,1)} %collective-permute-done), channel_id=1, source_target_pairs={{0,1},{1,2},{2,3},{3,4},{4,5},{5,6},{6,7},{7,8},{8,9},{9,10},{10,1... | collective-permute-start | bytes 6291464 | tf_op jit(solution)/shard_map/ppermute | solution.py:12
  44.2 233.0 %collective-permute-start.4 = (bf16[1,1024]{1,0:T(2,128)(2,1)}, bf16[1,1024]{1,0:T(2,128)(2,1)}, u32[]{:S(2)}, u32[]{:S(2)}) collective-permute-start(bf16[1,1024]{1,0:T(2,128)(2,1)} %slice.355), channel_id=1, source_target_pairs={{0,15},{1,0},{2,1},{3,2},{4,3},{5,4},{6,5},{7,6},{8,7},{9,8},{10,9... | collective-permute-start | bytes 6152 | tf_op jit(solution)/shard_map/ppermute | solution.py:12
  53.9 228.5 %all-to-all-start = ((bf16[16,16,1024]{2,1,0:T(8,128)(2,1)}), bf16[16,16,1024]{2,1,0:T(8,128)(2,1)}, u32[]{:S(2)}, u32[]{:S(2)}) async-start(bf16[16,16,1024]{2,1,0:T(8,128)(2,1)} %bitcast.200), calls=%async_computation | async-start | bytes 1048576 | tf_op jit(solution)/shard_map/all_to_all | solution.py:152
  76.4 28.8 %collective-permute-start.2 = (bf16[512,2048]{1,0:T(8,128)(2,1)}, bf16[512,2048]{1,0:T(8,128)(2,1)}, u32[]{:S(2)}, u32[]{:S(2)}) collective-permute-start(bf16[512,2048]{1,0:T(8,128)(2,1)} %collective-permute-done.1), channel_id=1, source_target_pairs={{0,1},{1,2},{2,3},{3,4},{4,5},{5,6},{6,7},{7,8},{8,9},{9,10},{10,1... | collective-permute-start | bytes 6291464 | tf_op jit(solution)/shard_map/ppermute | solution.py:12
  87.4 58.2 %copy-start.11 = (s32[512]{0:T(512)}, s32[512]{0:T(512)S(1)}, u32[]{:S(2)}) copy-start(s32[512]{0:T(512)S(1)} %add_select_fusion.2) | copy-start | bytes 6148
  88.6 67.4 %copy-start.13 = (s32[512]{0:T(512)}, s32[512]{0:T(512)S(1)}, u32[]{:S(2)}) copy-start(s32[512]{0:T(512)S(1)} %get-tuple-element.259) | copy-start | bytes 6148
  105.3 120.8 %collective-permute-start.3 = (bf16[512,2048]{1,0:T(8,128)(2,1)}, bf16[512,2048]{1,0:T(8,128)(2,1)}, u32[]{:S(2)}, u32[]{:S(2)}) collective-permute-start(bf16[512,2048]{1,0:T(8,128)(2,1)} %collective-permute-done.2), channel_id=1, source_target_pairs={{0,1},{1,2},{2,3},{3,4},{4,5},{5,6},{6,7},{7,8},{8,9},{9,10},{10,1... | collective-permute-start | bytes 6291464 | tf_op jit(solution)/shard_map/ppermute | solution.py:12
  105.3 45.8 %copy-start.17 = (s32[1,2]{1,0:T(1,128)S(1)}, s32[1,2]{1,0:T(1,128)}, u32[]{:S(2)}) copy-start(s32[1,2]{1,0:T(1,128)} %param.20) | copy-start | bytes 28
  164.2 13.4 %copy-start.6 = (bf16[512,16,64]{0,2,1:T(8,128)(2,1)S(1)}, bf16[512,16,64]{0,2,1:T(8,128)(2,1)}, u32[]{:S(2)}) copy-start(bf16[512,16,64]{0,2,1:T(8,128)(2,1)} %get-tuple-element.72) | copy-start | bytes 3145732 | tf_op jit(solution)/shard_map/cond
  215.7 10.3 %copy-start.12 = (s32[512]{0:T(512)S(1)}, s32[512]{0:T(512)}, u32[]{:S(2)}) copy-start(s32[512]{0:T(512)} %copy-done.11) | copy-start | bytes 6148
  215.7 10.3 %copy-start.14 = (s32[512]{0:T(512)S(1)}, s32[512]{0:T(512)}, u32[]{:S(2)}) copy-start(s32[512]{0:T(512)} %copy-done.13) | copy-start | bytes 6148
  226.1 13.4 %copy-start.9 = (bf16[512,16,64]{0,2,1:T(8,128)(2,1)S(1)}, bf16[512,16,64]{0,2,1:T(8,128)(2,1)}, u32[]{:S(2)}) copy-start(bf16[512,16,64]{0,2,1:T(8,128)(2,1)} %get-tuple-element.93) | copy-start | bytes 3145732 | tf_op jit(solution)/shard_map/cond
  267.2 10.0 %copy-start.3 = (bf16[512,1024]{1,0:T(8,128)(2,1)S(1)}, bf16[512,1024]{1,0:T(8,128)(2,1)}, u32[]{:S(2)}) copy-start(bf16[512,1024]{1,0:T(8,128)(2,1)} %param.15) | copy-start | bytes 3145732
  272.7 1.3 copy-start.1
  274.0 7.8 %copy-start.15 = (s32[512]{0:T(512)S(1)}, s32[512]{0:T(512)}, u32[]{:S(2)}) copy-start(s32[512]{0:T(512)} %get-tuple-element.255) | copy-start | bytes 6148
  274.0 8.4 %copy-start.16 = (s32[128]{0:T(128)S(1)}, s32[128]{0:T(128)}, u32[]{:S(2)}) copy-start(s32[128]{0:T(128)} %add_add_fusion.1) | copy-start | bytes 1540
where the time goes:
time: 290 us; the launch traced here: 286 us
  matrix products  111 us (38%)
  waiting for transfers between devices  56.8 us (20%)
  local copies, waits for them, and re-layouts  42.3 us (15%)
  other arithmetic  34.8 us (12%)
  loops' own time  18 us (6%)
  between operations  13.6 us (5%)
  starting transfers between devices  8.98 us (3%)
    dot_general x3, matrix products, attend(): jnp.einsum('hqk,khd->qhd', weights, value_rows, preferred_element_type=jn...  93.3 us
    ppermute x5, waiting for transfers between devices, passed_along(): return lax.ppermute(value, axis, pairs)  56.8 us
    and x3, other arithmetic, attend(): allowed = (distance >= 0) & (query_user[:, None] == key_user[None, :])  19.1 us
    another operation x4, loops' own time, shards(): lax.cond(useful, contribute, nothing, (carried, key_pos, key_user))  18 us
    slice x4, local copies, waits for them, and re-layouts, split_pair(): paired[:, hidden_width:].reshape(event_row_count, head_count, head_size)  11.9 us
    another operation x6, local copies, waits for them, and re-layouts  11.2 us
    dot_general x1, matrix products, shards(): jnp.dot(normed, w_in, preferred_element_type=jnp.float32)  9.21 us
    reduce_sum x2, other arithmetic, layer_norm(): center = values - jnp.mean(values, -1, keepdims=True)  7.04 us
  transfers between devices with their start and end apart: 6, of which 3 were waited for; matrix products, arithmetic and copies ran while one was open for 59% of the time, Pallas kernels for 0%

commit v1 on v0

v1 whole, which is shorter than its diff:
```python
import functools

import jax
import jax.numpy as jnp
from jax import lax
from jax.experimental import pallas as pl
from jax.experimental.pallas import tpu as pltpu
from jax.sharding import PartitionSpec as P

BLOCKED = -1e9
LANES = 128
F32 = jnp.float32
BF16 = jnp.bfloat16
VMEM_BYTES = 56 * 2**20
NT = (((1,), (1,)), ((), ()))


def passed_along(value, pairs):
    return lax.ppermute(value, "ctx", pairs)


def centered(values):
    center = values - jnp.mean(values, -1, keepdims=True)
    spread = jnp.mean(center * center, -1, keepdims=True)
    return center * lax.rsqrt(spread + 1e-05)


def silu_of_half(half):
    return half * jnp.tanh(half) + half


def iota(shape, dim):
    return lax.broadcasted_iota(jnp.int32, shape, dim)


def time_base(block, count, rows):
    total = count * rows
    return lax.rem(block * rows + total // 4, total)


def starts_of(times, lengths_ref):
    end = jnp.int32(0)
    start = jnp.zeros_like(times)
    for user in range(lengths_ref.shape[0]):
        length = lengths_ref[user]
        end = end + length
        start = start + jnp.where(times >= end, length, 0)
    return start


def half_bias(rel_ref, head, bucket):
    return rel_ref[head, bucket] * 0.5


def bias_chain(distance, rel_ref, head, low, first, last):
    tile = jnp.full(distance.shape, half_bias(rel_ref, head, low), F32)
    for degree in range(first, last):
        tile = jnp.where(distance >= 2**degree, half_bias(rel_ref, head, degree + 1), tile)
    return tile


def head_rows(size, width, value):
    lane = iota((1, width), 1)
    return [
        jnp.where((lane >= size * num) & (lane < size * (num + 1)), value, 0.0).astype(BF16)
        for num in range(width // size)
    ]


def request_kernel(slot_cap, cand_ref, events_ref, out_ref):
    me = lax.axis_index("ctx")
    count, wanted = cand_ref.shape
    rows = events_ref.shape[0]
    slots = count * slot_cap
    cand = cand_ref[...]
    local = cand - me * rows
    mine = (local >= 0) & (local < rows)
    earlier = (iota((wanted, wanted), 0) < iota((wanted, wanted), 1)).astype(BF16)
    rank = jnp.dot(jnp.where(mine, 1.0, 0.0).astype(BF16), earlier, preferred_element_type=F32)
    code = jnp.where(mine, rank * rows + local.astype(F32), -1.0)
    slot_num = iota((slots, count), 0) - iota((slots, count), 1) * slot_cap
    spread = jnp.where((slot_num >= 0) & (slot_num < slot_cap), 1.0, 0.0)
    asked = jnp.dot(spread, code, preferred_element_type=F32, precision=lax.Precision.HIGHEST)
    slot = lax.rem(iota((slots, wanted), 0), slot_cap).astype(F32)
    found = asked - slot * rows
    ids = jnp.sum(jnp.where((found >= 0.0) & (found < rows), found + 1.0, 0.0), 1, keepdims=True)
    picks = (ids.astype(jnp.int32) - 1 == iota((slots, rows), 1)).astype(BF16)
    out_ref[...] = jnp.dot(picks, events_ref[...], preferred_element_type=F32).astype(BF16)


def project_kernel(events_ref, w_ref, out_ref, normed_ref):
    @pl.when(pl.program_id(0) == 0)
    def _():
        normed_ref[...] = centered(events_ref[...].astype(F32)).astype(BF16)

    value = jnp.dot(normed_ref[...], w_ref[...], preferred_element_type=F32)
    out_ref[...] = silu_of_half(0.5 * value).astype(BF16)


def own_kernel(head_size, lengths_ref, rel_ref, q_ref, v_ref, k_ref, out_ref, mask_ref):
    group = pl.program_id(0)
    rows, width = q_ref.shape
    half = rows // 2
    heads = width // head_size
    count = lax.axis_size("ctx")

    @pl.when(group == 0)
    def _():
        base = time_base(lax.axis_index("ctx"), count, rows)
        start = starts_of(base + iota((rows, LANES), 0), lengths_ref)
        for num in range(rows // LANES):
            key_time = base + num * LANES + iota((rows, LANES), 1)
            mask_ref[:, num * LANES : (num + 1) * LANES] = jnp.where(key_time >= start, 0.0, BLOCKED)

    away = iota((LANES, LANES), 0) - iota((LANES, LANES), 1)
    queries, values, keys = q_ref[...], v_ref[...], k_ref[...]
    scaled = head_rows(head_size, width, 0.5 * head_size**-0.5)
    chosen = head_rows(head_size, width, 1.0)
    parts = [([], []), ([], [])]
    for num in range(heads):
        head = group * heads + num
        tiles = [
            jnp.where(away < 0, BLOCKED, bias_chain(away, rel_ref, head, 0, 0, 7)),
            bias_chain(away + LANES, rel_ref, head, 1, 1, 8),
            jnp.where(away >= 0, half_bias(rel_ref, head, 9), half_bias(rel_ref, head, 8)),
            half_bias(rel_ref, head, 9),
        ]
        head_queries = queries * scaled[num]
        head_values = values * chosen[num]
        for part in range(2):
            seen = (part + 1) * half
            scores = lax.dot_general(
                head_queries[part * half : (part + 1) * half],
                keys[:seen],
                NT,
                preferred_element_type=F32,
            )
            lines = []
            for q_sub in range(half // LANES):
                q_tile = part * (half // LANES) + q_sub
                line = []
                for k_tile in range(seen // LANES):
                    if k_tile > q_tile:
                        line.append(jnp.zeros((LANES, LANES), BF16))
                        continue
                    part_scores = scores[
                        q_sub * LANES : (q_sub + 1) * LANES, k_tile * LANES : (k_tile + 1) * LANES
                    ]
                    mask = mask_ref[
                        q_tile * LANES : (q_tile + 1) * LANES, k_tile * LANES : (k_tile + 1) * LANES
                    ]
                    line.append(
                        silu_of_half(part_scores + tiles[q_tile - k_tile] + mask).astype(BF16)
                    )
                lines.append(jnp.concatenate(line, 1))
            parts[part][0].append(jnp.concatenate(lines, 0))
            parts[part][1].append(head_values[:seen])
    for part in range(2):
        weights = jnp.concatenate(parts[part][0], 1)
        stacked = jnp.concatenate(parts[part][1], 0)
        out_ref[part * half : (part + 1) * half] = jnp.dot(
            weights, stacked, preferred_element_type=F32
        )


def picks_kernel(chunk, last, head_size, slot_cap, *refs):
    lengths_ref, lists_ref, rel_ref, q_ref, before_ref = refs[:5]
    over_ref, far_ref, over_twin_ref, far_twin_ref, own_twin_ref, w_ref = refs[5:11]
    if last:
        gate_ref, events_ref, next_ref, flat_ref, cand_ref, w_out_ref = refs[11:17]
        layer_ref, score_ref, table_ref = refs[17:20]
        acc_ref, rows_ref, w_buf, pair_ref, mask_ref, near_ref, sems, out_buf = refs[20:]
    else:
        acc_ref = refs[11]
        rows_ref, w_buf, pair_ref, mask_ref, near_ref, sems = refs[12:]
    me = lax.axis_index("ctx")
    count = lax.axis_size("ctx")
    rows, hidden = q_ref.shape
    half = far_ref.shape[0]
    picks = lists_ref.shape[1]
    head_count, _ = rel_ref.shape
    second = lax.rem(me, 2) == 1
    shared = chunk * half

    copies = []
    for pick in range(picks):
        away = lists_ref[0, pick]
        target = rows_ref.at[pl.ds(pick * half, half)]
        sources = [
            (away == 2, over_ref),
            (away == 4, far_ref),
            (((away == 1) & jnp.logical_not(second)) | ((away == 3) & second), over_twin_ref),
            ((away == 3) & jnp.logical_not(second), far_twin_ref),
            ((away == 1) & second, own_twin_ref.at[pl.ds(shared, half)]),
        ]
        for flag, source in sources:

            @pl.when(flag)
            def _():
                pltpu.make_async_copy(source, target, sems.at[pick]).start()

        copies.append(pltpu.make_async_copy(over_ref, target, sems.at[pick]))
    step = hidden // 2
    weight_copies = []
    for part in range(2 * hidden // step):
        copy = pltpu.make_async_copy(
            w_ref.at[:, pl.ds(2 * hidden + part * step, step)],
            w_buf.at[:, pl.ds(part * step, step)],
            sems.at[picks + part],
        )
        copy.start()
        weight_copies.append(copy)
    if last:
        out_copy = pltpu.make_async_copy(w_out_ref, out_buf, sems.at[picks + 2 * hidden // step])
        out_copy.start()
    acc_ref[...] = before_ref[...]
    for copy in copies:
        copy.wait()
    normed = centered(rows_ref[...].astype(F32)).astype(BF16)
    for part, copy in enumerate(weight_copies):
        copy.wait()
        columns = pl.ds(part * step, step)
        value = jnp.dot(normed, w_buf[:, columns], preferred_element_type=F32)
        pair_ref[:, columns] = silu_of_half(0.5 * value).astype(BF16)

    base = time_base(me, count, rows)
    first_start = starts_of(base, lengths_ref)
    gap = iota((LANES, LANES), 0) - iota((LANES, LANES), 1)
    width = 4 * head_size
    scaled = head_rows(head_size, width, 0.5 * head_size**-0.5)
    chosen = head_rows(head_size, width, 1.0)
    q_tiles, k_tiles = rows // LANES, half // LANES
    shift = chunk * k_tiles

    @pl.loop(0, picks)
    def _(pick):
        away = lists_ref[0, pick]
        block = lax.rem(me - away + count, count)
        block_base = time_base(block, count, rows)
        key_base = block_base + shared
        useful = (block_base < base) & (key_base + half - 1 >= first_start)

        @pl.when(useful)
        def _():
            start = starts_of(base + iota((rows, LANES), 0), lengths_ref)
            for tile in range(k_tiles):
                key_time = key_base + tile * LANES + iota((rows, LANES), 1)
                mask_ref[:, tile * LANES : (tile + 1) * LANES] = jnp.where(
                    key_time >= start, 0.0, BLOCKED
                )
            lows, highs = {}, {}
            for diff in range(-(shift + k_tiles - 1), q_tiles - shift):
                delta = away * rows + diff * LANES
                bucket, power = jnp.int32(8), jnp.int32(0)
                for degree in range(8, rel_ref.shape[1] - 1):
                    bucket = bucket + (delta >= 2**degree).astype(jnp.int32)
                    power = power + (delta == 2**degree).astype(jnp.int32)
                highs[diff] = bucket
                lows[diff] = bucket - power
            special = 1 - q_tiles
            if special in highs:

                @pl.when(away == 1)
                def _():
                    @pl.loop(0, head_count)
                    def _(head):
                        near_ref[head] = bias_chain(gap + LANES, rel_ref, head, 1, 1, 8)

                @pl.when(away != 1)
                def _():
                    @pl.loop(0, head_count)
                    def _(head):
                        near_ref[head] = jnp.full(
                            gap.shape, half_bias(rel_ref, head, highs[special]), F32
                        )

            key_rows = pl.ds(pl.multiple_of(pick * half, half), half)
            for group in range(hidden // width):
                columns = slice(group * width, (group + 1) * width)
                queries = q_ref[:, columns]
                values = pair_ref[key_rows, columns]
                keys = pair_ref[key_rows, hidden + group * width : hidden + (group + 1) * width]
                weights, stacked = [], []
                for num in range(width // head_size):
                    head = group * (width // head_size) + num
                    scores = lax.dot_general(
                        queries * scaled[num], keys, NT, preferred_element_type=F32
                    )
                    lines = []
                    for q_tile in range(q_tiles):
                        line = []
                        for k_tile in range(k_tiles):
                            diff = q_tile - k_tile - shift
                            if diff == special:
                                bias = near_ref[head]
                            elif diff in (0, 2 - q_tiles):
                                bias = jnp.where(
                                    gap >= 0,
                                    half_bias(rel_ref, head, highs[diff]),
                                    half_bias(rel_ref, head, lows[diff]),
                                )
                            else:
                                bias = half_bias(rel_ref, head, highs[diff])
                            spot = (
                                slice(q_tile * LANES, (q_tile + 1) * LANES),
                                slice(k_tile * LANES, (k_tile + 1) * LANES),
                            )
                            line.append(
                                silu_of_half(scores[spot] + bias + mask_ref[spot]).astype(BF16)
                            )
                        lines.append(jnp.concatenate(line, 1))
                    weights.append(jnp.concatenate(lines, 0))
                    stacked.append(values * chosen[num])
                acc_ref[:, columns] += jnp.dot(
                    jnp.concatenate(weights, 1),
                    jnp.concatenate(stacked, 0),
                    preferred_element_type=F32,
                )

    if not last:
        return
    wanted = cand_ref.shape[1]
    own = jnp.broadcast_to(cand_ref[pl.ds(me, 1), :].astype(F32), (wanted, wanted))
    diagonal = iota((wanted, wanted), 0) == iota((wanted, wanted), 1)
    own_column = jnp.sum(jnp.where(diagonal, own, 0.0), 1, keepdims=True)
    owner = jnp.floor(own * (1.0 / rows))
    owner_column = jnp.floor(own_column * (1.0 / rows))
    before = iota((wanted, wanted), 1) < iota((wanted, wanted), 0)
    rank = jnp.sum(jnp.where((owner == owner_column) & before, 1.0, 0.0), 1, keepdims=True)
    slot = (owner_column * slot_cap + rank).astype(jnp.int32)
    hits = (slot == iota((wanted, flat_ref.shape[0]), 1)).astype(BF16)
    listed = jnp.dot(hits, flat_ref[...], preferred_element_type=F32).astype(BF16)
    out_copy.wait()
    scale = hidden**-0.5
    total = count * rows
    for part in range(2):
        block_rows = slice(part * half, (part + 1) * half)
        gated = centered(acc_ref[block_rows]) * gate_ref[block_rows].astype(F32)
        layer = events_ref[block_rows].astype(F32) + jnp.dot(
            gated.astype(BF16), out_buf[...], preferred_element_type=F32
        )
        layer = layer.astype(BF16)
        layer_ref[block_rows] = layer
        table_ref[block_rows] = (
            lax.dot_general(layer, listed, NT, preferred_element_type=F32) * scale
        )
        following = pltpu.roll(events_ref[block_rows].astype(F32), half - 1, 0)
        if part == 0:
            after = events_ref[half : half + 16][:1].astype(F32)
        else:
            after = next_ref[...][:1].astype(F32)
        following = jnp.where(iota((half, hidden), 0) == half - 1, after, following)
        inner = jnp.sum(layer.astype(F32) * following, 1, keepdims=True) * scale
        for tile in range(half // LANES):
            spot = inner[tile * LANES : (tile + 1) * LANES]
            line = jnp.sum(jnp.where(diagonal, spot, 0.0), 0, keepdims=True)
            offset = part * half + tile * LANES
            coming = base + offset + 1 + iota((1, LANES), 1)
            same = coming < total
            end = jnp.int32(0)
            for user in range(lengths_ref.shape[0]):
                end = end + lengths_ref[user]
                same = same & (coming != end)
            score_ref[offset // LANES : offset // LANES + 1] = jnp.where(same, line, 0.0)


def smem():
    return pl.BlockSpec(memory_space=pltpu.SMEM)


def vmem():
    return pl.BlockSpec(memory_space=pltpu.VMEM)


def anywhere():
    return pl.BlockSpec(memory_space=pl.ANY)


def params(*semantics):
    return pltpu.CompilerParams(
        dimension_semantics=semantics or None, vmem_limit_bytes=VMEM_BYTES
    )


def shards(events, w_in, w_out, rel_bias, lengths, block_lists, candidates):
    rows, hidden = events.shape
    head_count = rel_bias.shape[0]
    head_size = hidden // head_count
    count = lax.axis_size("ctx")
    me = lax.axis_index("ctx")
    wanted = candidates.shape[1]
    slot_cap = 2 * wanted // count
    slots = count * slot_cap
    half = rows // 2
    width = 4 * head_size
    picks = block_lists.shape[1]

    onward = [(s, (s + 4) % count) for s in range(count)]
    across = [(s, s ^ 2) for s in range(count)]
    twin = [(s, s ^ 1) for s in range(count)]
    back = [(s, (s - 1) % count) for s in range(count)]

    halves = [events[:half], events[half:]]
    far = [passed_along(h, onward) for h in halves]
    own_twin = passed_along(events, twin)
    next_first = passed_along(events[:1], back)

    fetched = pl.pallas_call(
        functools.partial(request_kernel, slot_cap),
        out_shape=jax.ShapeDtypeStruct((slots, hidden), BF16),
        in_specs=[vmem(), vmem()],
        out_specs=vmem(),
        compiler_params=params(),
        cost_estimate=pl.CostEstimate(flops=10**9, bytes_accessed=2**21, transcendentals=0),
        name="request",
    )(candidates, events)

    step = hidden // 2
    projected = pl.pallas_call(
        project_kernel,
        grid=(4 * hidden // step,),
        out_shape=jax.ShapeDtypeStruct((rows, 4 * hidden), BF16),
        in_specs=[
            pl.BlockSpec((rows, hidden), lambda i: (0, 0)),
            pl.BlockSpec((hidden, step), lambda i: (0, i)),
        ],
        out_specs=pl.BlockSpec((rows, step), lambda i: (0, i)),
        scratch_shapes=[pltpu.VMEM((rows, hidden), BF16)],
        compiler_params=params("arbitrary"),
        cost_estimate=pl.CostEstimate(flops=7 * 10**9, bytes_accessed=2**23, transcendentals=0),
        name="project",
    )(events, w_in)

    groups = hidden // width

    def columns(which):
        return pl.BlockSpec((rows, width), lambda i: (0, which * groups + i))

    attended = pl.pallas_call(
        functools.partial(own_kernel, head_size),
        grid=(groups,),
        out_shape=jax.ShapeDtypeStruct((rows, hidden), F32),
        in_specs=[smem(), smem(), columns(1), columns(2), columns(3)],
        out_specs=pl.BlockSpec((rows, width), lambda i: (0, i)),
        scratch_shapes=[pltpu.VMEM((rows, rows), F32)],
        compiler_params=params("arbitrary"),
        cost_estimate=pl.CostEstimate(flops=6 * 10**9, bytes_accessed=2**22, transcendentals=0),
        name="own",
    )(lengths, rel_bias, projected, projected, projected)

    lower = (me // 2) % 2 == 0
    over = [
        passed_along(jnp.where(lower, halves[i], far[i]), across) for i in range(2)
    ]
    far_twin = [passed_along(f, twin) for f in far]
    over_twin = [passed_along(o, twin) for o in over]
    fetched, _ = lax.optimization_barrier((fetched, far[1]))
    arrived = lax.all_to_all(
        fetched.reshape(count, slot_cap, hidden), "ctx", split_axis=0, concat_axis=0, tiled=True
    ).reshape(slots, hidden)

    def column_block(which):
        return pl.BlockSpec((rows, hidden), lambda i: (0, which))

    whole = lambda *shape: pl.BlockSpec(shape, lambda i: (0,) * len(shape))
    parts = 2 * hidden // step
    for i in range(2):
        last = i == 1
        in_specs = [smem(), smem(), smem(), column_block(1), whole(rows, hidden)]
        in_specs += [anywhere()] * 6
        operands = [lengths, block_lists, rel_bias, projected, attended]
        operands += [over[i], far[i], over_twin[i], far_twin[i], own_twin, w_in]
        scratch = [
            pltpu.VMEM((picks * half, hidden), BF16),
            pltpu.VMEM((hidden, 2 * hidden), BF16),
            pltpu.VMEM((picks * half, 2 * hidden), BF16),
            pltpu.VMEM((rows, half), F32),
            pltpu.VMEM((head_count, LANES, LANES), F32),
            pltpu.SemaphoreType.DMA((picks + parts + 1,)),
        ]
        if last:
            in_specs += [
                column_block(0),
                whole(rows, hidden),
                whole(1, hidden),
                whole(slots, hidden),
                whole(count, wanted),
                anywhere(),
            ]
            operands += [projected, events, next_first, arrived, candidates, w_out]
            out_shape = (
                jax.ShapeDtypeStruct((rows, hidden), BF16),
                jax.ShapeDtypeStruct((rows // LANES, LANES), F32),
                jax.ShapeDtypeStruct((rows, wanted), F32),
            )
            out_specs = (
                whole(rows, hidden),
                whole(rows // LANES, LANES),
                whole(rows, wanted),
            )
            scratch = (
                [pltpu.VMEM((rows, hidden), F32)]
                + scratch
                + [pltpu.VMEM((hidden, hidden), BF16)]
            )
        else:
            out_shape = jax.ShapeDtypeStruct((rows, hidden), F32)
            out_specs = whole(rows, hidden)
        attended = pl.pallas_call(
            functools.partial(picks_kernel, i, last, head_size, slot_cap),
            grid=(1,),
            out_shape=out_shape,
            in_specs=in_specs,
            out_specs=out_specs,
            scratch_shapes=scratch,
            compiler_params=params("arbitrary"),
            cost_estimate=pl.CostEstimate(
                flops=8 * 10**9, bytes_accessed=2**22, transcendentals=0
            ),
            name="last_picks" if last else "first_picks",
        )(*operands)
    layer_output, next_score, table = attended
    return (layer_output, next_score.reshape(rows), table)


def solution(mesh):
    in_specs = (
        P(("groups", "ctx"), None),
        P(),
        P(),
        P(),
        P("groups"),
        P(("groups", "ctx"), None),
        P("groups", None),
    )
    out_specs = (P(("groups", "ctx"), None), P(("groups", "ctx")), P(("groups", "ctx"), None))
    return jax.shard_map(shards, mesh=mesh, in_specs=in_specs, out_specs=out_specs, check_vma=False)
```

time: 290 us -> 99.2 us (0.34)
  the two profiles are of different devices: /device:TPU:2 before, /device:TPU:0 now
where the time goes in v1:
time: 99.2 us; the launch traced here: 98.7 us
  Pallas kernels  52.6 us (53%)
  waiting for transfers between devices  23.8 us (24%)
  starting transfers between devices  14.5 us (15%)
  local copies, waits for them, and re-layouts  4.67 us (5%)
  other arithmetic  2.14 us (2%)
    pallas_call x2, Pallas kernels, shards(): pl.pallas_call(functools.partial(picks_kernel, i, last, head_size, slot_c...  30.8 us
    ppermute x10, waiting for transfers between devices, passed_along(): return lax.ppermute(value, 'ctx', pairs)  23.8 us
    pallas_call x1, Pallas kernels, shards(): pl.pallas_call(project_kernel, grid=(4 * hidden // step,), out_shape=jax....  11.3 us
    ppermute x10, starting transfers between devices, passed_along(): return lax.ppermute(value, 'ctx', pairs)  10.8 us
    pallas_call x1, Pallas kernels, shards(): pl.pallas_call(functools.partial(own_kernel, head_size), grid=(groups,),...  7.42 us
    all_to_all x1, starting transfers between devices, shards(): lax.all_to_all(fetched.reshape(count, slot_cap, hidden), 'ctx', split_axi...  3.75 us
    unnamed x22, local copies, waits for them, and re-layouts  3.5 us
    pallas_call x1, Pallas kernels, shards(): pl.pallas_call(functools.partial(request_kernel, slot_cap), out_shape=jax...  3.05 us
  transfers between devices with their start and end apart: 11, of which 3 were waited for; matrix products, arithmetic and copies ran while one was open for 0% of the time, Pallas kernels for 36%

profile of v1, /device:TPU:0, one launch (start us, length us, event | category | flops | bytes accessed | tf_op | source)
XLA Modules:
  0.0 98.7 jit_solution(11959858698012786896)
XLA Ops:
  0.6 0.0 copy-start
  0.6 1.2 %slice.10 = bf16[256,1024]{1,0:T(8,128)(2,1)S(1)} slice(bf16[512,1024]{1,0:T(8,128)(2,1)} %refs_12_.1), slice={[256:512], [0:1024]} | slice | bytes 1048576 | tf_op jit(solution)/shard_map/slice | solution.py:403
  1.8 3.1 %collective-permute-start.5 = (bf16[256,1024]{1,0:T(8,128)(2,1)S(1)}, bf16[256,1024]{1,0:T(8,128)(2,1)S(1)}, u32[]{:S(2)}, u32[]{:S(2)}) collective-permute-start(bf16[256,1024]{1,0:T(8,128)(2,1)S(1)} %slice.10), channel_id=1, source_target_pairs={{0,4},{1,5},{2,6},{3,7},{4,8},{5,9},{6,10},{7,11},{8,12},{9,13},{1... | collective-permute-start | bytes 1572872 | tf_op jit(solution)/shard_map/ppermute | solution.py:19
  4.9 13.9 %collective-permute-done.5.refs_6_ = bf16[256,1024]{1,0:T(8,128)(2,1)S(1)} collective-permute-done((bf16[256,1024]{1,0:T(8,128)(2,1)S(1)}, bf16[256,1024]{1,0:T(8,128)(2,1)S(1)}, u32[]{:S(2)}, u32[]{:S(2)}) %collective-permute-start.5) | collective-permute-done | bytes 524320 | tf_op jit(solution)/shard_map/ppermute | solution.py:19
  18.8 0.8 copy-done.4
  19.6 2.1 %broadcast_select_fusion = (bf16[256,1024]{1,0:T(8,128)(2,1)}, bf16[256,1024]{1,0:T(8,128)(2,1)S(1)}) fusion(bf16[256,1024]{1,0:T(8,128)(2,1)S(1)} %collective-permute-done.5.refs_6_, pred[]{:T(512)S(6)} %eq.5, bf16[512,1024]{1,0:T(8,128)(2,1)} %refs_12_.1), kind=kLoop, calls=%fused_computation | loop fusion | flops 262144 | bytes 2621441 | tf_op jit(solution)/shard_map/jit(_where)/select_n | solution.py:453
  21.7 0.0 collective-permute-start
  21.7 0.1 collective-permute-start.4
  21.8 4.8 %collective-permute-start.9 = (bf16[1,1024]{1,0:T(2,128)(2,1)S(1)}, bf16[1,1024]{1,0:T(2,128)(2,1)S(1)}, u32[]{:S(2)}, u32[]{:S(2)}) collective-permute-start(bf16[1,1024]{1,0:T(2,128)(2,1)S(1)} %slice.11), channel_id=1, source_target_pairs={{0,15},{1,0},{2,1},{3,2},{4,3},{5,4},{6,5},{7,6},{8,7},{9,8},{10,9... | collective-permute-start | bytes 6152 | tf_op jit(solution)/shard_map/ppermute | solution.py:19
  26.6 3.1 %request.1 = bf16[256,1024]{1,0:T(8,128)(2,1)} custom-call(s32[16,128]{1,0:T(8,128)} %refs_15_.1, bf16[512,1024]{1,0:T(8,128)(2,1)} %refs_12_.1), custom_call_target="tpu_custom_call" | custom-call | flops 1000000000 | bytes 2097152 | tf_op jit(solution)/shard_map/request/pallas_call | solution.py:408
  29.7 7.0 %collective-permute-done.refs_6_ = bf16[256,1024]{1,0:T(8,128)(2,1)S(1)} collective-permute-done((bf16[256,1024]{1,0:T(8,128)(2,1)S(1)}, bf16[256,1024]{1,0:T(8,128)(2,1)S(1)}, u32[]{:S(2)}, u32[]{:S(2)}) %collective-permute-start) | collective-permute-done | bytes 524320 | tf_op jit(solution)/shard_map/ppermute | solution.py:19
  36.7 0.1 broadcast_select_fusion.1
  36.7 1.3 %collective-permute-start.1 = (bf16[256,1024]{1,0:T(8,128)(2,1)S(1)}, bf16[256,1024]{1,0:T(8,128)(2,1)}, u32[]{:S(2)}, u32[]{:S(2)}) collective-permute-start(bf16[256,1024]{1,0:T(8,128)(2,1)S(1)} %broadcast_select_fusion.1), channel_id=1, source_target_pairs={{0,2},{1,3},{2,0},{3,1},{4,6},{5,7},{6,4},{7,5},{8,10},{9,11},{10,... | collective-permute-start | bytes 1572872 | tf_op jit(solution)/shard_map/ppermute | solution.py:19
  38.0 11.3 %project.1.q_ref.v_ref.k_ref.refs_3_.refs_11_ = bf16[512,4096]{1,0:T(8,128)(2,1)} custom-call(bf16[512,1024]{1,0:T(8,128)(2,1)} %refs_12_.1, bf16[1024,4096]{1,0:T(8,128)(2,1)} %refs_10_.3), custom_call_target="tpu_custom_call" | custom-call | flops 7000000000 | bytes 8388608 | tf_op jit(solution)/shard_map/project/pallas_call | solution.py:419
  49.3 0.8 collective-permute-start.6
  50.1 3.8 %all-to-all-start = ((bf16[16,16,1024]{2,1,0:T(8,128)(2,1)}), bf16[16,16,1024]{2,1,0:T(8,128)(2,1)S(1)}, u32[]{:S(2)}, u32[]{:S(2)}) async-start(bf16[16,16,1024]{2,1,0:T(8,128)(2,1)} %bitcast), calls=%async_computation | async-start | bytes 1048576 | tf_op jit(solution)/shard_map/all_to_all | solution.py:458
  53.9 0.2 collective-permute-start.3
  54.1 0.0 collective-permute-done.1.refs_5_
  54.1 0.4 collective-permute-start.2
  54.5 7.4 %own.1.refs_4_ = f32[512,1024]{1,0:T(8,128)} custom-call(s32[4]{0:T(128)} %refs_0_.3, f32[16,16]{1,0:T(8,128)} %refs_2_.3, bf16[512,4096]{1,0:T(8,128)(2,1)} %project.1.q_ref.v_ref.k_ref.refs_3_.refs_11_, bf16[512,4096]{1,0:T(8,128)(2,1)} %project.1.q_ref.v_ref.k_ref.refs_3_.refs_11_, bf16[512,4096]{1,0:T(8,128)(2,1)} %project.1.q_ref.v_ref.k_ref.refs_3_.refs_11_), custom_call_target="tpu_custom_call" | custom-call | flops 6000000000 | bytes 4194304 | tf_op jit(solution)/shard_map/own/pallas_call | solution.py:439
  61.9 0.0 collective-permute-done.4.refs_9_
  61.9 0.2 collective-permute-start.8
  62.1 2.8 %collective-permute-done.6.refs_5_ = bf16[256,1024]{1,0:T(8,128)(2,1)} collective-permute-done((bf16[256,1024]{1,0:T(8,128)(2,1)}, bf16[256,1024]{1,0:T(8,128)(2,1)}, u32[]{:S(2)}, u32[]{:S(2)}) %collective-permute-start.6) | collective-permute-done | bytes 524320 | tf_op jit(solution)/shard_map/ppermute | solution.py:19
  64.9 0.0 collective-permute-done.2.refs_7_
  64.9 0.8 copy-done.8
  65.7 0.8 copy-done.9
  66.5 13.5 %first_picks.1.refs_4_ = f32[512,1024]{1,0:T(8,128)} custom-call(s32[4]{0:T(128)} %refs_0_.3, s32[1,2]{1,0:T(1,128)} %refs_1_.3, f32[16,16]{1,0:T(8,128)} %refs_2_.3, bf16[512,4096]{1,0:T(8,128)(2,1)} %project.1.q_ref.v_ref.k_ref.refs_3_.refs_11_, f32[512,1024]{1,0:T(8,128)} %own.1.refs_4_, bf16[256,1024]{1,0:T(8,128)(2,1)} %collective-permute-done.1.refs_5_, ...), custom_call_target="tpu_custom_call" | custom-call | flops 8000000000 | bytes 4194304 | tf_op jit(solution)/shard_map/first_picks/pallas_call | solution.py:509
  80.1 0.5 copy-done.10
  80.6 0.2 copy-done.6
  80.9 0.2 copy-done.2
  81.0 0.2 copy-done.7
  81.2 17.3 %last_picks.1 = (bf16[512,1024]{1,0:T(8,128)(2,1)}, f32[4,128]{1,0:T(4,128)}, f32[512,128]{1,0:T(8,128)}) custom-call(s32[4]{0:T(128)} %refs_0_.3, s32[1,2]{1,0:T(1,128)} %refs_1_.3, f32[16,16]{1,0:T(8,128)} %refs_2_.3, bf16[512,4096]{1,0:T(8,128)(2,1)} %project.1.q_ref.v_ref.k_ref.refs_3_.refs_11_, f32[512,1024]{1,0:T(8,128)} %first_picks.1.refs_4_, ...), custom_call_target="tpu_custom_call" | custom-call | flops 8000000000 | bytes 4194304 | tf_op jit(solution)/shard_map/last_picks/pallas_call | solution.py:509
  (21 shorter events, 0.0 us)
Async XLA Ops:
  0.6 21.1 %copy-start = (bf16[512,1024]{1,0:T(8,128)(2,1)S(1)}, bf16[512,1024]{1,0:T(8,128)(2,1)}, u32[]{:S(2)}) copy-start(bf16[512,1024]{1,0:T(8,128)(2,1)} %refs_12_.1) | copy-start | bytes 3145732
  1.8 17.0 %collective-permute-start.5 = (bf16[256,1024]{1,0:T(8,128)(2,1)S(1)}, bf16[256,1024]{1,0:T(8,128)(2,1)S(1)}, u32[]{:S(2)}, u32[]{:S(2)}) collective-permute-start(bf16[256,1024]{1,0:T(8,128)(2,1)S(1)} %slice.10), channel_id=1, source_target_pairs={{0,4},{1,5},{2,6},{3,7},{4,8},{5,9},{6,10},{7,11},{8,12},{9,13},{1... | collective-permute-start | bytes 1572872 | tf_op jit(solution)/shard_map/ppermute | solution.py:19
  18.8 0.8 copy-start.4
  21.7 15.0 %copy-start.1 = (bf16[512,1024]{1,0:T(8,128)(2,1)S(1)}, bf16[512,1024]{1,0:T(8,128)(2,1)}, u32[]{:S(2)}) copy-start(bf16[512,1024]{1,0:T(8,128)(2,1)} %refs_12_.1) | copy-start | bytes 3145732
  21.7 15.0 %collective-permute-start = (bf16[256,1024]{1,0:T(8,128)(2,1)S(1)}, bf16[256,1024]{1,0:T(8,128)(2,1)S(1)}, u32[]{:S(2)}, u32[]{:S(2)}) collective-permute-start(bf16[256,1024]{1,0:T(8,128)(2,1)S(1)} %get-tuple-element.12), channel_id=1, source_target_pairs={{0,4},{1,5},{2,6},{3,7},{4,8},{5,9},{6,10},{7,11},{8,12},{9,13},{1... | collective-permute-start | bytes 1572872 | tf_op jit(solution)/shard_map/ppermute | solution.py:19
  21.7 40.2 %collective-permute-start.4 = (bf16[512,1024]{1,0:T(8,128)(2,1)S(1)}, bf16[512,1024]{1,0:T(8,128)(2,1)}, u32[]{:S(2)}, u32[]{:S(2)}) collective-permute-start(bf16[512,1024]{1,0:T(8,128)(2,1)S(1)} %copy-done), channel_id=1, source_target_pairs={{0,1},{1,0},{2,3},{3,2},{4,5},{5,4},{6,7},{7,6},{8,9},{9,8},{10,11... | collective-permute-start | bytes 3145736 | tf_op jit(solution)/shard_map/ppermute | solution.py:19
  21.8 58.2 %collective-permute-start.9 = (bf16[1,1024]{1,0:T(2,128)(2,1)S(1)}, bf16[1,1024]{1,0:T(2,128)(2,1)S(1)}, u32[]{:S(2)}, u32[]{:S(2)}) collective-permute-start(bf16[1,1024]{1,0:T(2,128)(2,1)S(1)} %slice.11), channel_id=1, source_target_pairs={{0,15},{1,0},{2,1},{3,2},{4,3},{5,4},{6,5},{7,6},{8,7},{9,8},{10,9... | collective-permute-start | bytes 6152 | tf_op jit(solution)/shard_map/ppermute | solution.py:19
  36.7 17.2 %copy-start.3 = (bf16[256,1024]{1,0:T(8,128)(2,1)}, bf16[256,1024]{1,0:T(8,128)(2,1)S(1)}, u32[]{:S(2)}) copy-start(bf16[256,1024]{1,0:T(8,128)(2,1)S(1)} %collective-permute-done.refs_6_) | copy-start | bytes 1572868
  36.7 17.4 %collective-permute-start.1 = (bf16[256,1024]{1,0:T(8,128)(2,1)S(1)}, bf16[256,1024]{1,0:T(8,128)(2,1)}, u32[]{:S(2)}, u32[]{:S(2)}) collective-permute-start(bf16[256,1024]{1,0:T(8,128)(2,1)S(1)} %broadcast_select_fusion.1), channel_id=1, source_target_pairs={{0,2},{1,3},{2,0},{3,1},{4,6},{5,7},{6,4},{7,5},{8,10},{9,11},{10,... | collective-permute-start | bytes 1572872 | tf_op jit(solution)/shard_map/ppermute | solution.py:19
  49.3 15.6 %collective-permute-start.6 = (bf16[256,1024]{1,0:T(8,128)(2,1)}, bf16[256,1024]{1,0:T(8,128)(2,1)}, u32[]{:S(2)}, u32[]{:S(2)}) collective-permute-start(bf16[256,1024]{1,0:T(8,128)(2,1)} %get-tuple-element.11), channel_id=1, source_target_pairs={{0,2},{1,3},{2,0},{3,1},{4,6},{5,7},{6,4},{7,5},{8,10},{9,11},{10,... | collective-permute-start | bytes 1572872 | tf_op jit(solution)/shard_map/ppermute | solution.py:19
  50.1 29.9 %all-to-all-start = ((bf16[16,16,1024]{2,1,0:T(8,128)(2,1)}), bf16[16,16,1024]{2,1,0:T(8,128)(2,1)S(1)}, u32[]{:S(2)}, u32[]{:S(2)}) async-start(bf16[16,16,1024]{2,1,0:T(8,128)(2,1)} %bitcast), calls=%async_computation | async-start | bytes 1048576 | tf_op jit(solution)/shard_map/all_to_all | solution.py:458
  53.9 8.0 %copy-start.5 = (bf16[256,1024]{1,0:T(8,128)(2,1)S(1)}, bf16[256,1024]{1,0:T(8,128)(2,1)}, u32[]{:S(2)}) copy-start(bf16[256,1024]{1,0:T(8,128)(2,1)} %copy-done.4) | copy-start | bytes 1572868
  53.9 11.0 %collective-permute-start.3 = (bf16[256,1024]{1,0:T(8,128)(2,1)S(1)}, bf16[256,1024]{1,0:T(8,128)(2,1)S(1)}, u32[]{:S(2)}, u32[]{:S(2)}) collective-permute-start(bf16[256,1024]{1,0:T(8,128)(2,1)S(1)} %collective-permute-done.refs_6_), channel_id=1, source_target_pairs={{0,1},{1,0},{2,3},{3,2},{4,5},{5,4},{6,7},{7,6},{8,9},{9,8},{10,11... | collective-permute-start | bytes 1572872 | tf_op jit(solution)/shard_map/ppermute | solution.py:19
  54.1 10.8 %collective-permute-start.2 = (bf16[256,1024]{1,0:T(8,128)(2,1)}, bf16[256,1024]{1,0:T(8,128)(2,1)S(1)}, u32[]{:S(2)}, u32[]{:S(2)}) collective-permute-start(bf16[256,1024]{1,0:T(8,128)(2,1)} %collective-permute-done.1.refs_5_), channel_id=1, source_target_pairs={{0,1},{1,0},{2,3},{3,2},{4,5},{5,4},{6,7},{7,6},{8,9},{9,8},{10,11... | collective-permute-start | bytes 1572872 | tf_op jit(solution)/shard_map/ppermute | solution.py:19
  61.9 18.1 %collective-permute-start.8 = (bf16[256,1024]{1,0:T(8,128)(2,1)S(1)}, bf16[256,1024]{1,0:T(8,128)(2,1)S(1)}, u32[]{:S(2)}, u32[]{:S(2)}) collective-permute-start(bf16[256,1024]{1,0:T(8,128)(2,1)S(1)} %copy-done.5), channel_id=1, source_target_pairs={{0,1},{1,0},{2,3},{3,2},{4,5},{5,4},{6,7},{7,6},{8,9},{9,8},{10,11... | collective-permute-start | bytes 1572872 | tf_op jit(solution)/shard_map/ppermute | solution.py:19
  64.9 15.2 %collective-permute-start.7 = (bf16[256,1024]{1,0:T(8,128)(2,1)}, bf16[256,1024]{1,0:T(8,128)(2,1)S(1)}, u32[]{:S(2)}, u32[]{:S(2)}) collective-permute-start(bf16[256,1024]{1,0:T(8,128)(2,1)} %collective-permute-done.6.refs_5_), channel_id=1, source_target_pairs={{0,1},{1,0},{2,3},{3,2},{4,5},{5,4},{6,7},{7,6},{8,9},{9,8},{10,11... | collective-permute-start | bytes 1572872 | tf_op jit(solution)/shard_map/ppermute | solution.py:19
  64.9 0.8 copy-start.8
  65.7 0.8 copy-start.9
  80.0 0.6 copy-start.10
  80.1 0.8 copy-start.6
  80.1 1.0 copy-start.2
  80.1 1.1 %copy-start.7 = (bf16[256,1024]{1,0:T(8,128)(2,1)}, bf16[256,1024]{1,0:T(8,128)(2,1)S(1)}, u32[]{:S(2)}) copy-start(bf16[256,1024]{1,0:T(8,128)(2,1)S(1)} %collective-permute-done.7.refs_7_) | copy-start | bytes 1572868

commit v2 on v1

v2 whole, which is shorter than its diff:
```python
import functools

import jax
import jax.numpy as jnp
from jax import lax
from jax.experimental import pallas as pl
from jax.experimental.pallas import tpu as pltpu
from jax.sharding import PartitionSpec as P

BLOCKED = -1e9
LANES = 128
F32 = jnp.float32
BF16 = jnp.bfloat16
NT = (((1,), (1,)), ((), ()))


def passed_along(value, pairs):
    return lax.ppermute(value, "ctx", pairs)


def centered(values):
    center = values - jnp.mean(values, -1, keepdims=True)
    spread = jnp.mean(center * center, -1, keepdims=True)
    return center * lax.rsqrt(spread + 1e-05)


def silu_of_half(half):
    return half * jnp.tanh(half) + half


def iota(shape, dim):
    return lax.broadcasted_iota(jnp.int32, shape, dim)


def time_base(block, count, rows):
    total = count * rows
    return lax.rem(block * rows + total // 4, total)


def starts_of(times, lengths_ref):
    end = jnp.int32(0)
    start = jnp.zeros_like(times)
    for user in range(lengths_ref.shape[0]):
        length = lengths_ref[user]
        end = end + length
        start = start + jnp.where(times >= end, length, 0)
    return start


def half_bias(rel_ref, head, bucket):
    return rel_ref[head, bucket] * 0.5


def bias_chain(distance, rel_ref, head, low, first, last):
    tile = jnp.full(distance.shape, half_bias(rel_ref, head, low), F32)
    for degree in range(first, last):
        tile = jnp.where(distance >= 2**degree, half_bias(rel_ref, head, degree + 1), tile)
    return tile


def head_rows(size, width, value):
    lane = iota((1, width), 1)
    return [
        jnp.where((lane >= size * num) & (lane < size * (num + 1)), value, 0.0).astype(BF16)
        for num in range(width // size)
    ]


def requested_rows(slot_cap, cand_ref, events):
    me = lax.axis_index("ctx")
    count, wanted = cand_ref.shape
    rows = events.shape[0]
    slots = count * slot_cap
    cand = cand_ref[...]
    local = cand - me * rows
    mine = (local >= 0) & (local < rows)
    earlier = (iota((wanted, wanted), 0) < iota((wanted, wanted), 1)).astype(BF16)
    rank = jnp.dot(jnp.where(mine, 1.0, 0.0).astype(BF16), earlier, preferred_element_type=F32)
    code = jnp.where(mine, rank * rows + local.astype(F32), -1.0)
    slot_num = iota((slots, count), 0) - iota((slots, count), 1) * slot_cap
    spread = jnp.where((slot_num >= 0) & (slot_num < slot_cap), 1.0, 0.0)
    asked = jnp.dot(spread, code, preferred_element_type=F32, precision=lax.Precision.HIGHEST)
    slot = lax.rem(iota((slots, wanted), 0), slot_cap).astype(F32)
    found = asked - slot * rows
    ids = jnp.sum(jnp.where((found >= 0.0) & (found < rows), found + 1.0, 0.0), 1, keepdims=True)
    picks = (ids.astype(jnp.int32) - 1 == iota((slots, rows), 1)).astype(BF16)
    return jnp.dot(picks, events, preferred_element_type=F32).astype(BF16)


def request_kernel(slot_cap, cand_ref, events_ref, sent_ref):
    sent_ref[...] = requested_rows(slot_cap, cand_ref, events_ref[...])


def front_kernel(events_hbm, w_ref, out_ref, bottom_ref, *scratch):
    events_ref, w_buf, out_buf, in_sems, out_sems = scratch
    arrival = pltpu.make_async_copy(events_hbm, events_ref, in_sems.at[4])
    arrival.start()
    hidden = events_ref.shape[1]
    piece = hidden // 4
    order = [1, 3, 2, 0]
    columns = [pl.ds(part * hidden, hidden) for part in range(len(order))]
    arrivals = [
        pltpu.make_async_copy(w_ref.at[:, spot], w_buf.at[:, spot], in_sems.at[part])
        for part, spot in enumerate(columns)
    ]
    leaving = [
        pltpu.make_async_copy(out_buf.at[:, spot], out_ref.at[:, spot], out_sems.at[part])
        for part, spot in enumerate(columns)
    ]
    for part in order:
        arrivals[part].start()
    half = bottom_ref.shape[0]
    bottom = pltpu.make_async_copy(events_ref.at[pl.ds(half, half)], bottom_ref, out_sems.at[4])
    arrival.wait()
    bottom.start()
    normed = centered(events_ref[...].astype(F32)).astype(BF16)
    for part in order:
        arrivals[part].wait()
        for start in range(part * hidden, (part + 1) * hidden, piece):
            spot = slice(start, start + piece)
            value = jnp.dot(normed, w_buf[:, spot], preferred_element_type=F32)
            out_buf[:, spot] = silu_of_half(0.5 * value).astype(BF16)
        leaving[part].start()
    for part in order:
        leaving[part].wait()
    bottom.wait()


def own_kernel(head_size, lengths_ref, rel_ref, q_ref, v_ref, k_ref, out_ref, mask_ref):
    group = pl.program_id(0)
    rows, width = q_ref.shape
    half = rows // 2
    heads = width // head_size
    count = lax.axis_size("ctx")

    @pl.when(group == 0)
    def _():
        base = time_base(lax.axis_index("ctx"), count, rows)
        start = starts_of(base + iota((rows, LANES), 0), lengths_ref)
        for num in range(rows // LANES):
            key_time = base + num * LANES + iota((rows, LANES), 1)
            mask_ref[:, num * LANES : (num + 1) * LANES] = jnp.where(key_time >= start, 0.0, BLOCKED)

    away = iota((LANES, LANES), 0) - iota((LANES, LANES), 1)
    queries, values, keys = q_ref[...], v_ref[...], k_ref[...]
    scaled = head_rows(head_size, width, 0.5 * head_size**-0.5)
    chosen = head_rows(head_size, width, 1.0)
    parts = [([], []), ([], [])]
    for num in range(heads):
        head = group * heads + num
        tiles = [
            jnp.where(away < 0, BLOCKED, bias_chain(away, rel_ref, head, 0, 0, 7)),
            bias_chain(away + LANES, rel_ref, head, 1, 1, 8),
            jnp.where(away >= 0, half_bias(rel_ref, head, 9), half_bias(rel_ref, head, 8)),
            half_bias(rel_ref, head, 9),
        ]
        head_queries = queries * scaled[num]
        head_values = values * chosen[num]
        for part in range(2):
            seen = (part + 1) * half
            scores = lax.dot_general(
                head_queries[part * half : (part + 1) * half],
                keys[:seen],
                NT,
                preferred_element_type=F32,
            )
            lines = []
            for q_sub in range(half // LANES):
                q_tile = part * (half // LANES) + q_sub
                line = []
                for k_tile in range(seen // LANES):
                    if k_tile > q_tile:
                        line.append(jnp.zeros((LANES, LANES), BF16))
                        continue
                    part_scores = scores[
                        q_sub * LANES : (q_sub + 1) * LANES, k_tile * LANES : (k_tile + 1) * LANES
                    ]
                    mask = mask_ref[
                        q_tile * LANES : (q_tile + 1) * LANES, k_tile * LANES : (k_tile + 1) * LANES
                    ]
                    line.append(
                        silu_of_half(part_scores + tiles[q_tile - k_tile] + mask).astype(BF16)
                    )
                lines.append(jnp.concatenate(line, 1))
            parts[part][0].append(jnp.concatenate(lines, 0))
            parts[part][1].append(head_values[:seen])
    for part in range(2):
        weights = jnp.concatenate(parts[part][0], 1)
        stacked = jnp.concatenate(parts[part][1], 0)
        out_ref[part * half : (part + 1) * half] = jnp.dot(
            weights, stacked, preferred_element_type=F32
        )


def picks_kernel(head_size, *refs):
    lengths_ref, lists_ref, rel_ref, projected_ref, before_ref = refs[:5]
    far_ref, far_twin_ref, own_twin_ref, across_ref, across_twin_ref = refs[5:10]
    passed_ref, passed_twin_ref, over_ref, over_twin_ref, w_ref = refs[10:15]
    events_hbm, next_ref, w_out_ref = refs[15:18]
    layer_hbm, score_ref = refs[18:20]
    acc_ref, q_ref, earlier_ref, rows_ref, w_buf, pair_ref, mask_ref, near_ref = refs[20:28]
    sems, out_buf, gate_ref, events_ref, layer_ref, layer_sems = refs[28:]
    me = lax.axis_index("ctx")
    count = lax.axis_size("ctx")
    rows, hidden = q_ref.shape
    half = rows // 2
    picks = lists_ref.shape[1]
    head_count, _ = rel_ref.shape
    second = lax.rem(me, 2) == 1
    first = jnp.logical_not(second)
    upper = lax.rem(me, 4) >= 2
    lower = jnp.logical_not(upper)

    copies = []
    for pick in range(picks):
        away = lists_ref[0, pick]
        crossed = ((away == 1) & first) | ((away == 3) & second)
        target = rows_ref.at[pl.ds(pick * rows, rows)]
        head = rows_ref.at[pl.ds(pick * rows, half)]
        tail = rows_ref.at[pl.ds(pick * rows + half, half)]
        sources = [
            (away == 4, far_ref, target),
            ((away == 3) & first, far_twin_ref, target),
            ((away == 1) & second, own_twin_ref, target),
            ((away == 2) & upper, across_ref, head),
            ((away == 2) & lower, passed_ref, head),
            (away == 2, over_ref, tail),
            (crossed & upper, across_twin_ref, head),
            (crossed & lower, passed_twin_ref, head),
            (crossed, over_twin_ref, tail),
        ]
        for flag, source, spot in sources:

            @pl.when(flag)
            def _():
                pltpu.make_async_copy(source, spot, sems.at[pick]).start()

        copies.append(pltpu.make_async_copy(far_ref, target, sems.at[pick]))
    step = hidden // 2
    parts = 2 * hidden // step
    later = [
        (w_ref.at[:, pl.ds(2 * hidden + part * step, step)], w_buf.at[:, pl.ds(part * step, step)])
        for part in range(parts)
    ]
    later.append((projected_ref.at[:, pl.ds(hidden, hidden)], q_ref))
    later.append((before_ref, earlier_ref))
    later.append((w_out_ref, out_buf))
    later.append((projected_ref.at[:, pl.ds(0, hidden)], gate_ref))
    later.append((events_hbm, events_ref))
    later = [
        pltpu.make_async_copy(source, target, sems.at[picks + num])
        for num, (source, target) in enumerate(later)
    ]
    for copy in later[:parts]:
        copy.start()
    acc_ref[...] = jnp.zeros_like(acc_ref)
    for copy in copies:
        copy.wait()
    normed = centered(rows_ref[...].astype(F32)).astype(BF16)
    for part in range(parts):
        later[part].wait()
        if part == 0:
            for copy in later[parts:]:
                copy.start()
        columns = pl.ds(part * step, step)
        value = jnp.dot(normed, w_buf[:, columns], preferred_element_type=F32)
        pair_ref[:, columns] = silu_of_half(0.5 * value).astype(BF16)
    later[parts].wait()

    base = time_base(me, count, rows)
    first_start = starts_of(base, lengths_ref)
    gap = iota((LANES, LANES), 0) - iota((LANES, LANES), 1)
    width = 4 * head_size
    scaled = head_rows(head_size, width, 0.5 * head_size**-0.5)
    chosen = head_rows(head_size, width, 1.0)
    tiles = rows // LANES

    @pl.loop(0, picks)
    def _(pick):
        away = lists_ref[0, pick]
        block = lax.rem(me - away + count, count)
        key_base = time_base(block, count, rows)
        useful = (key_base < base) & (key_base + rows - 1 >= first_start)

        @pl.when(useful)
        def _():
            start = starts_of(base + iota((rows, LANES), 0), lengths_ref)
            for tile in range(tiles):
                key_time = key_base + tile * LANES + iota((rows, LANES), 1)
                mask_ref[:, tile * LANES : (tile + 1) * LANES] = jnp.where(
                    key_time >= start, 0.0, BLOCKED
                )
            lows, highs = {}, {}
            for diff in range(1 - tiles, tiles):
                delta = away * rows + diff * LANES
                bucket, power = jnp.int32(8), jnp.int32(0)
                for degree in range(8, rel_ref.shape[1] - 1):
                    bucket = bucket + (delta >= 2**degree).astype(jnp.int32)
                    power = power + (delta == 2**degree).astype(jnp.int32)
                highs[diff] = bucket
                lows[diff] = bucket - power
            special = 1 - tiles

            @pl.when(away == 1)
            def _():
                @pl.loop(0, head_count)
                def _(head):
                    near_ref[head] = bias_chain(gap + LANES, rel_ref, head, 1, 1, 8)

            @pl.when(away != 1)
            def _():
                @pl.loop(0, head_count)
                def _(head):
                    near_ref[head] = jnp.full(
                        gap.shape, half_bias(rel_ref, head, highs[special]), F32
                    )

            key_rows = pl.ds(pl.multiple_of(pick * rows, rows), rows)
            for group in range(hidden // width):
                columns = slice(group * width, (group + 1) * width)
                queries = q_ref[:, columns]
                values = pair_ref[key_rows, columns]
                keys = pair_ref[key_rows, hidden + group * width : hidden + (group + 1) * width]
                weights, stacked = [], []
                for num in range(width // head_size):
                    head = group * (width // head_size) + num
                    scores = lax.dot_general(
                        queries * scaled[num], keys, NT, preferred_element_type=F32
                    )
                    lines = []
                    for q_tile in range(tiles):
                        line = []
                        for k_tile in range(tiles):
                            diff = q_tile - k_tile
                            if diff == special:
                                bias = near_ref[head]
                            elif diff in (0, 2 - tiles):
                                bias = jnp.where(
                                    gap >= 0,
                                    half_bias(rel_ref, head, highs[diff]),
                                    half_bias(rel_ref, head, lows[diff]),
                                )
                            else:
                                bias = half_bias(rel_ref, head, highs[diff])
                            spot = (
                                slice(q_tile * LANES, (q_tile + 1) * LANES),
                                slice(k_tile * LANES, (k_tile + 1) * LANES),
                            )
                            line.append(
                                silu_of_half(scores[spot] + bias + mask_ref[spot]).astype(BF16)
                            )
                        lines.append(jnp.concatenate(line, 1))
                    weights.append(jnp.concatenate(lines, 0))
                    stacked.append(values * chosen[num])
                acc_ref[:, columns] += jnp.dot(
                    jnp.concatenate(weights, 1),
                    jnp.concatenate(stacked, 0),
                    preferred_element_type=F32,
                )

    later[parts + 1].wait()
    diagonal = iota((LANES, LANES), 0) == iota((LANES, LANES), 1)
    for copy in later[parts + 2 :]:
        copy.wait()
    scale = hidden**-0.5
    total = count * rows
    departures = []
    for part in range(2):
        block_rows = slice(part * half, (part + 1) * half)
        attended = acc_ref[block_rows] + earlier_ref[block_rows]
        gated = centered(attended) * gate_ref[block_rows].astype(F32)
        layer = events_ref[block_rows].astype(F32) + jnp.dot(
            gated.astype(BF16), out_buf[...], preferred_element_type=F32
        )
        layer = layer.astype(BF16)
        layer_ref[block_rows] = layer
        leaving = pltpu.make_async_copy(
            layer_ref.at[pl.ds(part * half, half)],
            layer_hbm.at[pl.ds(part * half, half)],
            layer_sems.at[part],
        )
        leaving.start()
        departures.append(leaving)
        following = pltpu.roll(events_ref[block_rows].astype(F32), half - 1, 0)
        if part == 0:
            after = events_ref[half : half + 16][:1].astype(F32)
        else:
            after = next_ref[...].astype(F32)
        following = jnp.where(iota((half, hidden), 0) == half - 1, after, following)
        inner = jnp.sum(layer.astype(F32) * following, 1, keepdims=True) * scale
        for tile in range(half // LANES):
            spot = inner[tile * LANES : (tile + 1) * LANES]
            line = jnp.sum(jnp.where(diagonal, spot, 0.0), 0, keepdims=True)
            offset = part * half + tile * LANES
            coming = base + offset + 1 + iota((1, LANES), 1)
            same = coming < total
            end = jnp.int32(0)
            for user in range(lengths_ref.shape[0]):
                end = end + lengths_ref[user]
                same = same & (coming != end)
            score_ref[offset // LANES : offset // LANES + 1] = jnp.where(same, line, 0.0)
    for leaving in departures:
        leaving.wait()


def table_kernel(slot_cap, layer_ref, flat_ref, cand_ref, table_ref):
    me = lax.axis_index("ctx")
    rows, hidden = layer_ref.shape
    wanted = cand_ref.shape[1]
    own = jnp.broadcast_to(cand_ref[pl.ds(me, 1), :].astype(F32), (wanted, wanted))
    diagonal = iota((wanted, wanted), 0) == iota((wanted, wanted), 1)
    own_column = jnp.sum(jnp.where(diagonal, own, 0.0), 1, keepdims=True)
    owner = jnp.floor(own * (1.0 / rows))
    owner_column = jnp.floor(own_column * (1.0 / rows))
    before = iota((wanted, wanted), 1) < iota((wanted, wanted), 0)
    rank = jnp.sum(jnp.where((owner == owner_column) & before, 1.0, 0.0), 1, keepdims=True)
    slot = (owner_column * slot_cap + rank).astype(jnp.int32)
    hits = (slot == iota((wanted, flat_ref.shape[0]), 1)).astype(BF16)
    listed = jnp.dot(hits, flat_ref[...], preferred_element_type=F32).astype(BF16)
    scores = lax.dot_general(layer_ref[...], listed, NT, preferred_element_type=F32)
    table_ref[...] = scores * hidden**-0.5


def smem():
    return pl.BlockSpec(memory_space=pltpu.SMEM)


def vmem():
    return pl.BlockSpec(memory_space=pltpu.VMEM)


def hbm():
    return pl.BlockSpec(memory_space=pltpu.HBM)


def anywhere():
    return pl.BlockSpec(memory_space=pl.ANY)


def placed(value):
    return pltpu.with_memory_space_constraint(value, pltpu.HBM)


def params(mebibytes, *semantics):
    return pltpu.CompilerParams(
        dimension_semantics=semantics or None, vmem_limit_bytes=mebibytes * 2**20
    )


def shards(events, w_in, w_out, rel_bias, lengths, block_lists, candidates):
    rows, hidden = events.shape
    head_count = rel_bias.shape[0]
    head_size = hidden // head_count
    count = lax.axis_size("ctx")
    wanted = candidates.shape[1]
    slot_cap = 2 * wanted // count
    slots = count * slot_cap
    half = rows // 2
    width = 4 * head_size
    picks = block_lists.shape[1]

    ring = range(count)
    across_pairs = [(s, s ^ 2) for s in ring]
    over_pairs = [(s, (s + 2) % count) for s in ring]
    far_pairs = [(s, (s + 4) % count) for s in ring]
    passing_pairs = [(s, (s + 4) % count) for s in ring if s % 4 < 2]
    back_pairs = [(s, (s - 1) % count) for s in ring]
    up_pairs = [(s, s + 1) for s in ring if s % 2 == 0]
    down_pairs = [(s, s - 1) for s in ring if s % 2 == 1]
    twin_pairs = [(s, s ^ 1) for s in ring]
    upper_twins = [(s, s ^ 1) for s in ring if s % 4 >= 2]
    lower_twins = [(s, s ^ 1) for s in ring if s % 4 < 2]

    next_first = passed_along(events[:1], back_pairs)
    own_twin = passed_along(events, up_pairs)
    across = passed_along(events[:half], across_pairs)
    far = passed_along(events, far_pairs)

    projected, bottom = pl.pallas_call(
        front_kernel,
        out_shape=(pltpu.HBM((rows, 4 * hidden), BF16), pltpu.HBM((half, hidden), BF16)),
        in_specs=[hbm(), hbm()],
        out_specs=(hbm(), hbm()),
        scratch_shapes=[
            pltpu.VMEM((rows, hidden), BF16),
            pltpu.VMEM((hidden, 4 * hidden), BF16),
            pltpu.VMEM((rows, 4 * hidden), BF16),
            pltpu.SemaphoreType.DMA((5,)),
            pltpu.SemaphoreType.DMA((5,)),
        ],
        compiler_params=params(30),
        cost_estimate=pl.CostEstimate(flops=8 * 10**9, bytes_accessed=2**23, transcendentals=0),
        name="front",
    )(placed(events), placed(w_in))

    across, projected = lax.optimization_barrier((across, projected))
    passed = passed_along(across, passing_pairs)
    over = passed_along(bottom, over_pairs)
    groups = hidden // width

    def columns(which):
        return pl.BlockSpec((rows, width), lambda i: (0, which * groups + i))

    attended = pl.pallas_call(
        functools.partial(own_kernel, head_size),
        grid=(groups,),
        out_shape=pltpu.HBM((rows, hidden), F32),
        in_specs=[smem(), smem(), columns(1), columns(2), columns(3)],
        out_specs=pl.BlockSpec((rows, width), lambda i: (0, i)),
        scratch_shapes=[pltpu.VMEM((rows, rows), F32)],
        compiler_params=params(16, "arbitrary"),
        cost_estimate=pl.CostEstimate(flops=6 * 10**9, bytes_accessed=2**22, transcendentals=0),
        name="own",
    )(lengths, rel_bias, *[placed(projected)] * 3)

    across, far, whole, _ = lax.optimization_barrier((across, far, events, attended))
    fetched = pl.pallas_call(
        functools.partial(request_kernel, slot_cap),
        out_shape=jax.ShapeDtypeStruct((slots, hidden), BF16),
        in_specs=[vmem(), vmem()],
        out_specs=vmem(),
        compiler_params=params(10),
        cost_estimate=pl.CostEstimate(flops=10**9, bytes_accessed=2**21, transcendentals=0),
        name="request",
    )(candidates, whole)
    over, passed, _ = lax.optimization_barrier((over, passed, fetched))
    across_twin = passed_along(across, upper_twins)
    over_twin = passed_along(over, twin_pairs)
    far_twin = passed_along(far, down_pairs)
    passed_twin = passed_along(passed, lower_twins)
    arrived = lax.all_to_all(
        fetched.reshape(count, slot_cap, hidden), "ctx", split_axis=0, concat_axis=0, tiled=True
    ).reshape(slots, hidden)

    parts = 4
    operands = [placed(projected), placed(attended), far, far_twin, own_twin, across]
    operands += [across_twin, passed, passed_twin, over, over_twin, placed(w_in), placed(events)]
    layer_output, next_score = pl.pallas_call(
        functools.partial(picks_kernel, head_size),
        out_shape=(
            pltpu.HBM((rows, hidden), BF16),
            jax.ShapeDtypeStruct((rows // LANES, LANES), F32),
        ),
        in_specs=[smem()] * 3 + [hbm()] * 2 + [anywhere()] * 9 + [hbm()] * 2 + [vmem(), hbm()],
        out_specs=(hbm(), vmem()),
        scratch_shapes=[
            pltpu.VMEM((rows, hidden), F32),
            pltpu.VMEM((rows, hidden), BF16),
            pltpu.VMEM((rows, hidden), F32),
            pltpu.VMEM((picks * rows, hidden), BF16),
            pltpu.VMEM((hidden, 2 * hidden), BF16),
            pltpu.VMEM((picks * rows, 2 * hidden), BF16),
            pltpu.VMEM((rows, rows), F32),
            pltpu.VMEM((head_count, LANES, LANES), F32),
            pltpu.SemaphoreType.DMA((picks + parts + 5,)),
            pltpu.VMEM((hidden, hidden), BF16),
            pltpu.VMEM((rows, hidden), BF16),
            pltpu.VMEM((rows, hidden), BF16),
            pltpu.VMEM((rows, hidden), BF16),
            pltpu.SemaphoreType.DMA((2,)),
        ],
        compiler_params=params(50),
        cost_estimate=pl.CostEstimate(
            flops=20 * 10**9, bytes_accessed=2**23, transcendentals=0
        ),
        name="picks",
    )(lengths, block_lists, rel_bias, *operands, next_first, placed(w_out))
    table = pl.pallas_call(
        functools.partial(table_kernel, slot_cap),
        out_shape=jax.ShapeDtypeStruct((rows, wanted), F32),
        in_specs=[vmem()] * 3,
        out_specs=vmem(),
        compiler_params=params(10),
        cost_estimate=pl.CostEstimate(flops=10**9, bytes_accessed=2**21, transcendentals=0),
        name="table",
    )(layer_output, arrived, candidates)
    return (layer_output, next_score.reshape(rows), table)


def solution(mesh):
    in_specs = (
        P(("groups", "ctx"), None),
        P(),
        P(),
        P(),
        P("groups"),
        P(("groups", "ctx"), None),
        P("groups", None),
    )
    out_specs = (P(("groups", "ctx"), None), P(("groups", "ctx")), P(("groups", "ctx"), None))
    return jax.shard_map(shards, mesh=mesh, in_specs=in_specs, out_specs=out_specs, check_vma=False)
```

time: 99.2 us -> 76.2 us (0.77)
  waiting for transfers between devices: 23.8 us -> 5.37 us
  starting transfers between devices: 14.5 us -> 25.2 us
  Pallas kernels: 52.6 us -> 42 us
  local copies, waits for them, and re-layouts: 4.67 us -> 2.36 us
  other arithmetic: 2.14 us -> 0 us
    ppermute x10, waiting for transfers between devices: 23.8 us -> 5.37 us  [passed_along(): return lax.ppermute(value, 'ctx', pairs)]
    ppermute x10, starting transfers between devices: 10.8 us -> 21.6 us  [passed_along(): return lax.ppermute(value, 'ctx', pairs)]
    pallas_call x3, Pallas kernels: 42.1 us -> 32.8 us  [the longest x1 22.8 us: shards(): pl.pallas_call(functools.partial(picks_kernel, head_size), out_shape=(plt...]
    unnamed x22 -> x12, local copies, waits for them, and re-layouts: 3.5 us -> 1.24 us
    select_n x2 -> x0, other arithmetic: 2.14 us -> none  [shards(): jnp.where(lower, halves[i], far[i])]
    pallas_call x1, Pallas kernels: 3.05 us -> 1.81 us  [shards(): pl.pallas_call(functools.partial(request_kernel, slot_cap), out_shape=jax...]
  transfers between devices with their start and end apart: 11 -> 11, of which waited for: 3 -> 3; matrix products, arithmetic and copies ran while one was open for 0% -> 1% of each run, Pallas kernels for 36% -> 54%
where the time goes in v2:
time: 76.2 us; the launch traced here: 75.7 us
  Pallas kernels  42 us (55%)
  starting transfers between devices  25.2 us (33%)
  waiting for transfers between devices  5.37 us (7%)
  local copies, waits for them, and re-layouts  2.36 us (3%)
  between operations  0.8 us (1%)
    pallas_call x1, Pallas kernels, shards(): pl.pallas_call(functools.partial(picks_kernel, head_size), out_shape=(plt...  22.8 us
    ppermute x10, starting transfers between devices, passed_along(): return lax.ppermute(value, 'ctx', pairs)  21.6 us
    pallas_call x1, Pallas kernels, shards(): pl.pallas_call(front_kernel, out_shape=(pltpu.HBM((rows, 4 * hidden), BF1...  8.58 us
    pallas_call x1, Pallas kernels, shards(): pl.pallas_call(functools.partial(own_kernel, head_size), grid=(groups,),...  7.4 us
    ppermute x10, waiting for transfers between devices, passed_along(): return lax.ppermute(value, 'ctx', pairs)  5.37 us
    all_to_all x1, starting transfers between devices, shards(): lax.all_to_all(fetched.reshape(count, slot_cap, hidden), 'ctx', split_axi...  3.57 us
    pallas_call x1, Pallas kernels, shards(): pl.pallas_call(functools.partial(request_kernel, slot_cap), out_shape=jax...  1.81 us
  transfers between devices with their start and end apart: 11, of which 3 were waited for; matrix products, arithmetic and copies ran while one was open for 1% of the time, Pallas kernels for 54%

profile of v2, /device:TPU:0, one launch (start us, length us, event | category | flops | bytes accessed | tf_op | source)
XLA Modules:
  0.0 75.7 jit_solution(18112144190208373846)
XLA Ops:
  0.6 3.4 %collective-permute-start.3 = (bf16[512,1024]{1,0:T(8,128)(2,1)}, bf16[512,1024]{1,0:T(8,128)(2,1)}, u32[]{:S(2)}, u32[]{:S(2)}) collective-permute-start(bf16[512,1024]{1,0:T(8,128)(2,1)} %refs_15_.1), channel_id=1, source_target_pairs={{0,1},{2,3},{4,5},{6,7},{8,9},{10,11},{12,13},{14,15},{16,17},{18,... | collective-permute-start | bytes 3145736 | tf_op jit(solution)/shard_map/ppermute | solution.py:18
  4.1 2.4 %collective-permute-start.1 = (bf16[512,1024]{1,0:T(8,128)(2,1)}, bf16[512,1024]{1,0:T(8,128)(2,1)}, u32[]{:S(2)}, u32[]{:S(2)}) collective-permute-start(bf16[512,1024]{1,0:T(8,128)(2,1)} %refs_15_.1), channel_id=1, source_target_pairs={{0,4},{1,5},{2,6},{3,7},{4,8},{5,9},{6,10},{7,11},{8,12},{9,13},{1... | collective-permute-start | bytes 3145736 | tf_op jit(solution)/shard_map/ppermute | solution.py:18
  6.5 1.1 %slice.6 = bf16[256,1024]{1,0:T(8,128)(2,1)S(1)} slice(bf16[512,1024]{1,0:T(8,128)(2,1)} %refs_15_.1), slice={[0:256], [0:1024]} | slice | bytes 1048576 | tf_op jit(solution)/shard_map/slice | solution.py:476
  7.6 0.0 copy-start.1
  7.6 0.0 copy-start.3
  7.6 1.6 %collective-permute-start = (bf16[256,1024]{1,0:T(8,128)(2,1)S(1)}, bf16[256,1024]{1,0:T(8,128)(2,1)S(1)}, u32[]{:S(2)}, u32[]{:S(2)}) collective-permute-start(bf16[256,1024]{1,0:T(8,128)(2,1)S(1)} %slice.6), channel_id=1, source_target_pairs={{0,2},{1,3},{2,0},{3,1},{4,6},{5,7},{6,4},{7,5},{8,10},{9,11},{10,... | collective-permute-start | bytes 1572872 | tf_op jit(solution)/shard_map/ppermute | solution.py:18
  9.2 8.6 %front.1 = (bf16[512,4096]{1,0:T(8,128)(2,1)}, bf16[256,1024]{1,0:T(8,128)(2,1)}) custom-call(bf16[512,1024]{1,0:T(8,128)(2,1)} %refs_15_.1, bf16[1024,4096]{1,0:T(8,128)(2,1)} %refs_14_.1), custom_call_target="tpu_custom_call" | custom-call | flops 8000000000 | bytes 8388608 | tf_op jit(solution)/shard_map/front/pallas_call | solution.py:479
  17.8 0.6 collective-permute-start.5
  18.3 2.4 %collective-permute-done.refs_8_ = bf16[256,1024]{1,0:T(8,128)(2,1)S(1)} collective-permute-done((bf16[256,1024]{1,0:T(8,128)(2,1)S(1)}, bf16[256,1024]{1,0:T(8,128)(2,1)S(1)}, u32[]{:S(2)}, u32[]{:S(2)}) %collective-permute-start) | collective-permute-done | bytes 524320 | tf_op jit(solution)/shard_map/ppermute | solution.py:18
  20.7 3.6 %collective-permute-start.6 = (bf16[256,1024]{1,0:T(8,128)(2,1)S(1)}, bf16[256,1024]{1,0:T(8,128)(2,1)S(1)}, u32[]{:S(2)}, u32[]{:S(2)}) collective-permute-start(bf16[256,1024]{1,0:T(8,128)(2,1)S(1)} %collective-permute-done.refs_8_), channel_id=1, source_target_pairs={{0,4},{1,5},{4,8},{5,9},{8,12},{9,13},{12,0},{13,1},{16,20},{17,21... | collective-permute-start | bytes 1572872 | tf_op jit(solution)/shard_map/ppermute | solution.py:18
  24.4 7.4 %own.1.refs_4_ = f32[512,1024]{1,0:T(8,128)} custom-call(s32[4]{0:T(128)S(1)} %copy-done.3, f32[16,16]{1,0:T(8,128)S(1)} %copy-done.1, bf16[512,4096]{1,0:T(8,128)(2,1)} %get-tuple-element.15.q_ref.v_ref.k_ref.refs_3_, bf16[512,4096]{1,0:T(8,128)(2,1)} %get-tuple-element.15.q_ref.v_ref.k_ref.refs_3_, ...), custom_call_target="tpu_custom_call" | custom-call | flops 6000000000 | bytes 4194304 | tf_op jit(solution)/shard_map/own/pallas_call | solution.py:504
  31.8 1.1 %collective-permute-done.1.refs_5_ = bf16[512,1024]{1,0:T(8,128)(2,1)} collective-permute-done((bf16[512,1024]{1,0:T(8,128)(2,1)}, bf16[512,1024]{1,0:T(8,128)(2,1)}, u32[]{:S(2)}, u32[]{:S(2)}) %collective-permute-start.1) | collective-permute-done | bytes 1048608 | tf_op jit(solution)/shard_map/ppermute | solution.py:18
  32.9 1.3 %collective-permute-start.2 = (bf16[512,1024]{1,0:T(8,128)(2,1)}, bf16[512,1024]{1,0:T(8,128)(2,1)}, u32[]{:S(2)}, u32[]{:S(2)}) collective-permute-start(bf16[512,1024]{1,0:T(8,128)(2,1)} %collective-permute-done.1.refs_5_), channel_id=1, source_target_pairs={{1,0},{3,2},{5,4},{7,6},{9,8},{11,10},{13,12},{15,14},{17,16},{19,... | collective-permute-start | bytes 3145736 | tf_op jit(solution)/shard_map/ppermute | solution.py:18
  34.2 4.8 %collective-permute-start.9 = (bf16[1,1024]{1,0:T(2,128)(2,1)S(1)}, bf16[1,1024]{1,0:T(2,128)(2,1)S(1)}, u32[]{:S(2)}, u32[]{:S(2)}) collective-permute-start(bf16[1,1024]{1,0:T(2,128)(2,1)S(1)} %slice.7), channel_id=1, source_target_pairs={{0,15},{1,0},{2,1},{3,2},{4,3},{5,4},{6,5},{7,6},{8,7},{9,8},{10,9... | collective-permute-start | bytes 6152 | tf_op jit(solution)/shard_map/ppermute | solution.py:18
  39.0 1.8 %request.1 = bf16[256,1024]{1,0:T(8,128)(2,1)} custom-call(s32[16,128]{1,0:T(8,128)S(1)} %copy-done.2, bf16[512,1024]{1,0:T(8,128)(2,1)S(1)} %copy-done), custom_call_target="tpu_custom_call" | custom-call | flops 1000000000 | bytes 2097152 | tf_op jit(solution)/shard_map/request/pallas_call | solution.py:517
  40.8 1.8 %collective-permute-done.5.refs_12_ = bf16[256,1024]{1,0:T(8,128)(2,1)S(1)} collective-permute-done((bf16[256,1024]{1,0:T(8,128)(2,1)}, bf16[256,1024]{1,0:T(8,128)(2,1)S(1)}, u32[]{:S(2)}, u32[]{:S(2)}) %collective-permute-start.5) | collective-permute-done | bytes 524320 | tf_op jit(solution)/shard_map/ppermute | solution.py:18
  42.6 0.0 collective-permute-done.6.refs_10_
  42.6 1.9 %collective-permute-start.7 = (bf16[256,1024]{1,0:T(8,128)(2,1)S(1)}, bf16[256,1024]{1,0:T(8,128)(2,1)S(1)}, u32[]{:S(2)}, u32[]{:S(2)}) collective-permute-start(bf16[256,1024]{1,0:T(8,128)(2,1)S(1)} %collective-permute-done.6.refs_10_), channel_id=1, source_target_pairs={{0,1},{1,0},{4,5},{5,4},{8,9},{9,8},{12,13},{13,12},{16,17},{17,16... | collective-permute-start | bytes 1572872 | tf_op jit(solution)/shard_map/ppermute | solution.py:18
  44.6 0.6 collective-permute-start.8
  45.1 0.0 collective-permute-done.9.refs_16_
  45.1 1.5 %collective-permute-start.4 = (bf16[256,1024]{1,0:T(8,128)(2,1)S(1)}, bf16[256,1024]{1,0:T(8,128)(2,1)}, u32[]{:S(2)}, u32[]{:S(2)}) collective-permute-start(bf16[256,1024]{1,0:T(8,128)(2,1)S(1)} %collective-permute-done.refs_8_), channel_id=1, source_target_pairs={{2,3},{3,2},{6,7},{7,6},{10,11},{11,10},{14,15},{15,14},{18,19},{1... | collective-permute-start | bytes 1572872 | tf_op jit(solution)/shard_map/ppermute | solution.py:18
  46.6 3.6 %all-to-all-start = ((bf16[16,16,1024]{2,1,0:T(8,128)(2,1)}), bf16[16,16,1024]{2,1,0:T(8,128)(2,1)S(1)}, u32[]{:S(2)}, u32[]{:S(2)}) async-start(bf16[16,16,1024]{2,1,0:T(8,128)(2,1)} %bitcast.1), calls=%async_computation | async-start | bytes 1048576 | tf_op jit(solution)/shard_map/all_to_all | solution.py:531
  50.2 0.0 collective-permute-done.3.refs_7_
  50.2 0.0 collective-permute-done.7.refs_11_
  50.2 0.0 collective-permute-done.8.refs_13_
  50.2 0.0 collective-permute-done.4.refs_9_
  50.2 0.0 collective-permute-done.2.refs_6_
  50.2 22.8 %picks.1 = (bf16[512,1024]{1,0:T(8,128)(2,1)}, f32[4,128]{1,0:T(4,128)}) custom-call(s32[4]{0:T(128)S(1)} %copy-done.3, s32[1,2]{1,0:T(1,128)S(1)} %copy-done.4, f32[16,16]{1,0:T(8,128)S(1)} %copy-done.1, bf16[512,4096]{1,0:T(8,128)(2,1)} %get-tuple-element.15.q_ref.v_ref.k_ref.refs_3_, f32[512,1024]{1,0:T(8,128)} %own.1.refs_4_, ...), custom_call_target="tpu_custom_call" | custom-call | flops 20000000000 | bytes 8388608 | tf_op jit(solution)/shard_map/picks/pallas_call | solution.py:538
  73.0 0.0 all-to-all-done
  73.0 0.0 copy-start.5
  73.0 1.2 %copy-done.5 = bf16[512,1024]{1,0:T(8,128)(2,1)S(1)} copy-done((bf16[512,1024]{1,0:T(8,128)(2,1)S(1)}, bf16[512,1024]{1,0:T(8,128)(2,1)}, u32[]{:S(2)}) %copy-start.5) | copy-done | bytes 1048600
  74.3 1.5 %table.1 = f32[512,128]{1,0:T(8,128)} custom-call(bf16[512,1024]{1,0:T(8,128)(2,1)S(1)} %copy-done.5, bf16[256,1024]{1,0:T(8,128)(2,1)S(1)} %bitcast.3, s32[16,128]{1,0:T(8,128)S(1)} %copy-done.2), custom_call_target="tpu_custom_call" | custom-call | flops 1000000000 | bytes 2097152 | tf_op jit(solution)/shard_map/table/pallas_call | solution.py:568
  (9 shorter events, 0.0 us)
Async XLA Ops:
  0.6 49.5 %collective-permute-start.3 = (bf16[512,1024]{1,0:T(8,128)(2,1)}, bf16[512,1024]{1,0:T(8,128)(2,1)}, u32[]{:S(2)}, u32[]{:S(2)}) collective-permute-start(bf16[512,1024]{1,0:T(8,128)(2,1)} %refs_15_.1), channel_id=1, source_target_pairs={{0,1},{2,3},{4,5},{6,7},{8,9},{10,11},{12,13},{14,15},{16,17},{18,... | collective-permute-start | bytes 3145736 | tf_op jit(solution)/shard_map/ppermute | solution.py:18
  4.1 28.8 %collective-permute-start.1 = (bf16[512,1024]{1,0:T(8,128)(2,1)}, bf16[512,1024]{1,0:T(8,128)(2,1)}, u32[]{:S(2)}, u32[]{:S(2)}) collective-permute-start(bf16[512,1024]{1,0:T(8,128)(2,1)} %refs_15_.1), channel_id=1, source_target_pairs={{0,4},{1,5},{2,6},{3,7},{4,8},{5,9},{6,10},{7,11},{8,12},{9,13},{1... | collective-permute-start | bytes 3145736 | tf_op jit(solution)/shard_map/ppermute | solution.py:18
  7.6 16.8 %copy-start.1 = (f32[16,16]{1,0:T(8,128)S(1)}, f32[16,16]{1,0:T(8,128)}, u32[]{:S(2)}) copy-start(f32[16,16]{1,0:T(8,128)} %refs_2_.1) | copy-start | bytes 3076
  7.6 16.8 %copy-start.3 = (s32[4]{0:T(128)S(1)}, s32[4]{0:T(128)}, u32[]{:S(2)}) copy-start(s32[4]{0:T(128)} %refs_0_.1) | copy-start | bytes 52
  7.6 13.1 %collective-permute-start = (bf16[256,1024]{1,0:T(8,128)(2,1)S(1)}, bf16[256,1024]{1,0:T(8,128)(2,1)S(1)}, u32[]{:S(2)}, u32[]{:S(2)}) collective-permute-start(bf16[256,1024]{1,0:T(8,128)(2,1)S(1)} %slice.6), channel_id=1, source_target_pairs={{0,2},{1,3},{2,0},{3,1},{4,6},{5,7},{6,4},{7,5},{8,10},{9,11},{10,... | collective-permute-start | bytes 1572872 | tf_op jit(solution)/shard_map/ppermute | solution.py:18
  17.8 24.9 %collective-permute-start.5 = (bf16[256,1024]{1,0:T(8,128)(2,1)}, bf16[256,1024]{1,0:T(8,128)(2,1)S(1)}, u32[]{:S(2)}, u32[]{:S(2)}) collective-permute-start(bf16[256,1024]{1,0:T(8,128)(2,1)} %get-tuple-element.19), channel_id=1, source_target_pairs={{0,2},{1,3},{2,4},{3,5},{4,6},{5,7},{6,8},{7,9},{8,10},{9,11},{10,... | collective-permute-start | bytes 1572872 | tf_op jit(solution)/shard_map/ppermute | solution.py:18
  20.7 13.4 %copy-start = (bf16[512,1024]{1,0:T(8,128)(2,1)S(1)}, bf16[512,1024]{1,0:T(8,128)(2,1)}, u32[]{:S(2)}) copy-start(bf16[512,1024]{1,0:T(8,128)(2,1)} %refs_15_.1) | copy-start | bytes 3145732
  20.7 18.3 %copy-start.2 = (s32[16,128]{1,0:T(8,128)S(1)}, s32[16,128]{1,0:T(8,128)}, u32[]{:S(2)}) copy-start(s32[16,128]{1,0:T(8,128)} %cand_ref.3) | copy-start | bytes 24580
  20.7 21.9 %collective-permute-start.6 = (bf16[256,1024]{1,0:T(8,128)(2,1)S(1)}, bf16[256,1024]{1,0:T(8,128)(2,1)S(1)}, u32[]{:S(2)}, u32[]{:S(2)}) collective-permute-start(bf16[256,1024]{1,0:T(8,128)(2,1)S(1)} %collective-permute-done.refs_8_), channel_id=1, source_target_pairs={{0,4},{1,5},{4,8},{5,9},{8,12},{9,13},{12,0},{13,1},{16,20},{17,21... | collective-permute-start | bytes 1572872 | tf_op jit(solution)/shard_map/ppermute | solution.py:18
  31.8 18.5 %copy-start.4 = (s32[1,2]{1,0:T(1,128)S(1)}, s32[1,2]{1,0:T(1,128)}, u32[]{:S(2)}) copy-start(s32[1,2]{1,0:T(1,128)} %refs_1_.1) | copy-start | bytes 28
  32.9 17.3 %collective-permute-start.2 = (bf16[512,1024]{1,0:T(8,128)(2,1)}, bf16[512,1024]{1,0:T(8,128)(2,1)}, u32[]{:S(2)}, u32[]{:S(2)}) collective-permute-start(bf16[512,1024]{1,0:T(8,128)(2,1)} %collective-permute-done.1.refs_5_), channel_id=1, source_target_pairs={{1,0},{3,2},{5,4},{7,6},{9,8},{11,10},{13,12},{15,14},{17,16},{19,... | collective-permute-start | bytes 3145736 | tf_op jit(solution)/shard_map/ppermute | solution.py:18
  34.2 10.9 %collective-permute-start.9 = (bf16[1,1024]{1,0:T(2,128)(2,1)S(1)}, bf16[1,1024]{1,0:T(2,128)(2,1)S(1)}, u32[]{:S(2)}, u32[]{:S(2)}) collective-permute-start(bf16[1,1024]{1,0:T(2,128)(2,1)S(1)} %slice.7), channel_id=1, source_target_pairs={{0,15},{1,0},{2,1},{3,2},{4,3},{5,4},{6,5},{7,6},{8,7},{9,8},{10,9... | collective-permute-start | bytes 6152 | tf_op jit(solution)/shard_map/ppermute | solution.py:18
  42.6 7.5 %collective-permute-start.7 = (bf16[256,1024]{1,0:T(8,128)(2,1)S(1)}, bf16[256,1024]{1,0:T(8,128)(2,1)S(1)}, u32[]{:S(2)}, u32[]{:S(2)}) collective-permute-start(bf16[256,1024]{1,0:T(8,128)(2,1)S(1)} %collective-permute-done.6.refs_10_), channel_id=1, source_target_pairs={{0,1},{1,0},{4,5},{5,4},{8,9},{9,8},{12,13},{13,12},{16,17},{17,16... | collective-permute-start | bytes 1572872 | tf_op jit(solution)/shard_map/ppermute | solution.py:18
  44.6 5.6 %collective-permute-start.8 = (bf16[256,1024]{1,0:T(8,128)(2,1)S(1)}, bf16[256,1024]{1,0:T(8,128)(2,1)S(1)}, u32[]{:S(2)}, u32[]{:S(2)}) collective-permute-start(bf16[256,1024]{1,0:T(8,128)(2,1)S(1)} %collective-permute-done.5.refs_12_), channel_id=1, source_target_pairs={{0,1},{1,0},{2,3},{3,2},{4,5},{5,4},{6,7},{7,6},{8,9},{9,8},{10,11... | collective-permute-start | bytes 1572872 | tf_op jit(solution)/shard_map/ppermute | solution.py:18
  45.1 5.1 %collective-permute-start.4 = (bf16[256,1024]{1,0:T(8,128)(2,1)S(1)}, bf16[256,1024]{1,0:T(8,128)(2,1)}, u32[]{:S(2)}, u32[]{:S(2)}) collective-permute-start(bf16[256,1024]{1,0:T(8,128)(2,1)S(1)} %collective-permute-done.refs_8_), channel_id=1, source_target_pairs={{2,3},{3,2},{6,7},{7,6},{10,11},{11,10},{14,15},{15,14},{18,19},{1... | collective-permute-start | bytes 1572872 | tf_op jit(solution)/shard_map/ppermute | solution.py:18
  46.6 26.4 %all-to-all-start = ((bf16[16,16,1024]{2,1,0:T(8,128)(2,1)}), bf16[16,16,1024]{2,1,0:T(8,128)(2,1)S(1)}, u32[]{:S(2)}, u32[]{:S(2)}) async-start(bf16[16,16,1024]{2,1,0:T(8,128)(2,1)} %bitcast.1), calls=%async_computation | async-start | bytes 1048576 | tf_op jit(solution)/shard_map/all_to_all | solution.py:531
  73.0 1.2 %copy-start.5 = (bf16[512,1024]{1,0:T(8,128)(2,1)S(1)}, bf16[512,1024]{1,0:T(8,128)(2,1)}, u32[]{:S(2)}) copy-start(bf16[512,1024]{1,0:T(8,128)(2,1)} %get-tuple-element.11.layer_ref) | copy-start | bytes 3145732

commit v3 on v2

--- a/solution.py
+++ b/solution.py
@@ -87,109 +87,110 @@
     return jnp.dot(picks, events, preferred_element_type=F32).astype(BF16)
 
 
-def request_kernel(slot_cap, cand_ref, events_ref, sent_ref):
-    sent_ref[...] = requested_rows(slot_cap, cand_ref, events_ref[...])
-
-
-def front_kernel(events_hbm, w_ref, out_ref, bottom_ref, *scratch):
-    events_ref, w_buf, out_buf, in_sems, out_sems = scratch
-    arrival = pltpu.make_async_copy(events_hbm, events_ref, in_sems.at[4])
+def own_attention(head_size, lengths_ref, rel_ref, pair_buf, mask_ref, out_ref, finish):
+    rows, hidden = out_ref.shape
+    half = rows // 2
+    width = 4 * head_size
+    heads = width // head_size
+    base = time_base(lax.axis_index("ctx"), lax.axis_size("ctx"), rows)
+    start = starts_of(base + iota((rows, LANES), 0), lengths_ref)
+    for num in range(rows // LANES):
+        key_time = base + num * LANES + iota((rows, LANES), 1)
+        mask_ref[:, num * LANES : (num + 1) * LANES] = jnp.where(key_time >= start, 0.0, BLOCKED)
+    away = iota((LANES, LANES), 0) - iota((LANES, LANES), 1)
+    scaled = head_rows(head_size, width, 0.5 * head_size**-0.5)
+    chosen = head_rows(head_size, width, 1.0)
+    for group in range(hidden // width):
+        spot = slice(group * width, (group + 1) * width)
+        queries, values, keys = [
+            pair_buf[:, which * hidden + spot.start : which * hidden + spot.stop]
+            for which in (1, 2, 3)
+        ]
+        parts = [([], []), ([], [])]
+        for num in range(heads):
+            head = group * heads + num
+            tiles = [
+                jnp.where(away < 0, BLOCKED, bias_chain(away, rel_ref, head, 0, 0, 7)),
+                bias_chain(away + LANES, rel_ref, head, 1, 1, 8),
+                jnp.where(away >= 0, half_bias(rel_ref, head, 9), half_bias(rel_ref, head, 8)),
+                half_bias(rel_ref, head, 9),
+            ]
+            head_queries = queries * scaled[num]
+            head_values = values * chosen[num]
+            for part in range(2):
+                seen = (part + 1) * half
+                scores = lax.dot_general(
+                    head_queries[part * half : (part + 1) * half],
+                    keys[:seen],
+                    NT,
+                    preferred_element_type=F32,
+                )
+                lines = []
+                for q_sub in range(half // LANES):
+                    q_tile = part * (half // LANES) + q_sub
+                    line = []
+                    for k_tile in range(seen // LANES):
+                        if k_tile > q_tile:
+                            line.append(jnp.zeros((LANES, LANES), BF16))
+                            continue
+                        k_spot = slice(k_tile * LANES, (k_tile + 1) * LANES)
+                        part_scores = scores[q_sub * LANES : (q_sub + 1) * LANES, k_spot]
+                        mask = mask_ref[q_tile * LANES : (q_tile + 1) * LANES, k_spot]
+                        line.append(
+                            silu_of_half(part_scores + tiles[q_tile - k_tile] + mask).astype(BF16)
+                        )
+                    lines.append(jnp.concatenate(line, 1))
+                parts[part][0].append(jnp.concatenate(lines, 0))
+                parts[part][1].append(head_values[:seen])
+        for part in range(2):
+            out_ref[part * half : (part + 1) * half, spot] = jnp.dot(
+                jnp.concatenate(parts[part][0], 1),
+                jnp.concatenate(parts[part][1], 0),
+                preferred_element_type=F32,
+            )
+    finish()
+
+
+def front_kernel(head_size, slot_cap, *refs):
+    lengths_ref, rel_ref, cand_ref, events_hbm, w_ref = refs[:5]
+    sent_ref, kept_hbm, attended_hbm, bottom_hbm = refs[5:9]
+    events_ref, w_buf, pair_buf, out_buf, mask_ref, in_sems, out_sems = refs[9:]
+    rows, hidden = events_ref.shape
+    half = rows // 2
+    step = hidden // 2
+    arrival = pltpu.make_async_copy(events_hbm, events_ref, in_sems.at[8])
     arrival.start()
-    hidden = events_ref.shape[1]
-    piece = hidden // 4
-    order = [1, 3, 2, 0]
-    columns = [pl.ds(part * hidden, hidden) for part in range(len(order))]
+    order = [2, 3, 6, 7, 4, 5, 0, 1]
     arrivals = [
-        pltpu.make_async_copy(w_ref.at[:, spot], w_buf.at[:, spot], in_sems.at[part])
-        for part, spot in enumerate(columns)
+        pltpu.make_async_copy(
+            w_ref.at[:, pl.ds(part * step, step)],
+            w_buf.at[:, pl.ds(part * step, step)],
+            in_sems.at[part],
+        )
+        for part in order
     ]
-    leaving = [
-        pltpu.make_async_copy(out_buf.at[:, spot], out_ref.at[:, spot], out_sems.at[part])
-        for part, spot in enumerate(columns)
-    ]
-    for part in order:
-        arrivals[part].start()
-    half = bottom_ref.shape[0]
-    bottom = pltpu.make_async_copy(events_ref.at[pl.ds(half, half)], bottom_ref, out_sems.at[4])
+    bottom = pltpu.make_async_copy(events_ref.at[pl.ds(half, half)], bottom_hbm, out_sems.at[0])
+    kept = pltpu.make_async_copy(pair_buf.at[:, pl.ds(0, 2 * hidden)], kept_hbm, out_sems.at[1])
+    attended = pltpu.make_async_copy(out_buf, attended_hbm, out_sems.at[2])
+    ahead = 2
+    for copy in arrivals[:ahead]:
+        copy.start()
     arrival.wait()
     bottom.start()
     normed = centered(events_ref[...].astype(F32)).astype(BF16)
-    for part in order:
-        arrivals[part].wait()
-        for start in range(part * hidden, (part + 1) * hidden, piece):
-            spot = slice(start, start + piece)
+    for num, part in enumerate(order):
+        arrivals[num].wait()
+        if num + ahead < len(arrivals):
+            arrivals[num + ahead].start()
+        for start in range(part * step, (part + 1) * step, step // 2):
+            spot = slice(start, start + step // 2)
             value = jnp.dot(normed, w_buf[:, spot], preferred_element_type=F32)
-            out_buf[:, spot] = silu_of_half(0.5 * value).astype(BF16)
-        leaving[part].start()
-    for part in order:
-        leaving[part].wait()
-    bottom.wait()
-
-
-def own_kernel(head_size, lengths_ref, rel_ref, q_ref, v_ref, k_ref, out_ref, mask_ref):
-    group = pl.program_id(0)
-    rows, width = q_ref.shape
-    half = rows // 2
-    heads = width // head_size
-    count = lax.axis_size("ctx")
-
-    @pl.when(group == 0)
-    def _():
-        base = time_base(lax.axis_index("ctx"), count, rows)
-        start = starts_of(base + iota((rows, LANES), 0), lengths_ref)
-        for num in range(rows // LANES):
-            key_time = base + num * LANES + iota((rows, LANES), 1)
-            mask_ref[:, num * LANES : (num + 1) * LANES] = jnp.where(key_time >= start, 0.0, BLOCKED)
-
-    away = iota((LANES, LANES), 0) - iota((LANES, LANES), 1)
-    queries, values, keys = q_ref[...], v_ref[...], k_ref[...]
-    scaled = head_rows(head_size, width, 0.5 * head_size**-0.5)
-    chosen = head_rows(head_size, width, 1.0)
-    parts = [([], []), ([], [])]
-    for num in range(heads):
-        head = group * heads + num
-        tiles = [
-            jnp.where(away < 0, BLOCKED, bias_chain(away, rel_ref, head, 0, 0, 7)),
-            bias_chain(away + LANES, rel_ref, head, 1, 1, 8),
-            jnp.where(away >= 0, half_bias(rel_ref, head, 9), half_bias(rel_ref, head, 8)),
-            half_bias(rel_ref, head, 9),
-        ]
-        head_queries = queries * scaled[num]
-        head_values = values * chosen[num]
-        for part in range(2):
-            seen = (part + 1) * half
-            scores = lax.dot_general(
-                head_queries[part * half : (part + 1) * half],
-                keys[:seen],
-                NT,
-                preferred_element_type=F32,
-            )
-            lines = []
-            for q_sub in range(half // LANES):
-                q_tile = part * (half // LANES) + q_sub
-                line = []
-                for k_tile in range(seen // LANES):
-                    if k_tile > q_tile:
-                        line.append(jnp.zeros((LANES, LANES), BF16))
-                        continue
-                    part_scores = scores[
-                        q_sub * LANES : (q_sub + 1) * LANES, k_tile * LANES : (k_tile + 1) * LANES
-                    ]
-                    mask = mask_ref[
-                        q_tile * LANES : (q_tile + 1) * LANES, k_tile * LANES : (k_tile + 1) * LANES
-                    ]
-                    line.append(
-                        silu_of_half(part_scores + tiles[q_tile - k_tile] + mask).astype(BF16)
-                    )
-                lines.append(jnp.concatenate(line, 1))
-            parts[part][0].append(jnp.concatenate(lines, 0))
-            parts[part][1].append(head_values[:seen])
-    for part in range(2):
-        weights = jnp.concatenate(parts[part][0], 1)
-        stacked = jnp.concatenate(parts[part][1], 0)
-        out_ref[part * half : (part + 1) * half] = jnp.dot(
-            weights, stacked, preferred_element_type=F32
-        )
+            pair_buf[:, spot] = silu_of_half(0.5 * value).astype(BF16)
+    kept.start()
+    sent_ref[...] = requested_rows(slot_cap, cand_ref, events_ref[...])
+    own_attention(head_size, lengths_ref, rel_ref, pair_buf, mask_ref, out_buf, attended.start)
+    for copy in (bottom, kept, attended):
+        copy.wait()
 
 
 def picks_kernel(head_size, *refs):
@@ -251,20 +252,23 @@
         pltpu.make_async_copy(source, target, sems.at[picks + num])
         for num, (source, target) in enumerate(later)
     ]
-    for copy in later[:parts]:
-        copy.start()
     acc_ref[...] = jnp.zeros_like(acc_ref)
     for copy in copies:
         copy.wait()
+    later[0].start()
+    later[1].start()
     normed = centered(rows_ref[...].astype(F32)).astype(BF16)
     for part in range(parts):
         later[part].wait()
-        if part == 0:
-            for copy in later[parts:]:
+        if part + 2 < parts:
+            later[part + 2].start()
+        else:
+            for copy in later[parts + 3 * (part + 2 - parts) :][:3]:
                 copy.start()
-        columns = pl.ds(part * step, step)
-        value = jnp.dot(normed, w_buf[:, columns], preferred_element_type=F32)
-        pair_ref[:, columns] = silu_of_half(0.5 * value).astype(BF16)
+        for piece in range(2):
+            columns = pl.ds(part * step + piece * (step // 2), step // 2)
+            value = jnp.dot(normed, w_buf[:, columns], preferred_element_type=F32)
+            pair_ref[:, columns] = silu_of_half(0.5 * value).astype(BF16)
     later[parts].wait()
 
     base = time_base(me, count, rows)
@@ -403,7 +407,9 @@
         leaving.wait()
 
 
-def table_kernel(slot_cap, layer_ref, flat_ref, cand_ref, table_ref):
+def table_kernel(slot_cap, layer_hbm, flat_ref, cand_ref, table_ref, layer_ref, sem):
+    arrival = pltpu.make_async_copy(layer_hbm, layer_ref, sem)
+    arrival.start()
     me = lax.axis_index("ctx")
     rows, hidden = layer_ref.shape
     wanted = cand_ref.shape[1]
@@ -417,6 +423,7 @@
     slot = (owner_column * slot_cap + rank).astype(jnp.int32)
     hits = (slot == iota((wanted, flat_ref.shape[0]), 1)).astype(BF16)
     listed = jnp.dot(hits, flat_ref[...], preferred_element_type=F32).astype(BF16)
+    arrival.wait()
     scores = lax.dot_general(layer_ref[...], listed, NT, preferred_element_type=F32)
     table_ref[...] = scores * hidden**-0.5
 
@@ -476,65 +483,48 @@
     across = passed_along(events[:half], across_pairs)
     far = passed_along(events, far_pairs)
 
-    projected, bottom = pl.pallas_call(
-        front_kernel,
-        out_shape=(pltpu.HBM((rows, 4 * hidden), BF16), pltpu.HBM((half, hidden), BF16)),
-        in_specs=[hbm(), hbm()],
-        out_specs=(hbm(), hbm()),
+    fetched, kept, attended, bottom = pl.pallas_call(
+        functools.partial(front_kernel, head_size, slot_cap),
+        out_shape=(
+            jax.ShapeDtypeStruct((slots, hidden), BF16),
+            pltpu.HBM((rows, 2 * hidden), BF16),
+            pltpu.HBM((rows, hidden), F32),
+            pltpu.HBM((half, hidden), BF16),
+        ),
+        in_specs=[smem(), smem(), vmem(), hbm(), hbm()],
+        out_specs=(vmem(), hbm(), hbm(), hbm()),
         scratch_shapes=[
             pltpu.VMEM((rows, hidden), BF16),
             pltpu.VMEM((hidden, 4 * hidden), BF16),
             pltpu.VMEM((rows, 4 * hidden), BF16),
-            pltpu.SemaphoreType.DMA((5,)),
-            pltpu.SemaphoreType.DMA((5,)),
+            pltpu.VMEM((rows, hidden), F32),
+            pltpu.VMEM((rows, rows), F32),
+            pltpu.SemaphoreType.DMA((9,)),
+            pltpu.SemaphoreType.DMA((3,)),
         ],
-        compiler_params=params(30),
-        cost_estimate=pl.CostEstimate(flops=8 * 10**9, bytes_accessed=2**23, transcendentals=0),
+        compiler_params=params(48),
+        cost_estimate=pl.CostEstimate(
+            flops=14 * 10**9, bytes_accessed=2**23, transcendentals=0
+        ),
         name="front",
-    )(placed(events), placed(w_in))
-
-    across, projected = lax.optimization_barrier((across, projected))
+    )(placed(lengths), placed(rel_bias), placed(candidates), placed(events), placed(w_in))
+
+    across, kept = lax.optimization_barrier((across, kept))
+    far, attended = lax.optimization_barrier((far, attended))
     passed = passed_along(across, passing_pairs)
     over = passed_along(bottom, over_pairs)
-    groups = hidden // width
-
-    def columns(which):
-        return pl.BlockSpec((rows, width), lambda i: (0, which * groups + i))
-
-    attended = pl.pallas_call(
-        functools.partial(own_kernel, head_size),
-        grid=(groups,),
-        out_shape=pltpu.HBM((rows, hidden), F32),
-        in_specs=[smem(), smem(), columns(1), columns(2), columns(3)],
-        out_specs=pl.BlockSpec((rows, width), lambda i: (0, i)),
-        scratch_shapes=[pltpu.VMEM((rows, rows), F32)],
-        compiler_params=params(16, "arbitrary"),
-        cost_estimate=pl.CostEstimate(flops=6 * 10**9, bytes_accessed=2**22, transcendentals=0),
-        name="own",
-    )(lengths, rel_bias, *[placed(projected)] * 3)
-
-    across, far, whole, _ = lax.optimization_barrier((across, far, events, attended))
-    fetched = pl.pallas_call(
-        functools.partial(request_kernel, slot_cap),
-        out_shape=jax.ShapeDtypeStruct((slots, hidden), BF16),
-        in_specs=[vmem(), vmem()],
-        out_specs=vmem(),
-        compiler_params=params(10),
-        cost_estimate=pl.CostEstimate(flops=10**9, bytes_accessed=2**21, transcendentals=0),
-        name="request",
-    )(candidates, whole)
-    over, passed, _ = lax.optimization_barrier((over, passed, fetched))
+    over_done, passed_done, fetched = lax.optimization_barrier((over, passed, fetched))
     across_twin = passed_along(across, upper_twins)
-    over_twin = passed_along(over, twin_pairs)
+    over_twin = passed_along(over_done, twin_pairs)
     far_twin = passed_along(far, down_pairs)
-    passed_twin = passed_along(passed, lower_twins)
+    passed_twin = passed_along(passed_done, lower_twins)
     arrived = lax.all_to_all(
         fetched.reshape(count, slot_cap, hidden), "ctx", split_axis=0, concat_axis=0, tiled=True
     ).reshape(slots, hidden)
 
     parts = 4
-    operands = [placed(projected), placed(attended), far, far_twin, own_twin, across]
-    operands += [across_twin, passed, passed_twin, over, over_twin, placed(w_in), placed(events)]
+    operands = [placed(kept), placed(attended), far, far_twin, own_twin, across]
+    operands += [across_twin, passed_done, passed_twin, over_done, over_twin, placed(w_in), placed(events)]
     layer_output, next_score = pl.pallas_call(
         functools.partial(picks_kernel, head_size),
         out_shape=(
@@ -568,12 +558,13 @@
     table = pl.pallas_call(
         functools.partial(table_kernel, slot_cap),
         out_shape=jax.ShapeDtypeStruct((rows, wanted), F32),
-        in_specs=[vmem()] * 3,
+        in_specs=[hbm(), vmem(), vmem()],
         out_specs=vmem(),
+        scratch_shapes=[pltpu.VMEM((rows, hidden), BF16), pltpu.SemaphoreType.DMA],
         compiler_params=params(10),
         cost_estimate=pl.CostEstimate(flops=10**9, bytes_accessed=2**21, transcendentals=0),
         name="table",
-    )(layer_output, arrived, candidates)
+    )(placed(layer_output), arrived, candidates)
     return (layer_output, next_score.reshape(rows), table)
 
 

time: 76.2 us -> 74.3 us (0.975)
  starting transfers between devices: 25.2 us -> 23.9 us
    pallas_call x3 -> x1, Pallas kernels: 17.8 us -> 16 us  [shards(): pl.pallas_call(functools.partial(front_kernel, head_size, slot_cap), out_...]
    ppermute x10, starting transfers between devices: 21.6 us -> 20.3 us  [passed_along(): return lax.ppermute(value, 'ctx', pairs)]
    unnamed x12 -> x8, local copies, waits for them, and re-layouts: 1.24 us -> 0.03 us
    pallas_call x1, Pallas kernels: 1.47 us -> 2.57 us  [shards(): pl.pallas_call(functools.partial(table_kernel, slot_cap), out_shape=jax.S...]
  transfers between devices with their start and end apart: 11 -> 11, of which waited for: 3 -> 2; matrix products, arithmetic and copies ran while one was open for 1% -> 2% of each run, Pallas kernels for 54% -> 53%
where the time goes in v3:
time: 74.3 us; the launch traced here: 73.8 us
  Pallas kernels  41.4 us (56%)
  starting transfers between devices  23.9 us (32%)
  waiting for transfers between devices  5.65 us (8%)
  local copies, waits for them, and re-layouts  1.86 us (3%)
  between operations  0.98 us (1%)
    pallas_call x1, Pallas kernels, shards(): pl.pallas_call(functools.partial(picks_kernel, head_size), out_shape=(plt...  22.8 us
    ppermute x10, starting transfers between devices, passed_along(): return lax.ppermute(value, 'ctx', pairs)  20.3 us
    pallas_call x1, Pallas kernels, shards(): pl.pallas_call(functools.partial(front_kernel, head_size, slot_cap), out_...  16 us
    ppermute x10, waiting for transfers between devices, passed_along(): return lax.ppermute(value, 'ctx', pairs)  5.65 us
    all_to_all x1, starting transfers between devices, shards(): lax.all_to_all(fetched.reshape(count, slot_cap, hidden), 'ctx', split_axi...  3.57 us
    pallas_call x1, Pallas kernels, shards(): pl.pallas_call(functools.partial(table_kernel, slot_cap), out_shape=jax.S...  2.57 us
  transfers between devices with their start and end apart: 11, of which 2 were waited for; matrix products, arithmetic and copies ran while one was open for 2% of the time, Pallas kernels for 53%

profile of v3, /device:TPU:0, one launch (start us, length us, event | category | flops | bytes accessed | tf_op | source)
XLA Modules:
  0.0 73.8 jit_solution(1186036610334092141)
XLA Ops:
  0.6 3.1 %collective-permute-start.1 = (bf16[512,1024]{1,0:T(8,128)(2,1)}, bf16[512,1024]{1,0:T(8,128)(2,1)}, u32[]{:S(2)}, u32[]{:S(2)}) collective-permute-start(bf16[512,1024]{1,0:T(8,128)(2,1)} %refs_15_.1), channel_id=1, source_target_pairs={{0,4},{1,5},{2,6},{3,7},{4,8},{5,9},{6,10},{7,11},{8,12},{9,13},{1... | collective-permute-start | bytes 3145736 | tf_op jit(solution)/shard_map/ppermute | solution.py:18
  3.7 1.1 %slice.6 = bf16[256,1024]{1,0:T(8,128)(2,1)S(1)} slice(bf16[512,1024]{1,0:T(8,128)(2,1)} %refs_15_.1), slice={[0:256], [0:1024]} | slice | bytes 1048576 | tf_op jit(solution)/shard_map/slice | solution.py:483
  4.8 0.0 copy-start
  4.8 0.0 copy-start.2
  4.8 0.0 copy-start.3
  4.9 1.6 %collective-permute-start = (bf16[256,1024]{1,0:T(8,128)(2,1)S(1)}, bf16[256,1024]{1,0:T(8,128)(2,1)S(1)}, u32[]{:S(2)}, u32[]{:S(2)}) collective-permute-start(bf16[256,1024]{1,0:T(8,128)(2,1)S(1)} %slice.6), channel_id=1, source_target_pairs={{0,2},{1,3},{2,0},{3,1},{4,6},{5,7},{6,4},{7,5},{8,10},{9,11},{10,... | collective-permute-start | bytes 1572872 | tf_op jit(solution)/shard_map/ppermute | solution.py:18
  6.4 16.0 %front.1 = (bf16[256,1024]{1,0:T(8,128)(2,1)}, bf16[512,2048]{1,0:T(8,128)(2,1)}, f32[512,1024]{1,0:T(8,128)}, bf16[256,1024]{1,0:T(8,128)(2,1)}) custom-call(s32[4]{0:T(128)} %refs_0_.3, f32[16,16]{1,0:T(8,128)} %refs_2_.3, s32[16,128]{1,0:T(8,128)} %cand_ref.1, bf16[512,1024]{1,0:T(8,128)(2,1)} %refs_15_.1, bf16[1024,4096]{1,0:T(8,128)(2,1)} %refs_14_.1), custom_call_target="tpu_custom_call" | custom-call | flops 14000000000 | bytes 8388608 | tf_op jit(solution)/shard_map/front/pallas_call | solution.py:486
  22.5 0.6 collective-permute-start.5
  23.1 0.0 collective-permute-done.refs_8_
  23.1 3.5 %collective-permute-start.6 = (bf16[256,1024]{1,0:T(8,128)(2,1)S(1)}, bf16[256,1024]{1,0:T(8,128)(2,1)S(1)}, u32[]{:S(2)}, u32[]{:S(2)}) collective-permute-start(bf16[256,1024]{1,0:T(8,128)(2,1)S(1)} %collective-permute-done.refs_8_), channel_id=1, source_target_pairs={{0,4},{1,5},{4,8},{5,9},{8,12},{9,13},{12,0},{13,1},{16,20},{17,21... | collective-permute-start | bytes 1572872 | tf_op jit(solution)/shard_map/ppermute | solution.py:18
  26.5 2.3 %collective-permute-start.3 = (bf16[512,1024]{1,0:T(8,128)(2,1)}, bf16[512,1024]{1,0:T(8,128)(2,1)}, u32[]{:S(2)}, u32[]{:S(2)}) collective-permute-start(bf16[512,1024]{1,0:T(8,128)(2,1)} %refs_15_.1), channel_id=1, source_target_pairs={{0,1},{2,3},{4,5},{6,7},{8,9},{10,11},{12,13},{14,15},{16,17},{18,... | collective-permute-start | bytes 3145736 | tf_op jit(solution)/shard_map/ppermute | solution.py:18
  28.8 1.1 %collective-permute-done.1.refs_5_ = bf16[512,1024]{1,0:T(8,128)(2,1)} collective-permute-done((bf16[512,1024]{1,0:T(8,128)(2,1)}, bf16[512,1024]{1,0:T(8,128)(2,1)}, u32[]{:S(2)}, u32[]{:S(2)}) %collective-permute-start.1) | collective-permute-done | bytes 1048608 | tf_op jit(solution)/shard_map/ppermute | solution.py:18
  29.9 1.3 %collective-permute-start.2 = (bf16[512,1024]{1,0:T(8,128)(2,1)}, bf16[512,1024]{1,0:T(8,128)(2,1)}, u32[]{:S(2)}, u32[]{:S(2)}) collective-permute-start(bf16[512,1024]{1,0:T(8,128)(2,1)} %collective-permute-done.1.refs_5_), channel_id=1, source_target_pairs={{1,0},{3,2},{5,4},{7,6},{9,8},{11,10},{13,12},{15,14},{17,16},{19,... | collective-permute-start | bytes 3145736 | tf_op jit(solution)/shard_map/ppermute | solution.py:18
  31.2 0.7 slice.7
  31.9 4.9 %collective-permute-start.9 = (bf16[1,1024]{1,0:T(2,128)(2,1)S(1)}, bf16[1,1024]{1,0:T(2,128)(2,1)S(1)}, u32[]{:S(2)}, u32[]{:S(2)}) collective-permute-start(bf16[1,1024]{1,0:T(2,128)(2,1)S(1)} %slice.7), channel_id=1, source_target_pairs={{0,15},{1,0},{2,1},{3,2},{4,3},{5,4},{6,5},{7,6},{8,7},{9,8},{10,9... | collective-permute-start | bytes 6152 | tf_op jit(solution)/shard_map/ppermute | solution.py:18
  36.8 4.5 %collective-permute-done.5.refs_12_ = bf16[256,1024]{1,0:T(8,128)(2,1)S(1)} collective-permute-done((bf16[256,1024]{1,0:T(8,128)(2,1)}, bf16[256,1024]{1,0:T(8,128)(2,1)S(1)}, u32[]{:S(2)}, u32[]{:S(2)}) %collective-permute-start.5) | collective-permute-done | bytes 524320 | tf_op jit(solution)/shard_map/ppermute | solution.py:18
  41.3 0.7 collective-permute-start.4
  42.0 0.0 collective-permute-done.6.refs_10_
  42.0 1.9 %collective-permute-start.7 = (bf16[256,1024]{1,0:T(8,128)(2,1)S(1)}, bf16[256,1024]{1,0:T(8,128)(2,1)S(1)}, u32[]{:S(2)}, u32[]{:S(2)}) collective-permute-start(bf16[256,1024]{1,0:T(8,128)(2,1)S(1)} %collective-permute-done.6.refs_10_), channel_id=1, source_target_pairs={{0,1},{1,0},{4,5},{5,4},{8,9},{9,8},{12,13},{13,12},{16,17},{17,16... | collective-permute-start | bytes 1572872 | tf_op jit(solution)/shard_map/ppermute | solution.py:18
  44.0 0.0 collective-permute-done.9.refs_16_
  44.0 0.6 collective-permute-start.8
  44.5 3.6 %all-to-all-start = ((bf16[16,16,1024]{2,1,0:T(8,128)(2,1)}), bf16[16,16,1024]{2,1,0:T(8,128)(2,1)S(1)}, u32[]{:S(2)}, u32[]{:S(2)}) async-start(bf16[16,16,1024]{2,1,0:T(8,128)(2,1)} %bitcast.1), calls=%async_computation | async-start | bytes 1048576 | tf_op jit(solution)/shard_map/all_to_all | solution.py:521
  48.1 0.0 copy-start.1
  48.1 0.0 collective-permute-done.3.refs_7_
  48.1 0.0 collective-permute-done.4.refs_9_
  48.2 0.0 collective-permute-done.7.refs_11_
  48.2 0.0 collective-permute-done.8.refs_13_
  48.2 0.0 collective-permute-done.2.refs_6_
  48.2 0.0 copy-done
  48.2 22.8 %picks.1 = (bf16[512,1024]{1,0:T(8,128)(2,1)}, f32[4,128]{1,0:T(4,128)}) custom-call(s32[4]{0:T(128)S(1)} %copy-done.2, s32[1,2]{1,0:T(1,128)S(1)} %copy-done.3, f32[16,16]{1,0:T(8,128)S(1)} %copy-done, bf16[512,2048]{1,0:T(8,128)(2,1)} %get-tuple-element.17.refs_3_, f32[512,1024]{1,0:T(8,128)} %get-tuple-element.19.refs_4_, ...), custom_call_target="tpu_custom_call" | custom-call | flops 20000000000 | bytes 8388608 | tf_op jit(solution)/shard_map/picks/pallas_call | solution.py:528
  71.0 0.0 all-to-all-done
  71.0 2.6 %table.1 = f32[512,128]{1,0:T(8,128)} custom-call(bf16[512,1024]{1,0:T(8,128)(2,1)} %get-tuple-element.13.layer_hbm, bf16[256,1024]{1,0:T(8,128)(2,1)S(1)} %bitcast.3, s32[16,128]{1,0:T(8,128)S(1)} %copy-done.1), custom_call_target="tpu_custom_call" | custom-call | flops 1000000000 | bytes 2097152 | tf_op jit(solution)/shard_map/table/pallas_call | solution.py:558
  (3 shorter events, 0.0 us)
Async XLA Ops:
  0.6 29.3 %collective-permute-start.1 = (bf16[512,1024]{1,0:T(8,128)(2,1)}, bf16[512,1024]{1,0:T(8,128)(2,1)}, u32[]{:S(2)}, u32[]{:S(2)}) collective-permute-start(bf16[512,1024]{1,0:T(8,128)(2,1)} %refs_15_.1), channel_id=1, source_target_pairs={{0,4},{1,5},{2,6},{3,7},{4,8},{5,9},{6,10},{7,11},{8,12},{9,13},{1... | collective-permute-start | bytes 3145736 | tf_op jit(solution)/shard_map/ppermute | solution.py:18
  4.8 43.4 %copy-start = (f32[16,16]{1,0:T(8,128)S(1)}, f32[16,16]{1,0:T(8,128)}, u32[]{:S(2)}) copy-start(f32[16,16]{1,0:T(8,128)} %refs_2_.3) | copy-start | bytes 3076
  4.8 43.4 %copy-start.2 = (s32[4]{0:T(128)S(1)}, s32[4]{0:T(128)}, u32[]{:S(2)}) copy-start(s32[4]{0:T(128)} %refs_0_.3) | copy-start | bytes 52
  4.8 43.4 %copy-start.3 = (s32[1,2]{1,0:T(1,128)S(1)}, s32[1,2]{1,0:T(1,128)}, u32[]{:S(2)}) copy-start(s32[1,2]{1,0:T(1,128)} %refs_1_.3) | copy-start | bytes 28
  4.9 18.2 %collective-permute-start = (bf16[256,1024]{1,0:T(8,128)(2,1)S(1)}, bf16[256,1024]{1,0:T(8,128)(2,1)S(1)}, u32[]{:S(2)}, u32[]{:S(2)}) collective-permute-start(bf16[256,1024]{1,0:T(8,128)(2,1)S(1)} %slice.6), channel_id=1, source_target_pairs={{0,2},{1,3},{2,0},{3,1},{4,6},{5,7},{6,4},{7,5},{8,10},{9,11},{10,... | collective-permute-start | bytes 1572872 | tf_op jit(solution)/shard_map/ppermute | solution.py:18
  22.5 18.8 %collective-permute-start.5 = (bf16[256,1024]{1,0:T(8,128)(2,1)}, bf16[256,1024]{1,0:T(8,128)(2,1)S(1)}, u32[]{:S(2)}, u32[]{:S(2)}) collective-permute-start(bf16[256,1024]{1,0:T(8,128)(2,1)} %get-tuple-element.22), channel_id=1, source_target_pairs={{0,2},{1,3},{2,4},{3,5},{4,6},{5,7},{6,8},{7,9},{8,10},{9,11},{10,... | collective-permute-start | bytes 1572872 | tf_op jit(solution)/shard_map/ppermute | solution.py:18
  23.1 19.0 %collective-permute-start.6 = (bf16[256,1024]{1,0:T(8,128)(2,1)S(1)}, bf16[256,1024]{1,0:T(8,128)(2,1)S(1)}, u32[]{:S(2)}, u32[]{:S(2)}) collective-permute-start(bf16[256,1024]{1,0:T(8,128)(2,1)S(1)} %collective-permute-done.refs_8_), channel_id=1, source_target_pairs={{0,4},{1,5},{4,8},{5,9},{8,12},{9,13},{12,0},{13,1},{16,20},{17,21... | collective-permute-start | bytes 1572872 | tf_op jit(solution)/shard_map/ppermute | solution.py:18
  26.5 21.6 %collective-permute-start.3 = (bf16[512,1024]{1,0:T(8,128)(2,1)}, bf16[512,1024]{1,0:T(8,128)(2,1)}, u32[]{:S(2)}, u32[]{:S(2)}) collective-permute-start(bf16[512,1024]{1,0:T(8,128)(2,1)} %refs_15_.1), channel_id=1, source_target_pairs={{0,1},{2,3},{4,5},{6,7},{8,9},{10,11},{12,13},{14,15},{16,17},{18,... | collective-permute-start | bytes 3145736 | tf_op jit(solution)/shard_map/ppermute | solution.py:18
  29.9 18.3 %collective-permute-start.2 = (bf16[512,1024]{1,0:T(8,128)(2,1)}, bf16[512,1024]{1,0:T(8,128)(2,1)}, u32[]{:S(2)}, u32[]{:S(2)}) collective-permute-start(bf16[512,1024]{1,0:T(8,128)(2,1)} %collective-permute-done.1.refs_5_), channel_id=1, source_target_pairs={{1,0},{3,2},{5,4},{7,6},{9,8},{11,10},{13,12},{15,14},{17,16},{19,... | collective-permute-start | bytes 3145736 | tf_op jit(solution)/shard_map/ppermute | solution.py:18
  31.9 12.0 %collective-permute-start.9 = (bf16[1,1024]{1,0:T(2,128)(2,1)S(1)}, bf16[1,1024]{1,0:T(2,128)(2,1)S(1)}, u32[]{:S(2)}, u32[]{:S(2)}) collective-permute-start(bf16[1,1024]{1,0:T(2,128)(2,1)S(1)} %slice.7), channel_id=1, source_target_pairs={{0,15},{1,0},{2,1},{3,2},{4,3},{5,4},{6,5},{7,6},{8,7},{9,8},{10,9... | collective-permute-start | bytes 6152 | tf_op jit(solution)/shard_map/ppermute | solution.py:18
  41.3 6.8 %collective-permute-start.4 = (bf16[256,1024]{1,0:T(8,128)(2,1)S(1)}, bf16[256,1024]{1,0:T(8,128)(2,1)S(1)}, u32[]{:S(2)}, u32[]{:S(2)}) collective-permute-start(bf16[256,1024]{1,0:T(8,128)(2,1)S(1)} %collective-permute-done.refs_8_), channel_id=1, source_target_pairs={{2,3},{3,2},{6,7},{7,6},{10,11},{11,10},{14,15},{15,14},{18,19},{1... | collective-permute-start | bytes 1572872 | tf_op jit(solution)/shard_map/ppermute | solution.py:18
  42.0 6.1 %collective-permute-start.7 = (bf16[256,1024]{1,0:T(8,128)(2,1)S(1)}, bf16[256,1024]{1,0:T(8,128)(2,1)S(1)}, u32[]{:S(2)}, u32[]{:S(2)}) collective-permute-start(bf16[256,1024]{1,0:T(8,128)(2,1)S(1)} %collective-permute-done.6.refs_10_), channel_id=1, source_target_pairs={{0,1},{1,0},{4,5},{5,4},{8,9},{9,8},{12,13},{13,12},{16,17},{17,16... | collective-permute-start | bytes 1572872 | tf_op jit(solution)/shard_map/ppermute | solution.py:18
  44.0 4.2 %collective-permute-start.8 = (bf16[256,1024]{1,0:T(8,128)(2,1)S(1)}, bf16[256,1024]{1,0:T(8,128)(2,1)}, u32[]{:S(2)}, u32[]{:S(2)}) collective-permute-start(bf16[256,1024]{1,0:T(8,128)(2,1)S(1)} %collective-permute-done.5.refs_12_), channel_id=1, source_target_pairs={{0,1},{1,0},{2,3},{3,2},{4,5},{5,4},{6,7},{7,6},{8,9},{9,8},{10,11... | collective-permute-start | bytes 1572872 | tf_op jit(solution)/shard_map/ppermute | solution.py:18
  44.5 26.5 %all-to-all-start = ((bf16[16,16,1024]{2,1,0:T(8,128)(2,1)}), bf16[16,16,1024]{2,1,0:T(8,128)(2,1)S(1)}, u32[]{:S(2)}, u32[]{:S(2)}) async-start(bf16[16,16,1024]{2,1,0:T(8,128)(2,1)} %bitcast.1), calls=%async_computation | async-start | bytes 1048576 | tf_op jit(solution)/shard_map/all_to_all | solution.py:521
  48.1 22.9 %copy-start.1 = (s32[16,128]{1,0:T(8,128)S(1)}, s32[16,128]{1,0:T(8,128)}, u32[]{:S(2)}) copy-start(s32[16,128]{1,0:T(8,128)} %cand_ref.1) | copy-start | bytes 24580

commit v4 on v3

--- a/solution.py
+++ b/solution.py
@@ -85,6 +85,22 @@
     ids = jnp.sum(jnp.where((found >= 0.0) & (found < rows), found + 1.0, 0.0), 1, keepdims=True)
     picks = (ids.astype(jnp.int32) - 1 == iota((slots, rows), 1)).astype(BF16)
     return jnp.dot(picks, events, preferred_element_type=F32).astype(BF16)
+
+
+def slot_hits(slot_cap, rows, cand_ref):
+    me = lax.axis_index("ctx")
+    count = cand_ref.shape[0]
+    wanted = cand_ref.shape[1]
+    own = jnp.broadcast_to(cand_ref[pl.ds(me, 1), :].astype(F32), (wanted, wanted))
+    diagonal = iota((wanted, wanted), 0) == iota((wanted, wanted), 1)
+    own_column = jnp.sum(jnp.where(diagonal, own, 0.0), 1, keepdims=True)
+    owner = jnp.floor(own * (1.0 / rows))
+    owner_column = jnp.floor(own_column * (1.0 / rows))
+    before = iota((wanted, wanted), 1) < iota((wanted, wanted), 0)
+    rank = jnp.sum(jnp.where((owner == owner_column) & before, 1.0, 0.0), 1, keepdims=True)
+    slot = (owner_column * slot_cap + rank).astype(jnp.int32)
+    hits = (slot == iota((wanted, count * slot_cap), 1)).astype(BF16)
+    return hits
 
 
 def own_attention(head_size, lengths_ref, rel_ref, pair_buf, mask_ref, out_ref, finish):
@@ -153,8 +169,8 @@
 
 def front_kernel(head_size, slot_cap, *refs):
     lengths_ref, rel_ref, cand_ref, events_hbm, w_ref = refs[:5]
-    sent_ref, kept_hbm, attended_hbm, bottom_hbm = refs[5:9]
-    events_ref, w_buf, pair_buf, out_buf, mask_ref, in_sems, out_sems = refs[9:]
+    sent_ref, hits_ref, kept_hbm, attended_hbm, bottom_hbm = refs[5:10]
+    events_ref, w_buf, pair_buf, out_buf, mask_ref, in_sems, out_sems = refs[10:]
     rows, hidden = events_ref.shape
     half = rows // 2
     step = hidden // 2
@@ -182,12 +198,12 @@
         arrivals[num].wait()
         if num + ahead < len(arrivals):
             arrivals[num + ahead].start()
-        for start in range(part * step, (part + 1) * step, step // 2):
-            spot = slice(start, start + step // 2)
-            value = jnp.dot(normed, w_buf[:, spot], preferred_element_type=F32)
-            pair_buf[:, spot] = silu_of_half(0.5 * value).astype(BF16)
+        spot = slice(part * step, (part + 1) * step)
+        value = jnp.dot(normed, w_buf[:, spot], preferred_element_type=F32)
+        pair_buf[:, spot] = silu_of_half(0.5 * value).astype(BF16)
     kept.start()
     sent_ref[...] = requested_rows(slot_cap, cand_ref, events_ref[...])
+    hits_ref[...] = slot_hits(slot_cap, rows, cand_ref)
     own_attention(head_size, lengths_ref, rel_ref, pair_buf, mask_ref, out_buf, attended.start)
     for copy in (bottom, kept, attended):
         copy.wait()
@@ -199,8 +215,8 @@
     passed_ref, passed_twin_ref, over_ref, over_twin_ref, w_ref = refs[10:15]
     events_hbm, next_ref, w_out_ref = refs[15:18]
     layer_hbm, score_ref = refs[18:20]
-    acc_ref, q_ref, earlier_ref, rows_ref, w_buf, pair_ref, mask_ref, near_ref = refs[20:28]
-    sems, out_buf, gate_ref, events_ref, layer_ref, layer_sems = refs[28:]
+    acc_ref, q_ref, rows_ref, w_buf, pair_ref, mask_ref, near_ref = refs[20:27]
+    sems, out_buf, gate_ref, events_ref, layer_ref, layer_sems = refs[27:]
     me = lax.axis_index("ctx")
     count = lax.axis_size("ctx")
     rows, hidden = q_ref.shape
@@ -244,7 +260,7 @@
         for part in range(parts)
     ]
     later.append((projected_ref.at[:, pl.ds(hidden, hidden)], q_ref))
-    later.append((before_ref, earlier_ref))
+    later.append((before_ref, acc_ref))
     later.append((w_out_ref, out_buf))
     later.append((projected_ref.at[:, pl.ds(0, hidden)], gate_ref))
     later.append((events_hbm, events_ref))
@@ -252,7 +268,6 @@
         pltpu.make_async_copy(source, target, sems.at[picks + num])
         for num, (source, target) in enumerate(later)
     ]
-    acc_ref[...] = jnp.zeros_like(acc_ref)
     for copy in copies:
         copy.wait()
     later[0].start()
@@ -265,11 +280,11 @@
         else:
             for copy in later[parts + 3 * (part + 2 - parts) :][:3]:
                 copy.start()
-        for piece in range(2):
-            columns = pl.ds(part * step + piece * (step // 2), step // 2)
-            value = jnp.dot(normed, w_buf[:, columns], preferred_element_type=F32)
-            pair_ref[:, columns] = silu_of_half(0.5 * value).astype(BF16)
+        columns = pl.ds(part * step, step)
+        value = jnp.dot(normed, w_buf[:, columns], preferred_element_type=F32)
+        pair_ref[:, columns] = silu_of_half(0.5 * value).astype(BF16)
     later[parts].wait()
+    later[parts + 1].wait()
 
     base = time_base(me, count, rows)
     first_start = starts_of(base, lengths_ref)
@@ -362,7 +377,6 @@
                     preferred_element_type=F32,
                 )
 
-    later[parts + 1].wait()
     diagonal = iota((LANES, LANES), 0) == iota((LANES, LANES), 1)
     for copy in later[parts + 2 :]:
         copy.wait()
@@ -371,8 +385,7 @@
     departures = []
     for part in range(2):
         block_rows = slice(part * half, (part + 1) * half)
-        attended = acc_ref[block_rows] + earlier_ref[block_rows]
-        gated = centered(attended) * gate_ref[block_rows].astype(F32)
+        gated = centered(acc_ref[block_rows]) * gate_ref[block_rows].astype(F32)
         layer = events_ref[block_rows].astype(F32) + jnp.dot(
             gated.astype(BF16), out_buf[...], preferred_element_type=F32
         )
@@ -407,25 +420,16 @@
         leaving.wait()
 
 
-def table_kernel(slot_cap, layer_hbm, flat_ref, cand_ref, table_ref, layer_ref, sem):
-    arrival = pltpu.make_async_copy(layer_hbm, layer_ref, sem)
+def table_kernel(layer_hbm, flat_hbm, hits_ref, table_ref, layer_ref, flat_ref, sems):
+    flat_arrival = pltpu.make_async_copy(flat_hbm, flat_ref, sems.at[0])
+    flat_arrival.start()
+    arrival = pltpu.make_async_copy(layer_hbm, layer_ref, sems.at[1])
     arrival.start()
-    me = lax.axis_index("ctx")
-    rows, hidden = layer_ref.shape
-    wanted = cand_ref.shape[1]
-    own = jnp.broadcast_to(cand_ref[pl.ds(me, 1), :].astype(F32), (wanted, wanted))
-    diagonal = iota((wanted, wanted), 0) == iota((wanted, wanted), 1)
-    own_column = jnp.sum(jnp.where(diagonal, own, 0.0), 1, keepdims=True)
-    owner = jnp.floor(own * (1.0 / rows))
-    owner_column = jnp.floor(own_column * (1.0 / rows))
-    before = iota((wanted, wanted), 1) < iota((wanted, wanted), 0)
-    rank = jnp.sum(jnp.where((owner == owner_column) & before, 1.0, 0.0), 1, keepdims=True)
-    slot = (owner_column * slot_cap + rank).astype(jnp.int32)
-    hits = (slot == iota((wanted, flat_ref.shape[0]), 1)).astype(BF16)
-    listed = jnp.dot(hits, flat_ref[...], preferred_element_type=F32).astype(BF16)
+    flat_arrival.wait()
+    listed = jnp.dot(hits_ref[...], flat_ref[...], preferred_element_type=F32).astype(BF16)
     arrival.wait()
     scores = lax.dot_general(layer_ref[...], listed, NT, preferred_element_type=F32)
-    table_ref[...] = scores * hidden**-0.5
+    table_ref[...] = scores * layer_ref.shape[1] ** -0.5
 
 
 def smem():
@@ -483,16 +487,17 @@
     across = passed_along(events[:half], across_pairs)
     far = passed_along(events, far_pairs)
 
-    fetched, kept, attended, bottom = pl.pallas_call(
+    fetched, hits, kept, attended, bottom = pl.pallas_call(
         functools.partial(front_kernel, head_size, slot_cap),
         out_shape=(
             jax.ShapeDtypeStruct((slots, hidden), BF16),
+            jax.ShapeDtypeStruct((wanted, slots), BF16),
             pltpu.HBM((rows, 2 * hidden), BF16),
             pltpu.HBM((rows, hidden), F32),
             pltpu.HBM((half, hidden), BF16),
         ),
         in_specs=[smem(), smem(), vmem(), hbm(), hbm()],
-        out_specs=(vmem(), hbm(), hbm(), hbm()),
+        out_specs=(vmem(), vmem(), hbm(), hbm(), hbm()),
         scratch_shapes=[
             pltpu.VMEM((rows, hidden), BF16),
             pltpu.VMEM((hidden, 4 * hidden), BF16),
@@ -536,7 +541,6 @@
         scratch_shapes=[
             pltpu.VMEM((rows, hidden), F32),
             pltpu.VMEM((rows, hidden), BF16),
-            pltpu.VMEM((rows, hidden), F32),
             pltpu.VMEM((picks * rows, hidden), BF16),
             pltpu.VMEM((hidden, 2 * hidden), BF16),
             pltpu.VMEM((picks * rows, 2 * hidden), BF16),
@@ -556,15 +560,19 @@
         name="picks",
     )(lengths, block_lists, rel_bias, *operands, next_first, placed(w_out))
     table = pl.pallas_call(
-        functools.partial(table_kernel, slot_cap),
+        table_kernel,
         out_shape=jax.ShapeDtypeStruct((rows, wanted), F32),
-        in_specs=[hbm(), vmem(), vmem()],
+        in_specs=[hbm(), anywhere(), vmem()],
         out_specs=vmem(),
-        scratch_shapes=[pltpu.VMEM((rows, hidden), BF16), pltpu.SemaphoreType.DMA],
+        scratch_shapes=[
+            pltpu.VMEM((rows, hidden), BF16),
+            pltpu.VMEM((slots, hidden), BF16),
+            pltpu.SemaphoreType.DMA((2,)),
+        ],
         compiler_params=params(10),
         cost_estimate=pl.CostEstimate(flops=10**9, bytes_accessed=2**21, transcendentals=0),
         name="table",
-    )(placed(layer_output), arrived, candidates)
+    )(placed(layer_output), arrived, hits)
     return (layer_output, next_score.reshape(rows), table)
 
 

time: 74.3 us -> 74.1 us (level)
  no operation moved by 1% of the time
where the time goes in v4:
time: 74.1 us; the launch traced here: 73.5 us
  Pallas kernels  41.2 us (56%)
  starting transfers between devices  23.9 us (32%)
  waiting for transfers between devices  5.58 us (8%)
  local copies, waits for them, and re-layouts  1.85 us (2%)
  between operations  0.96 us (1%)
    pallas_call x1, Pallas kernels, shards(): pl.pallas_call(functools.partial(picks_kernel, head_size), out_shape=(plt...  22.7 us
    ppermute x10, starting transfers between devices, passed_along(): return lax.ppermute(value, 'ctx', pairs)  20.3 us
    pallas_call x1, Pallas kernels, shards(): pl.pallas_call(functools.partial(front_kernel, head_size, slot_cap), out_...  16.1 us
    ppermute x10, waiting for transfers between devices, passed_along(): return lax.ppermute(value, 'ctx', pairs)  5.57 us
    all_to_all x1, starting transfers between devices, shards(): lax.all_to_all(fetched.reshape(count, slot_cap, hidden), 'ctx', split_axi...  3.57 us
    pallas_call x1, Pallas kernels, shards(): pl.pallas_call(table_kernel, out_shape=jax.ShapeDtypeStruct((rows, wanted...  2.41 us
  transfers between devices with their start and end apart: 11, of which 2 were waited for; matrix products, arithmetic and copies ran while one was open for 2% of the time, Pallas kernels for 53%

profile of v4, /device:TPU:0, one launch (start us, length us, event | category | flops | bytes accessed | tf_op | source)
XLA Modules:
  0.0 73.5 jit_solution(12835031226904097046)
XLA Ops:
  0.6 3.1 %collective-permute-start.1 = (bf16[512,1024]{1,0:T(8,128)(2,1)}, bf16[512,1024]{1,0:T(8,128)(2,1)}, u32[]{:S(2)}, u32[]{:S(2)}) collective-permute-start(bf16[512,1024]{1,0:T(8,128)(2,1)} %refs_15_.1), channel_id=1, source_target_pairs={{0,4},{1,5},{2,6},{3,7},{4,8},{5,9},{6,10},{7,11},{8,12},{9,13},{1... | collective-permute-start | bytes 3145736 | tf_op jit(solution)/shard_map/ppermute | solution.py:18
  3.7 1.1 %slice.6 = bf16[256,1024]{1,0:T(8,128)(2,1)S(1)} slice(bf16[512,1024]{1,0:T(8,128)(2,1)} %refs_15_.1), slice={[0:256], [0:1024]} | slice | bytes 1048576 | tf_op jit(solution)/shard_map/slice | solution.py:487
  4.8 0.0 copy-start
  4.8 0.0 copy-start.1
  4.8 0.0 copy-start.2
  4.9 1.6 %collective-permute-start = (bf16[256,1024]{1,0:T(8,128)(2,1)S(1)}, bf16[256,1024]{1,0:T(8,128)(2,1)S(1)}, u32[]{:S(2)}, u32[]{:S(2)}) collective-permute-start(bf16[256,1024]{1,0:T(8,128)(2,1)S(1)} %slice.6), channel_id=1, source_target_pairs={{0,2},{1,3},{2,0},{3,1},{4,6},{5,7},{6,4},{7,5},{8,10},{9,11},{10,... | collective-permute-start | bytes 1572872 | tf_op jit(solution)/shard_map/ppermute | solution.py:18
  6.4 16.1 %front.1 = (bf16[256,1024]{1,0:T(8,128)(2,1)}, bf16[128,256]{1,0:T(8,128)(2,1)S(1)}, bf16[512,2048]{1,0:T(8,128)(2,1)}, f32[512,1024]{1,0:T(8,128)}, bf16[256,1024]{1,0:T(8,128)(2,1)}) custom-call(s32[4]{0:T(128)} %refs_0_.3, f32[16,16]{1,0:T(8,128)} %refs_2_.3, s32[16,128]{1,0:T(8,128)} %refs_2_.2, bf16[512,1024]{1,0:T(8,128)(2,1)} %refs_15_.1, ...), custom_call_target="tpu_custom_call" | custom-call | flops 14000000000 | bytes 8388608 | tf_op jit(solution)/shard_map/front/pallas_call | solution.py:490
  22.5 0.6 collective-permute-start.5
  23.1 0.0 collective-permute-done.refs_8_
  23.1 3.5 %collective-permute-start.6 = (bf16[256,1024]{1,0:T(8,128)(2,1)S(1)}, bf16[256,1024]{1,0:T(8,128)(2,1)S(1)}, u32[]{:S(2)}, u32[]{:S(2)}) collective-permute-start(bf16[256,1024]{1,0:T(8,128)(2,1)S(1)} %collective-permute-done.refs_8_), channel_id=1, source_target_pairs={{0,4},{1,5},{4,8},{5,9},{8,12},{9,13},{12,0},{13,1},{16,20},{17,21... | collective-permute-start | bytes 1572872 | tf_op jit(solution)/shard_map/ppermute | solution.py:18
  26.6 2.3 %collective-permute-start.3 = (bf16[512,1024]{1,0:T(8,128)(2,1)}, bf16[512,1024]{1,0:T(8,128)(2,1)}, u32[]{:S(2)}, u32[]{:S(2)}) collective-permute-start(bf16[512,1024]{1,0:T(8,128)(2,1)} %refs_15_.1), channel_id=1, source_target_pairs={{0,1},{2,3},{4,5},{6,7},{8,9},{10,11},{12,13},{14,15},{16,17},{18,... | collective-permute-start | bytes 3145736 | tf_op jit(solution)/shard_map/ppermute | solution.py:18
  28.9 1.0 %collective-permute-done.1.refs_5_ = bf16[512,1024]{1,0:T(8,128)(2,1)} collective-permute-done((bf16[512,1024]{1,0:T(8,128)(2,1)}, bf16[512,1024]{1,0:T(8,128)(2,1)}, u32[]{:S(2)}, u32[]{:S(2)}) %collective-permute-start.1) | collective-permute-done | bytes 1048608 | tf_op jit(solution)/shard_map/ppermute | solution.py:18
  29.9 1.3 %collective-permute-start.2 = (bf16[512,1024]{1,0:T(8,128)(2,1)}, bf16[512,1024]{1,0:T(8,128)(2,1)}, u32[]{:S(2)}, u32[]{:S(2)}) collective-permute-start(bf16[512,1024]{1,0:T(8,128)(2,1)} %collective-permute-done.1.refs_5_), channel_id=1, source_target_pairs={{1,0},{3,2},{5,4},{7,6},{9,8},{11,10},{13,12},{15,14},{17,16},{19,... | collective-permute-start | bytes 3145736 | tf_op jit(solution)/shard_map/ppermute | solution.py:18
  31.2 0.7 slice.7
  31.9 4.9 %collective-permute-start.9 = (bf16[1,1024]{1,0:T(2,128)(2,1)S(1)}, bf16[1,1024]{1,0:T(2,128)(2,1)S(1)}, u32[]{:S(2)}, u32[]{:S(2)}) collective-permute-start(bf16[1,1024]{1,0:T(2,128)(2,1)S(1)} %slice.7), channel_id=1, source_target_pairs={{0,15},{1,0},{2,1},{3,2},{4,3},{5,4},{6,5},{7,6},{8,7},{9,8},{10,9... | collective-permute-start | bytes 6152 | tf_op jit(solution)/shard_map/ppermute | solution.py:18
  36.8 4.5 %collective-permute-done.5.refs_12_ = bf16[256,1024]{1,0:T(8,128)(2,1)S(1)} collective-permute-done((bf16[256,1024]{1,0:T(8,128)(2,1)}, bf16[256,1024]{1,0:T(8,128)(2,1)S(1)}, u32[]{:S(2)}, u32[]{:S(2)}) %collective-permute-start.5) | collective-permute-done | bytes 524320 | tf_op jit(solution)/shard_map/ppermute | solution.py:18
  41.3 0.7 collective-permute-start.4
  42.0 0.0 collective-permute-done.6.refs_10_
  42.0 1.9 %collective-permute-start.7 = (bf16[256,1024]{1,0:T(8,128)(2,1)S(1)}, bf16[256,1024]{1,0:T(8,128)(2,1)S(1)}, u32[]{:S(2)}, u32[]{:S(2)}) collective-permute-start(bf16[256,1024]{1,0:T(8,128)(2,1)S(1)} %collective-permute-done.6.refs_10_), channel_id=1, source_target_pairs={{0,1},{1,0},{4,5},{5,4},{8,9},{9,8},{12,13},{13,12},{16,17},{17,16... | collective-permute-start | bytes 1572872 | tf_op jit(solution)/shard_map/ppermute | solution.py:18
  44.0 0.0 collective-permute-done.9.refs_16_
  44.0 0.6 collective-permute-start.8
  44.5 3.6 %all-to-all-start = ((bf16[16,16,1024]{2,1,0:T(8,128)(2,1)}), bf16[16,16,1024]{2,1,0:T(8,128)(2,1)S(1)}, u32[]{:S(2)}, u32[]{:S(2)}) async-start(bf16[16,16,1024]{2,1,0:T(8,128)(2,1)} %bitcast.1), calls=%async_computation | async-start | bytes 1048576 | tf_op jit(solution)/shard_map/all_to_all | solution.py:526
  48.1 0.0 collective-permute-done.3.refs_7_
  48.1 0.0 collective-permute-done.4.refs_9_
  48.1 0.0 collective-permute-done.7.refs_11_
  48.2 0.0 collective-permute-done.8.refs_13_
  48.2 0.0 collective-permute-done.2.refs_6_
  48.2 0.0 copy-done
  48.2 0.0 copy-done.1
  48.2 22.7 %picks.1 = (bf16[512,1024]{1,0:T(8,128)(2,1)}, f32[4,128]{1,0:T(4,128)}) custom-call(s32[4]{0:T(128)S(1)} %copy-done.1, s32[1,2]{1,0:T(1,128)S(1)} %copy-done.2, f32[16,16]{1,0:T(8,128)S(1)} %copy-done, bf16[512,2048]{1,0:T(8,128)(2,1)} %get-tuple-element.18.refs_3_, f32[512,1024]{1,0:T(8,128)} %get-tuple-element.20.refs_4_, ...), custom_call_target="tpu_custom_call" | custom-call | flops 20000000000 | bytes 8388608 | tf_op jit(solution)/shard_map/picks/pallas_call | solution.py:533
  70.9 0.0 all-to-all-done
  70.9 2.4 %table.1 = f32[512,128]{1,0:T(8,128)} custom-call(bf16[512,1024]{1,0:T(8,128)(2,1)} %get-tuple-element.14.layer_hbm, bf16[256,1024]{1,0:T(8,128)(2,1)S(1)} %bitcast.3, bf16[128,256]{1,0:T(8,128)(2,1)S(1)} %get-tuple-element.30.hits_ref), custom_call_target="tpu_custom_call" | custom-call | flops 1000000000 | bytes 2097152 | tf_op jit(solution)/shard_map/table/pallas_call | solution.py:562
  (1 shorter events, 0.0 us)
Async XLA Ops:
  0.6 29.3 %collective-permute-start.1 = (bf16[512,1024]{1,0:T(8,128)(2,1)}, bf16[512,1024]{1,0:T(8,128)(2,1)}, u32[]{:S(2)}, u32[]{:S(2)}) collective-permute-start(bf16[512,1024]{1,0:T(8,128)(2,1)} %refs_15_.1), channel_id=1, source_target_pairs={{0,4},{1,5},{2,6},{3,7},{4,8},{5,9},{6,10},{7,11},{8,12},{9,13},{1... | collective-permute-start | bytes 3145736 | tf_op jit(solution)/shard_map/ppermute | solution.py:18
  4.8 43.4 %copy-start = (f32[16,16]{1,0:T(8,128)S(1)}, f32[16,16]{1,0:T(8,128)}, u32[]{:S(2)}) copy-start(f32[16,16]{1,0:T(8,128)} %refs_2_.3) | copy-start | bytes 3076
  4.8 43.4 %copy-start.1 = (s32[4]{0:T(128)S(1)}, s32[4]{0:T(128)}, u32[]{:S(2)}) copy-start(s32[4]{0:T(128)} %refs_0_.3) | copy-start | bytes 52
  4.8 43.4 %copy-start.2 = (s32[1,2]{1,0:T(1,128)S(1)}, s32[1,2]{1,0:T(1,128)}, u32[]{:S(2)}) copy-start(s32[1,2]{1,0:T(1,128)} %refs_1_.3) | copy-start | bytes 28
  4.9 18.2 %collective-permute-start = (bf16[256,1024]{1,0:T(8,128)(2,1)S(1)}, bf16[256,1024]{1,0:T(8,128)(2,1)S(1)}, u32[]{:S(2)}, u32[]{:S(2)}) collective-permute-start(bf16[256,1024]{1,0:T(8,128)(2,1)S(1)} %slice.6), channel_id=1, source_target_pairs={{0,2},{1,3},{2,0},{3,1},{4,6},{5,7},{6,4},{7,5},{8,10},{9,11},{10,... | collective-permute-start | bytes 1572872 | tf_op jit(solution)/shard_map/ppermute | solution.py:18
  22.5 18.8 %collective-permute-start.5 = (bf16[256,1024]{1,0:T(8,128)(2,1)}, bf16[256,1024]{1,0:T(8,128)(2,1)S(1)}, u32[]{:S(2)}, u32[]{:S(2)}) collective-permute-start(bf16[256,1024]{1,0:T(8,128)(2,1)} %get-tuple-element.23), channel_id=1, source_target_pairs={{0,2},{1,3},{2,4},{3,5},{4,6},{5,7},{6,8},{7,9},{8,10},{9,11},{10,... | collective-permute-start | bytes 1572872 | tf_op jit(solution)/shard_map/ppermute | solution.py:18
  23.1 18.9 %collective-permute-start.6 = (bf16[256,1024]{1,0:T(8,128)(2,1)S(1)}, bf16[256,1024]{1,0:T(8,128)(2,1)S(1)}, u32[]{:S(2)}, u32[]{:S(2)}) collective-permute-start(bf16[256,1024]{1,0:T(8,128)(2,1)S(1)} %collective-permute-done.refs_8_), channel_id=1, source_target_pairs={{0,4},{1,5},{4,8},{5,9},{8,12},{9,13},{12,0},{13,1},{16,20},{17,21... | collective-permute-start | bytes 1572872 | tf_op jit(solution)/shard_map/ppermute | solution.py:18
  26.6 21.6 %collective-permute-start.3 = (bf16[512,1024]{1,0:T(8,128)(2,1)}, bf16[512,1024]{1,0:T(8,128)(2,1)}, u32[]{:S(2)}, u32[]{:S(2)}) collective-permute-start(bf16[512,1024]{1,0:T(8,128)(2,1)} %refs_15_.1), channel_id=1, source_target_pairs={{0,1},{2,3},{4,5},{6,7},{8,9},{10,11},{12,13},{14,15},{16,17},{18,... | collective-permute-start | bytes 3145736 | tf_op jit(solution)/shard_map/ppermute | solution.py:18
  29.9 18.3 %collective-permute-start.2 = (bf16[512,1024]{1,0:T(8,128)(2,1)}, bf16[512,1024]{1,0:T(8,128)(2,1)}, u32[]{:S(2)}, u32[]{:S(2)}) collective-permute-start(bf16[512,1024]{1,0:T(8,128)(2,1)} %collective-permute-done.1.refs_5_), channel_id=1, source_target_pairs={{1,0},{3,2},{5,4},{7,6},{9,8},{11,10},{13,12},{15,14},{17,16},{19,... | collective-permute-start | bytes 3145736 | tf_op jit(solution)/shard_map/ppermute | solution.py:18
  31.9 12.1 %collective-permute-start.9 = (bf16[1,1024]{1,0:T(2,128)(2,1)S(1)}, bf16[1,1024]{1,0:T(2,128)(2,1)S(1)}, u32[]{:S(2)}, u32[]{:S(2)}) collective-permute-start(bf16[1,1024]{1,0:T(2,128)(2,1)S(1)} %slice.7), channel_id=1, source_target_pairs={{0,15},{1,0},{2,1},{3,2},{4,3},{5,4},{6,5},{7,6},{8,7},{9,8},{10,9... | collective-permute-start | bytes 6152 | tf_op jit(solution)/shard_map/ppermute | solution.py:18
  41.3 6.8 %collective-permute-start.4 = (bf16[256,1024]{1,0:T(8,128)(2,1)S(1)}, bf16[256,1024]{1,0:T(8,128)(2,1)S(1)}, u32[]{:S(2)}, u32[]{:S(2)}) collective-permute-start(bf16[256,1024]{1,0:T(8,128)(2,1)S(1)} %collective-permute-done.refs_8_), channel_id=1, source_target_pairs={{2,3},{3,2},{6,7},{7,6},{10,11},{11,10},{14,15},{15,14},{18,19},{1... | collective-permute-start | bytes 1572872 | tf_op jit(solution)/shard_map/ppermute | solution.py:18
  42.0 6.1 %collective-permute-start.7 = (bf16[256,1024]{1,0:T(8,128)(2,1)S(1)}, bf16[256,1024]{1,0:T(8,128)(2,1)S(1)}, u32[]{:S(2)}, u32[]{:S(2)}) collective-permute-start(bf16[256,1024]{1,0:T(8,128)(2,1)S(1)} %collective-permute-done.6.refs_10_), channel_id=1, source_target_pairs={{0,1},{1,0},{4,5},{5,4},{8,9},{9,8},{12,13},{13,12},{16,17},{17,16... | collective-permute-start | bytes 1572872 | tf_op jit(solution)/shard_map/ppermute | solution.py:18
  44.0 4.2 %collective-permute-start.8 = (bf16[256,1024]{1,0:T(8,128)(2,1)S(1)}, bf16[256,1024]{1,0:T(8,128)(2,1)}, u32[]{:S(2)}, u32[]{:S(2)}) collective-permute-start(bf16[256,1024]{1,0:T(8,128)(2,1)S(1)} %collective-permute-done.5.refs_12_), channel_id=1, source_target_pairs={{0,1},{1,0},{2,3},{3,2},{4,5},{5,4},{6,7},{7,6},{8,9},{9,8},{10,11... | collective-permute-start | bytes 1572872 | tf_op jit(solution)/shard_map/ppermute | solution.py:18
  44.5 26.4 %all-to-all-start = ((bf16[16,16,1024]{2,1,0:T(8,128)(2,1)}), bf16[16,16,1024]{2,1,0:T(8,128)(2,1)S(1)}, u32[]{:S(2)}, u32[]{:S(2)}) async-start(bf16[16,16,1024]{2,1,0:T(8,128)(2,1)} %bitcast.1), calls=%async_computation | async-start | bytes 1048576 | tf_op jit(solution)/shard_map/all_to_all | solution.py:526

commit v5 on v4

--- a/solution.py
+++ b/solution.py
@@ -270,15 +270,13 @@
     ]
     for copy in copies:
         copy.wait()
-    later[0].start()
-    later[1].start()
+    for copy in later[:parts]:
+        copy.start()
     normed = centered(rows_ref[...].astype(F32)).astype(BF16)
     for part in range(parts):
         later[part].wait()
-        if part + 2 < parts:
-            later[part + 2].start()
-        else:
-            for copy in later[parts + 3 * (part + 2 - parts) :][:3]:
+        if part == 0:
+            for copy in later[parts:]:
                 copy.start()
         columns = pl.ds(part * step, step)
         value = jnp.dot(normed, w_buf[:, columns], preferred_element_type=F32)
@@ -383,12 +381,11 @@
     scale = hidden**-0.5
     total = count * rows
     departures = []
+    gated = (centered(acc_ref[...]) * gate_ref[...].astype(F32)).astype(BF16)
+    mixed = jnp.dot(gated, out_buf[...], preferred_element_type=F32)
     for part in range(2):
         block_rows = slice(part * half, (part + 1) * half)
-        gated = centered(acc_ref[block_rows]) * gate_ref[block_rows].astype(F32)
-        layer = events_ref[block_rows].astype(F32) + jnp.dot(
-            gated.astype(BF16), out_buf[...], preferred_element_type=F32
-        )
+        layer = events_ref[block_rows].astype(F32) + mixed[block_rows]
         layer = layer.astype(BF16)
         layer_ref[block_rows] = layer
         leaving = pltpu.make_async_copy(

time: 74.1 us -> 74 us (level)
  no operation moved by 1% of the time
where the time goes in v5:
time: 74 us; the launch traced here: 73.6 us
  Pallas kernels  41.3 us (56%)
  starting transfers between devices  23.9 us (32%)
  waiting for transfers between devices  5.58 us (8%)
  local copies, waits for them, and re-layouts  1.85 us (2%)
  between operations  0.96 us (1%)
    pallas_call x1, Pallas kernels, shards(): pl.pallas_call(functools.partial(picks_kernel, head_size), out_shape=(plt...  22.8 us
    ppermute x10, starting transfers between devices, passed_along(): return lax.ppermute(value, 'ctx', pairs)  20.3 us
    pallas_call x1, Pallas kernels, shards(): pl.pallas_call(functools.partial(front_kernel, head_size, slot_cap), out_...  16.1 us
    ppermute x10, waiting for transfers between devices, passed_along(): return lax.ppermute(value, 'ctx', pairs)  5.57 us
    all_to_all x1, starting transfers between devices, shards(): lax.all_to_all(fetched.reshape(count, slot_cap, hidden), 'ctx', split_axi...  3.57 us
    pallas_call x1, Pallas kernels, shards(): pl.pallas_call(table_kernel, out_shape=jax.ShapeDtypeStruct((rows, wanted...  2.41 us
  transfers between devices with their start and end apart: 11, of which 2 were waited for; matrix products, arithmetic and copies ran while one was open for 2% of the time, Pallas kernels for 53%

profile of v5, /device:TPU:0, one launch (start us, length us, event | category | flops | bytes accessed | tf_op | source)
XLA Modules:
  0.0 73.6 jit_solution(10340306775937619704)
XLA Ops:
  0.6 3.1 %collective-permute-start.1 = (bf16[512,1024]{1,0:T(8,128)(2,1)}, bf16[512,1024]{1,0:T(8,128)(2,1)}, u32[]{:S(2)}, u32[]{:S(2)}) collective-permute-start(bf16[512,1024]{1,0:T(8,128)(2,1)} %refs_15_.1), channel_id=1, source_target_pairs={{0,4},{1,5},{2,6},{3,7},{4,8},{5,9},{6,10},{7,11},{8,12},{9,13},{1... | collective-permute-start | bytes 3145736 | tf_op jit(solution)/shard_map/ppermute | solution.py:18
  3.7 1.1 %slice.6 = bf16[256,1024]{1,0:T(8,128)(2,1)S(1)} slice(bf16[512,1024]{1,0:T(8,128)(2,1)} %refs_15_.1), slice={[0:256], [0:1024]} | slice | bytes 1048576 | tf_op jit(solution)/shard_map/slice | solution.py:484
  4.8 0.0 copy-start
  4.8 0.0 copy-start.1
  4.8 0.0 copy-start.2
  4.9 1.6 %collective-permute-start = (bf16[256,1024]{1,0:T(8,128)(2,1)S(1)}, bf16[256,1024]{1,0:T(8,128)(2,1)S(1)}, u32[]{:S(2)}, u32[]{:S(2)}) collective-permute-start(bf16[256,1024]{1,0:T(8,128)(2,1)S(1)} %slice.6), channel_id=1, source_target_pairs={{0,2},{1,3},{2,0},{3,1},{4,6},{5,7},{6,4},{7,5},{8,10},{9,11},{10,... | collective-permute-start | bytes 1572872 | tf_op jit(solution)/shard_map/ppermute | solution.py:18
  6.4 16.1 %front.1 = (bf16[256,1024]{1,0:T(8,128)(2,1)}, bf16[128,256]{1,0:T(8,128)(2,1)S(1)}, bf16[512,2048]{1,0:T(8,128)(2,1)}, f32[512,1024]{1,0:T(8,128)}, bf16[256,1024]{1,0:T(8,128)(2,1)}) custom-call(s32[4]{0:T(128)} %refs_0_.3, f32[16,16]{1,0:T(8,128)} %refs_2_.3, s32[16,128]{1,0:T(8,128)} %refs_2_.2, bf16[512,1024]{1,0:T(8,128)(2,1)} %refs_15_.1, ...), custom_call_target="tpu_custom_call" | custom-call | flops 14000000000 | bytes 8388608 | tf_op jit(solution)/shard_map/front/pallas_call | solution.py:487
  22.5 0.6 collective-permute-start.5
  23.1 0.0 collective-permute-done.refs_8_
  23.1 3.5 %collective-permute-start.6 = (bf16[256,1024]{1,0:T(8,128)(2,1)S(1)}, bf16[256,1024]{1,0:T(8,128)(2,1)S(1)}, u32[]{:S(2)}, u32[]{:S(2)}) collective-permute-start(bf16[256,1024]{1,0:T(8,128)(2,1)S(1)} %collective-permute-done.refs_8_), channel_id=1, source_target_pairs={{0,4},{1,5},{4,8},{5,9},{8,12},{9,13},{12,0},{13,1},{16,20},{17,21... | collective-permute-start | bytes 1572872 | tf_op jit(solution)/shard_map/ppermute | solution.py:18
  26.6 2.3 %collective-permute-start.3 = (bf16[512,1024]{1,0:T(8,128)(2,1)}, bf16[512,1024]{1,0:T(8,128)(2,1)}, u32[]{:S(2)}, u32[]{:S(2)}) collective-permute-start(bf16[512,1024]{1,0:T(8,128)(2,1)} %refs_15_.1), channel_id=1, source_target_pairs={{0,1},{2,3},{4,5},{6,7},{8,9},{10,11},{12,13},{14,15},{16,17},{18,... | collective-permute-start | bytes 3145736 | tf_op jit(solution)/shard_map/ppermute | solution.py:18
  28.9 1.0 %collective-permute-done.1.refs_5_ = bf16[512,1024]{1,0:T(8,128)(2,1)} collective-permute-done((bf16[512,1024]{1,0:T(8,128)(2,1)}, bf16[512,1024]{1,0:T(8,128)(2,1)}, u32[]{:S(2)}, u32[]{:S(2)}) %collective-permute-start.1) | collective-permute-done | bytes 1048608 | tf_op jit(solution)/shard_map/ppermute | solution.py:18
  29.9 1.3 %collective-permute-start.2 = (bf16[512,1024]{1,0:T(8,128)(2,1)}, bf16[512,1024]{1,0:T(8,128)(2,1)}, u32[]{:S(2)}, u32[]{:S(2)}) collective-permute-start(bf16[512,1024]{1,0:T(8,128)(2,1)} %collective-permute-done.1.refs_5_), channel_id=1, source_target_pairs={{1,0},{3,2},{5,4},{7,6},{9,8},{11,10},{13,12},{15,14},{17,16},{19,... | collective-permute-start | bytes 3145736 | tf_op jit(solution)/shard_map/ppermute | solution.py:18
  31.2 0.7 slice.7
  31.9 4.9 %collective-permute-start.9 = (bf16[1,1024]{1,0:T(2,128)(2,1)S(1)}, bf16[1,1024]{1,0:T(2,128)(2,1)S(1)}, u32[]{:S(2)}, u32[]{:S(2)}) collective-permute-start(bf16[1,1024]{1,0:T(2,128)(2,1)S(1)} %slice.7), channel_id=1, source_target_pairs={{0,15},{1,0},{2,1},{3,2},{4,3},{5,4},{6,5},{7,6},{8,7},{9,8},{10,9... | collective-permute-start | bytes 6152 | tf_op jit(solution)/shard_map/ppermute | solution.py:18
  36.8 4.5 %collective-permute-done.5.refs_12_ = bf16[256,1024]{1,0:T(8,128)(2,1)S(1)} collective-permute-done((bf16[256,1024]{1,0:T(8,128)(2,1)}, bf16[256,1024]{1,0:T(8,128)(2,1)S(1)}, u32[]{:S(2)}, u32[]{:S(2)}) %collective-permute-start.5) | collective-permute-done | bytes 524320 | tf_op jit(solution)/shard_map/ppermute | solution.py:18
  41.3 0.7 collective-permute-start.4
  42.0 0.0 collective-permute-done.6.refs_10_
  42.0 1.9 %collective-permute-start.7 = (bf16[256,1024]{1,0:T(8,128)(2,1)S(1)}, bf16[256,1024]{1,0:T(8,128)(2,1)S(1)}, u32[]{:S(2)}, u32[]{:S(2)}) collective-permute-start(bf16[256,1024]{1,0:T(8,128)(2,1)S(1)} %collective-permute-done.6.refs_10_), channel_id=1, source_target_pairs={{0,1},{1,0},{4,5},{5,4},{8,9},{9,8},{12,13},{13,12},{16,17},{17,16... | collective-permute-start | bytes 1572872 | tf_op jit(solution)/shard_map/ppermute | solution.py:18
  44.0 0.0 collective-permute-done.9.refs_16_
  44.0 0.6 collective-permute-start.8
  44.5 3.6 %all-to-all-start = ((bf16[16,16,1024]{2,1,0:T(8,128)(2,1)}), bf16[16,16,1024]{2,1,0:T(8,128)(2,1)S(1)}, u32[]{:S(2)}, u32[]{:S(2)}) async-start(bf16[16,16,1024]{2,1,0:T(8,128)(2,1)} %bitcast.1), calls=%async_computation | async-start | bytes 1048576 | tf_op jit(solution)/shard_map/all_to_all | solution.py:523
  48.1 0.0 collective-permute-done.3.refs_7_
  48.1 0.0 collective-permute-done.4.refs_9_
  48.1 0.0 collective-permute-done.7.refs_11_
  48.2 0.0 collective-permute-done.8.refs_13_
  48.2 0.0 collective-permute-done.2.refs_6_
  48.2 0.0 copy-done
  48.2 0.0 copy-done.1
  48.2 22.8 %picks.1 = (bf16[512,1024]{1,0:T(8,128)(2,1)}, f32[4,128]{1,0:T(4,128)}) custom-call(s32[4]{0:T(128)S(1)} %copy-done.1, s32[1,2]{1,0:T(1,128)S(1)} %copy-done.2, f32[16,16]{1,0:T(8,128)S(1)} %copy-done, bf16[512,2048]{1,0:T(8,128)(2,1)} %get-tuple-element.18.refs_3_, f32[512,1024]{1,0:T(8,128)} %get-tuple-element.20.refs_4_, ...), custom_call_target="tpu_custom_call" | custom-call | flops 20000000000 | bytes 8388608 | tf_op jit(solution)/shard_map/picks/pallas_call | solution.py:530
  71.0 0.0 all-to-all-done
  71.0 2.4 %table.1 = f32[512,128]{1,0:T(8,128)} custom-call(bf16[512,1024]{1,0:T(8,128)(2,1)} %get-tuple-element.14.layer_hbm, bf16[256,1024]{1,0:T(8,128)(2,1)S(1)} %bitcast.3, bf16[128,256]{1,0:T(8,128)(2,1)S(1)} %get-tuple-element.30.hits_ref), custom_call_target="tpu_custom_call" | custom-call | flops 1000000000 | bytes 2097152 | tf_op jit(solution)/shard_map/table/pallas_call | solution.py:559
  (1 shorter events, 0.0 us)
Async XLA Ops:
  0.6 29.3 %collective-permute-start.1 = (bf16[512,1024]{1,0:T(8,128)(2,1)}, bf16[512,1024]{1,0:T(8,128)(2,1)}, u32[]{:S(2)}, u32[]{:S(2)}) collective-permute-start(bf16[512,1024]{1,0:T(8,128)(2,1)} %refs_15_.1), channel_id=1, source_target_pairs={{0,4},{1,5},{2,6},{3,7},{4,8},{5,9},{6,10},{7,11},{8,12},{9,13},{1... | collective-permute-start | bytes 3145736 | tf_op jit(solution)/shard_map/ppermute | solution.py:18
  4.8 43.4 %copy-start = (f32[16,16]{1,0:T(8,128)S(1)}, f32[16,16]{1,0:T(8,128)}, u32[]{:S(2)}) copy-start(f32[16,16]{1,0:T(8,128)} %refs_2_.3) | copy-start | bytes 3076
  4.8 43.4 %copy-start.1 = (s32[4]{0:T(128)S(1)}, s32[4]{0:T(128)}, u32[]{:S(2)}) copy-start(s32[4]{0:T(128)} %refs_0_.3) | copy-start | bytes 52
  4.8 43.4 %copy-start.2 = (s32[1,2]{1,0:T(1,128)S(1)}, s32[1,2]{1,0:T(1,128)}, u32[]{:S(2)}) copy-start(s32[1,2]{1,0:T(1,128)} %refs_1_.3) | copy-start | bytes 28
  4.9 18.2 %collective-permute-start = (bf16[256,1024]{1,0:T(8,128)(2,1)S(1)}, bf16[256,1024]{1,0:T(8,128)(2,1)S(1)}, u32[]{:S(2)}, u32[]{:S(2)}) collective-permute-start(bf16[256,1024]{1,0:T(8,128)(2,1)S(1)} %slice.6), channel_id=1, source_target_pairs={{0,2},{1,3},{2,0},{3,1},{4,6},{5,7},{6,4},{7,5},{8,10},{9,11},{10,... | collective-permute-start | bytes 1572872 | tf_op jit(solution)/shard_map/ppermute | solution.py:18
  22.5 18.8 %collective-permute-start.5 = (bf16[256,1024]{1,0:T(8,128)(2,1)}, bf16[256,1024]{1,0:T(8,128)(2,1)S(1)}, u32[]{:S(2)}, u32[]{:S(2)}) collective-permute-start(bf16[256,1024]{1,0:T(8,128)(2,1)} %get-tuple-element.23), channel_id=1, source_target_pairs={{0,2},{1,3},{2,4},{3,5},{4,6},{5,7},{6,8},{7,9},{8,10},{9,11},{10,... | collective-permute-start | bytes 1572872 | tf_op jit(solution)/shard_map/ppermute | solution.py:18
  23.1 18.9 %collective-permute-start.6 = (bf16[256,1024]{1,0:T(8,128)(2,1)S(1)}, bf16[256,1024]{1,0:T(8,128)(2,1)S(1)}, u32[]{:S(2)}, u32[]{:S(2)}) collective-permute-start(bf16[256,1024]{1,0:T(8,128)(2,1)S(1)} %collective-permute-done.refs_8_), channel_id=1, source_target_pairs={{0,4},{1,5},{4,8},{5,9},{8,12},{9,13},{12,0},{13,1},{16,20},{17,21... | collective-permute-start | bytes 1572872 | tf_op jit(solution)/shard_map/ppermute | solution.py:18
  26.6 21.6 %collective-permute-start.3 = (bf16[512,1024]{1,0:T(8,128)(2,1)}, bf16[512,1024]{1,0:T(8,128)(2,1)}, u32[]{:S(2)}, u32[]{:S(2)}) collective-permute-start(bf16[512,1024]{1,0:T(8,128)(2,1)} %refs_15_.1), channel_id=1, source_target_pairs={{0,1},{2,3},{4,5},{6,7},{8,9},{10,11},{12,13},{14,15},{16,17},{18,... | collective-permute-start | bytes 3145736 | tf_op jit(solution)/shard_map/ppermute | solution.py:18
  29.9 18.3 %collective-permute-start.2 = (bf16[512,1024]{1,0:T(8,128)(2,1)}, bf16[512,1024]{1,0:T(8,128)(2,1)}, u32[]{:S(2)}, u32[]{:S(2)}) collective-permute-start(bf16[512,1024]{1,0:T(8,128)(2,1)} %collective-permute-done.1.refs_5_), channel_id=1, source_target_pairs={{1,0},{3,2},{5,4},{7,6},{9,8},{11,10},{13,12},{15,14},{17,16},{19,... | collective-permute-start | bytes 3145736 | tf_op jit(solution)/shard_map/ppermute | solution.py:18
  31.9 12.1 %collective-permute-start.9 = (bf16[1,1024]{1,0:T(2,128)(2,1)S(1)}, bf16[1,1024]{1,0:T(2,128)(2,1)S(1)}, u32[]{:S(2)}, u32[]{:S(2)}) collective-permute-start(bf16[1,1024]{1,0:T(2,128)(2,1)S(1)} %slice.7), channel_id=1, source_target_pairs={{0,15},{1,0},{2,1},{3,2},{4,3},{5,4},{6,5},{7,6},{8,7},{9,8},{10,9... | collective-permute-start | bytes 6152 | tf_op jit(solution)/shard_map/ppermute | solution.py:18
  41.3 6.8 %collective-permute-start.4 = (bf16[256,1024]{1,0:T(8,128)(2,1)S(1)}, bf16[256,1024]{1,0:T(8,128)(2,1)S(1)}, u32[]{:S(2)}, u32[]{:S(2)}) collective-permute-start(bf16[256,1024]{1,0:T(8,128)(2,1)S(1)} %collective-permute-done.refs_8_), channel_id=1, source_target_pairs={{2,3},{3,2},{6,7},{7,6},{10,11},{11,10},{14,15},{15,14},{18,19},{1... | collective-permute-start | bytes 1572872 | tf_op jit(solution)/shard_map/ppermute | solution.py:18
  42.0 6.1 %collective-permute-start.7 = (bf16[256,1024]{1,0:T(8,128)(2,1)S(1)}, bf16[256,1024]{1,0:T(8,128)(2,1)S(1)}, u32[]{:S(2)}, u32[]{:S(2)}) collective-permute-start(bf16[256,1024]{1,0:T(8,128)(2,1)S(1)} %collective-permute-done.6.refs_10_), channel_id=1, source_target_pairs={{0,1},{1,0},{4,5},{5,4},{8,9},{9,8},{12,13},{13,12},{16,17},{17,16... | collective-permute-start | bytes 1572872 | tf_op jit(solution)/shard_map/ppermute | solution.py:18
  44.0 4.2 %collective-permute-start.8 = (bf16[256,1024]{1,0:T(8,128)(2,1)S(1)}, bf16[256,1024]{1,0:T(8,128)(2,1)}, u32[]{:S(2)}, u32[]{:S(2)}) collective-permute-start(bf16[256,1024]{1,0:T(8,128)(2,1)S(1)} %collective-permute-done.5.refs_12_), channel_id=1, source_target_pairs={{0,1},{1,0},{2,3},{3,2},{4,5},{5,4},{6,7},{7,6},{8,9},{9,8},{10,11... | collective-permute-start | bytes 1572872 | tf_op jit(solution)/shard_map/ppermute | solution.py:18
  44.5 26.4 %all-to-all-start = ((bf16[16,16,1024]{2,1,0:T(8,128)(2,1)}), bf16[16,16,1024]{2,1,0:T(8,128)(2,1)S(1)}, u32[]{:S(2)}, u32[]{:S(2)}) async-start(bf16[16,16,1024]{2,1,0:T(8,128)(2,1)} %bitcast.1), calls=%async_computation | async-start | bytes 1048576 | tf_op jit(solution)/shard_map/all_to_all | solution.py:523
